TPU v7x, 32 devices: a whole 2x2x4 slice. The times are simulated.
32 devices in a mesh: dp: 2 (over y), seq: 16 (over z, x, core).
Axes of the slice: x: 2, y: 2, z: 4, core: 2. Of those that a mesh axis runs over, the one named last changes fastest.
Arguments:
- tokens: int32 [2, 2, 2, 1024], P(None, 'dp', None, 'seq'), may hold values from 0 to 50303
- targets: int32 [2, 2, 1024], P(None, 'dp', 'seq'), may hold values from 0 to 50303
- counted: int32 [2, 2, 1024], P(None, 'dp', 'seq'), may hold values from 0 to 1, as said below
- cont_label: int32 [2, 2, 2], replicated, may hold values from 0 to 1, each once within a row
- pair_map: int32 [2, 2, 2], replicated, may hold values from 0 to 1, each once within a row
- ref_logp: float32 [2, 2, 2], replicated, may hold values from -128 to 128
- vocab_slot: int32 [50304], replicated, may hold values from 0 to 50303, each once
- embed_table: float32 [50304, 1088], P(('dp', 'seq')), may hold values from -0.375 to 0.375
- embed_first: float32 [50304, 1088], P(('dp', 'seq')), may hold values from -7.6293945e-05 to 7.6293945e-05
- embed_second: float32 [50304, 1088], P(('dp', 'seq')), may hold values from 1.4e-11 to 5.8e-11
- layer_weights: float32 [1088, 13056], P(None, ('dp', 'seq'))
- layer_first: float32 [1088, 13056], P(None, ('dp', 'seq')), may hold values from -7.6293945e-05 to 7.6293945e-05
- layer_second: float32 [1088, 13056], P(None, ('dp', 'seq')), may hold values from 1.4e-11 to 5.8e-11
- norm_params: float32 [6528], P(('dp', 'seq')), may hold values from -0.3 to 1.4, as said below
- norm_first: float32 [6528], P(('dp', 'seq')), may hold values from -0.0004272461 to 0.0004272461
- norm_second: float32 [6528], P(('dp', 'seq')), may hold values from 3.6e-10 to 1.4e-09
Outputs:
- embed_new: float32 [50304, 1088], P(('dp', 'seq'))
- embed_first_new: float32 [50304, 1088], P(('dp', 'seq'))
- embed_second_new: float32 [50304, 1088], P(('dp', 'seq'))
- embed_low: bfloat16 [50304, 1088], P(('dp', 'seq'))
- layer_new: float32 [1088, 13056], P(None, ('dp', 'seq'))
- layer_first_new: float32 [1088, 13056], P(None, ('dp', 'seq'))
- layer_second_new: float32 [1088, 13056], P(None, ('dp', 'seq'))
- layer_low: bfloat16 [1088, 13056], P(None, ('dp', 'seq'))
- norm_new: float32 [6528], P(('dp', 'seq'))
- norm_first_new: float32 [6528], P(('dp', 'seq'))
- norm_second_new: float32 [6528], P(('dp', 'seq'))
- norm_low: bfloat16 [6528], P(('dp', 'seq'))
- grad_norm: float32 [], replicated
- loss: float32 [], replicated
Inputs may be any that keep to these rules, and one draw needn't show every extreme that they name: `counted`: in each aligned block of 64 entries along the last dimension (the continuation rows of one device) exactly 32 entries are 1 and the others 0. `norm_params`: the first 3264 entries lie in 0.6 to 1.4.
All inputs are finite; a program needn't handle non-finite values.
Results may differ from a plain program's by a relative error of at most 0.02.
The roundings to bfloat16 on the way count: a program that leaves them out, or rounds other values in their place, can miss the bound.
Values may be sent and summed in bfloat16 or wider, within the bound.
A program may use at most 448 MiB of HBM per device.

v0:
```python
import jax
import jax.numpy as jnp
from jax import lax
from jax.sharding import PartitionSpec as P

HEADS = 17
HD = 64
FF = 4352
PICK = 32
CLEN = 512
MB = 2
STEP = 10


EPS_NORM = 1e-05
DPO_BETA = 0.05
CLIP_NORM = 1.0
LEARN_RATE = 0.03
NORM_RATE = 0.4
WEIGHT_DECAY = 0.1
MOMENT_ONE = 0.9
MOMENT_TWO = 0.999
EPS_ADAM = 1e-08
MASKED = -1e30


def merged(part, axis, combine):
    gathered = jax.tree.map(lambda a: lax.all_gather(a, axis), part)

    def take(source):
        return jax.tree.map(lambda a: lax.dynamic_index_in_dim(a, source, 0, False), gathered)

    return lax.fori_loop(
        1, lax.axis_size(axis), lambda source, state: combine(state, take(source)), take(0)
    )


def contract(left, right, left_dim, right_dim):
    return lax.dot_general(
        left, right, (((left_dim,), (right_dim,)), ((), ())), preferred_element_type=jnp.float32
    )


def norm_forward(values, gain, bias):
    centred = values - jnp.mean(values, axis=-1, keepdims=True)
    inverse = lax.rsqrt(jnp.mean(centred * centred, axis=-1, keepdims=True) + EPS_NORM)
    unit = centred * inverse
    return (unit * gain + bias, unit, inverse)


def norm_backward(upstream, unit, inverse, gain):
    scaled = upstream * gain
    inner = (
        scaled
        - jnp.mean(scaled, axis=-1, keepdims=True)
        - unit * jnp.mean(scaled * unit, axis=-1, keepdims=True)
    )
    return (inverse * inner, jnp.sum(upstream * unit, axis=0), jnp.sum(upstream, axis=0))


def probabilities(queries, keys, query_pos, key_pos):
    scores = jnp.einsum(
        "qhe,khe->hqk", queries, keys, preferred_element_type=jnp.float32
    ) * queries.shape[2] ** (-0.5)
    scores = jnp.where((key_pos[None, :] <= query_pos[:, None])[None], scores, MASKED)
    shifted = jnp.exp(scores - jnp.max(scores, axis=-1, keepdims=True))
    return shifted / jnp.sum(shifted, axis=-1, keepdims=True)


def attend_forward(queries, keys, values, query_pos, key_pos):
    probs = probabilities(queries, keys, query_pos, key_pos)
    return jnp.einsum(
        "hqk,khe->qhe", probs.astype(jnp.bfloat16), values, preferred_element_type=jnp.float32
    )


def attend_backward(queries, keys, values, query_pos, key_pos, grad_out):
    probs = probabilities(queries, keys, query_pos, key_pos)
    grad_probs = jnp.einsum("qhe,khe->hqk", grad_out, values, preferred_element_type=jnp.float32)
    grad_scores = (
        probs * (grad_probs - jnp.sum(probs * grad_probs, axis=-1, keepdims=True))
    ).astype(jnp.bfloat16)
    scale = queries.shape[2] ** (-0.5)
    grad_query = (
        jnp.einsum("hqk,khe->qhe", grad_scores, keys, preferred_element_type=jnp.float32) * scale
    )
    grad_keys = (
        jnp.einsum("hqk,qhe->khe", grad_scores, queries, preferred_element_type=jnp.float32) * scale
    )
    grad_values = jnp.einsum(
        "hqk,qhe->khe", probs.astype(jnp.bfloat16), grad_out, preferred_element_type=jnp.float32
    )
    return (grad_query, grad_keys, grad_values)


def key_sets(all_keys, all_values, seq_rank, rows_dev, half):
    start = seq_rank * rows_dev
    run_start = start // CLEN * CLEN
    prompt_keys = all_keys[0].reshape(half, HEADS, HD)
    prompt_values = all_values[0].reshape(half, HEADS, HD)
    run_keys = lax.dynamic_slice_in_dim(all_keys[1], run_start, CLEN, 0).reshape(CLEN, HEADS, HD)
    run_values = lax.dynamic_slice_in_dim(all_values[1], run_start, CLEN, 0).reshape(
        CLEN, HEADS, HD
    )
    offsets = jnp.arange(rows_dev, dtype=jnp.int32)
    prompt_pos = jnp.arange(half, dtype=jnp.int32)
    cont_pos = jnp.concatenate(
        [jnp.full((half,), -1, jnp.int32), jnp.arange(CLEN, dtype=jnp.int32)]
    )
    prompt_set = (prompt_keys, prompt_values, start + offsets, prompt_pos)
    cont_set = (
        jnp.concatenate([prompt_keys, run_keys]),
        jnp.concatenate([prompt_values, run_values]),
        start - run_start + offsets,
        cont_pos,
    )
    return ((prompt_set, cont_set), run_start)


def layer_forward(stream_in, weights, norms, seq_rank, half):
    width = stream_in.shape[1]
    rows_dev = stream_in.shape[0] // 2
    gains = norms.astype(jnp.float32).reshape(6, width)
    normed, unit_one, inverse_one = norm_forward(stream_in, gains[0], gains[3])
    hidden_one = normed.astype(jnp.bfloat16)
    qkv = jnp.dot(hidden_one, weights[:, : 3 * width], preferred_element_type=jnp.float32).astype(
        jnp.bfloat16
    )
    queries = qkv[:, :width].reshape(2, rows_dev, HEADS, HD)
    all_keys, all_values = (
        lax.all_gather(
            qkv[:, width : 2 * width].reshape(2, rows_dev, width), "seq", axis=1, tiled=True
        ),
        lax.all_gather(qkv[:, 2 * width :].reshape(2, rows_dev, width), "seq", axis=1, tiled=True),
    )
    sets, run_start = key_sets(all_keys, all_values, seq_rank, rows_dev, half)
    pieces = []
    for half_index in range(2):
        chosen_set = sets[half_index]
        pieces.append(
            attend_forward(
                queries[half_index], chosen_set[0], chosen_set[1], chosen_set[2], chosen_set[3]
            )
        )
    attended = jnp.concatenate(pieces).reshape(2 * rows_dev, width).astype(jnp.bfloat16)
    stream_one = stream_in + contract(attended, weights[:, 3 * width : 4 * width], 1, 1)
    normed, unit_two, inverse_two = norm_forward(stream_one, gains[1], gains[4])
    hidden_two = normed.astype(jnp.bfloat16)
    up_proj = jnp.dot(
        hidden_two, weights[:, 4 * width : 4 * width + FF], preferred_element_type=jnp.float32
    )
    activated = jax.nn.gelu(up_proj, approximate=False).astype(jnp.bfloat16)
    stream_two = stream_one + contract(activated, weights[:, 4 * width + FF :], 1, 1)
    normed, unit_final, inverse_final = norm_forward(stream_two, gains[2], gains[5])
    saved = (
        unit_one,
        inverse_one,
        hidden_one,
        queries,
        sets,
        run_start,
        attended,
        unit_two,
        inverse_two,
        hidden_two,
        up_proj,
        activated,
        unit_final,
        inverse_final,
    )
    return (normed.astype(jnp.bfloat16), saved)


def layer_backward(upstream, weights, norms, saved, half):
    (
        unit_one,
        inverse_one,
        hidden_one,
        queries,
        sets,
        run_start,
        attended,
        unit_two,
        inverse_two,
        hidden_two,
        up_proj,
        activated,
        unit_final,
        inverse_final,
    ) = saved
    width = upstream.shape[1]
    rows_dev = upstream.shape[0] // 2
    gains = norms.astype(jnp.float32).reshape(6, width)
    grad_two, gain_final, bias_final = norm_backward(upstream, unit_final, inverse_final, gains[2])
    grad_ffn = grad_two.astype(jnp.bfloat16)
    down_grad = contract(grad_ffn, activated, 0, 0)
    grad_act = jnp.dot(grad_ffn, weights[:, 4 * width + FF :], preferred_element_type=jnp.float32)
    _, gelu_pull = jax.vjp(lambda pre_act: jax.nn.gelu(pre_act, approximate=False), up_proj)
    grad_up = gelu_pull(grad_act)[0].astype(jnp.bfloat16)
    up_grad = contract(hidden_two, grad_up, 0, 0)
    grad_hidden = contract(grad_up, weights[:, 4 * width : 4 * width + FF], 1, 1)
    grad_mid, gain_two, bias_two = norm_backward(grad_hidden, unit_two, inverse_two, gains[1])
    grad_one = grad_two + grad_mid
    grad_branch = grad_one.astype(jnp.bfloat16)
    out_grad = contract(grad_branch, attended, 0, 0)
    grad_attended = (
        jnp.dot(grad_branch, weights[:, 3 * width : 4 * width], preferred_element_type=jnp.float32)
        .astype(jnp.bfloat16)
        .reshape(2, rows_dev, HEADS, HD)
    )
    results = []
    for half_index in range(2):
        chosen_set = sets[half_index]
        results.append(
            attend_backward(
                queries[half_index],
                chosen_set[0],
                chosen_set[1],
                chosen_set[2],
                chosen_set[3],
                grad_attended[half_index],
            )
        )
    blank = jnp.zeros((half, HEADS, HD), jnp.float32)
    key_grad = jnp.stack(
        [
            results[0][1] + results[1][1][:half],
            lax.dynamic_update_slice_in_dim(blank, results[1][1][half:], run_start, 0),
        ]
    ).reshape(2, half, width)
    value_grad = jnp.stack(
        [
            results[0][2] + results[1][2][:half],
            lax.dynamic_update_slice_in_dim(blank, results[1][2][half:], run_start, 0),
        ]
    ).reshape(2, half, width)
    own_keys, own_values = (
        lax.psum_scatter(
            key_grad.astype(jnp.bfloat16), "seq", scatter_dimension=1, tiled=True
        ).astype(jnp.float32),
        lax.psum_scatter(
            value_grad.astype(jnp.bfloat16), "seq", scatter_dimension=1, tiled=True
        ).astype(jnp.float32),
    )
    own_keys = own_keys.reshape(2 * rows_dev, width)
    own_values = own_values.reshape(2 * rows_dev, width)
    query_grad = jnp.concatenate([results[0][0], results[1][0]]).reshape(2 * rows_dev, width)
    grad_qkv = jnp.concatenate([query_grad, own_keys, own_values], axis=1).astype(jnp.bfloat16)
    qkv_grad = contract(hidden_one, grad_qkv, 0, 0)
    grad_low = contract(grad_qkv, weights[:, : 3 * width], 1, 1)
    grad_first, gain_one, bias_one = norm_backward(grad_low, unit_one, inverse_one, gains[0])
    weight_grad = jnp.concatenate([qkv_grad, out_grad, up_grad, down_grad], axis=1)
    norm_grad = jnp.concatenate([gain_one, gain_two, gain_final, bias_one, bias_two, bias_final])
    return (grad_one + grad_first, weight_grad, norm_grad)


def combine_stats(left, right):
    highest = jnp.maximum(left[0], right[0])
    summed = left[1] * jnp.exp(left[0] - highest) + right[1] * jnp.exp(right[0] - highest)
    return (highest, summed, left[2] + right[2])


def adamw(weight, moment_a, moment_b, gradient, rate, decay):
    moment_a = MOMENT_ONE * moment_a + (1.0 - MOMENT_ONE) * gradient
    moment_b = MOMENT_TWO * moment_b + (1.0 - MOMENT_TWO) * gradient * gradient
    update = (
        moment_a
        / (1.0 - MOMENT_ONE**STEP)
        / (jnp.sqrt(moment_b / (1.0 - MOMENT_TWO**STEP)) + EPS_ADAM)
    )
    weight = weight - rate * (update + decay * weight)
    return (weight, moment_a, moment_b, weight.astype(jnp.bfloat16))


def on_device(
    tokens,
    targets,
    counted,
    cont_label,
    pair_map,
    ref_logp,
    vocab_slot,
    embed_table,
    embed_first,
    embed_second,
    layer_weights,
    layer_first,
    layer_second,
    norm_params,
    norm_first,
    norm_second,
):
    seq_count = lax.axis_size("seq")
    seq_rank = lax.axis_index("seq")
    group_rank = lax.axis_index("dp")
    rows_dev = tokens.shape[3]
    half = rows_dev * seq_count
    width = embed_table.shape[1]
    vocab_dev = embed_table.shape[0]
    run_count = half // CLEN
    slab = lax.all_gather(embed_table.astype(jnp.bfloat16), "dp", axis=0, tiled=True)
    slab_rows = slab.shape[0]

    def locate(slots):
        owner = slots // vocab_dev
        inside = owner % seq_count == seq_rank
        return (jnp.where(inside, owner // seq_count * vocab_dev + slots % vocab_dev, 0), inside)

    weight_acc = jnp.zeros(layer_weights.shape, jnp.float32)
    norm_acc = jnp.zeros(norm_params.shape, jnp.float32)
    slab_grad = jnp.zeros((slab_rows, width), jnp.float32)
    loss_acc = jnp.zeros((), jnp.float32)
    positions = jnp.arange(rows_dev, dtype=jnp.int32)
    pick_ids = jnp.arange(PICK, dtype=jnp.int32)
    run_ids = jnp.arange(run_count, dtype=jnp.int32)
    vocab_ids = jnp.arange(slab_rows, dtype=jnp.int32)
    for micro in range(MB):
        slots = vocab_slot[tokens[micro, 0].reshape(1, 2 * rows_dev)]
        marks = counted[micro, 0]
        ranks = jnp.cumsum(marks) - 1
        pick_rows = jnp.sum(
            jnp.where(
                (ranks[None, :] == pick_ids[:, None]) & (marks[None, :] == 1), positions[None, :], 0
            ),
            axis=1,
        )
        pick_slots = vocab_slot[targets[micro, 0][pick_rows]]
        all_slots, all_targets = (
            lax.all_gather(slots, "seq", axis=0, tiled=True),
            lax.all_gather(pick_slots[None, :], "seq", axis=0, tiled=True),
        )
        local_rows, inside = locate(all_slots.reshape(-1))
        partial_value = jnp.where(
            inside[:, None], jnp.take(slab, local_rows, axis=0).astype(jnp.float32), 0.0
        )
        embedded = lax.psum_scatter(
            partial_value.astype(jnp.bfloat16), "seq", scatter_dimension=0, tiled=True
        ).astype(jnp.float32)
        full_weights, full_norms = (
            lax.all_gather(layer_weights.astype(jnp.bfloat16), ("dp", "seq"), axis=1, tiled=True),
            lax.all_gather(norm_params.astype(jnp.bfloat16), ("dp", "seq"), axis=0, tiled=True),
        )
        final, saved = layer_forward(embedded, full_weights, full_norms, seq_rank, half)
        picked = jnp.take(final[rows_dev:], pick_rows, axis=0)
        gathered_rows = lax.all_gather(picked, "seq", axis=0, tiled=True)
        logits = contract(gathered_rows, slab, 1, 1)
        highest = jnp.max(logits, axis=1)
        summed = jnp.sum(jnp.exp(logits - highest[:, None]), axis=1)
        target_rows, target_inside = locate(all_targets.reshape(-1))
        target_hit = (vocab_ids[None, :] == target_rows[:, None]) & target_inside[:, None]
        target_logit = jnp.sum(jnp.where(target_hit, logits, 0.0), axis=1)
        highest, summed, target_logit = merged(
            (highest, summed, target_logit), "seq", combine_stats
        )
        log_total = highest + jnp.log(summed)
        token_lp = target_logit - log_total
        run_of_row = jnp.arange(gathered_rows.shape[0], dtype=jnp.int32) // PICK * rows_dev // CLEN
        run_match = run_of_row[None, :] == run_ids[:, None]
        run_lp = jnp.sum(jnp.where(run_match, token_lp[None, :], 0.0), axis=1)
        labels = lax.dynamic_index_in_dim(cont_label[micro], group_rank, 0, keepdims=False)
        pairing = lax.dynamic_index_in_dim(pair_map[micro], group_rank, 0, keepdims=False)
        reference_lp = lax.dynamic_index_in_dim(ref_logp[micro], group_rank, 0, keepdims=False)
        label_match = labels[:, None] == run_ids[None, :]
        label_lp = jnp.sum(jnp.where(label_match, run_lp[:, None], 0.0), axis=0)
        margin = label_lp - reference_lp
        chosen_labels = pairing[0::2]
        rejected_labels = pairing[1::2]
        delta = margin[chosen_labels] - margin[rejected_labels]
        loss_acc = loss_acc + jnp.sum(jax.nn.softplus(-DPO_BETA * delta))
        pair_grad = -DPO_BETA * jax.nn.sigmoid(-DPO_BETA * delta)
        label_grad = jnp.sum(
            jnp.where(chosen_labels[:, None] == run_ids[None, :], pair_grad[:, None], 0.0)
            - jnp.where(rejected_labels[:, None] == run_ids[None, :], pair_grad[:, None], 0.0),
            axis=0,
        )
        run_grad = jnp.sum(jnp.where(label_match, label_grad[None, :], 0.0), axis=1)
        row_grad = jnp.sum(jnp.where(run_match, run_grad[:, None], 0.0), axis=0)
        logit_grad = (
            row_grad[:, None]
            * (target_hit.astype(jnp.float32) - jnp.exp(logits - log_total[:, None]))
        ).astype(jnp.bfloat16)
        slab_grad = slab_grad + contract(logit_grad, gathered_rows, 0, 0)
        row_back = lax.psum_scatter(
            contract(logit_grad, slab, 1, 0), "seq", scatter_dimension=0, tiled=True
        )
        upstream = (
            jnp.zeros((2 * rows_dev, width), jnp.float32).at[rows_dev + pick_rows].add(row_back)
        )
        back_weights, back_norms = (
            lax.all_gather(layer_weights.astype(jnp.bfloat16), ("dp", "seq"), axis=1, tiled=True),
            lax.all_gather(norm_params.astype(jnp.bfloat16), ("dp", "seq"), axis=0, tiled=True),
        )
        stream_grad, weight_grad, norm_grad = layer_backward(
            upstream, back_weights, back_norms, saved, half
        )
        all_grads = lax.all_gather(
            stream_grad[None].astype(jnp.bfloat16), "seq", axis=0, tiled=True
        ).astype(jnp.float32)
        slab_grad = slab_grad.at[local_rows].add(
            jnp.where(inside[:, None], all_grads.reshape(-1, width), 0.0)
        )
        weight_part = lax.psum_scatter(weight_grad, ("dp", "seq"), scatter_dimension=1, tiled=True)
        norm_part = lax.psum_scatter(norm_grad, ("dp", "seq"), scatter_dimension=0, tiled=True)
        weight_acc = weight_acc + weight_part
        norm_acc = norm_acc + norm_part
    embed_grad = lax.psum_scatter(slab_grad, "dp", scatter_dimension=0, tiled=True)
    squares = (
        jnp.sum(embed_grad * embed_grad)
        + jnp.sum(weight_acc * weight_acc)
        + jnp.sum(norm_acc * norm_acc)
    )
    square_total, loss_total = lax.psum((squares, loss_acc / seq_count), ("dp", "seq"))
    grad_norm = jnp.sqrt(square_total)
    factor = jnp.minimum(1.0, CLIP_NORM / grad_norm)
    embed_out = adamw(
        embed_table, embed_first, embed_second, embed_grad * factor, LEARN_RATE, WEIGHT_DECAY
    )
    layer_out = adamw(
        layer_weights, layer_first, layer_second, weight_acc * factor, LEARN_RATE, WEIGHT_DECAY
    )
    norm_out = adamw(norm_params, norm_first, norm_second, norm_acc * factor, NORM_RATE, 0.0)
    return (
        embed_out[0],
        embed_out[1],
        embed_out[2],
        embed_out[3],
        layer_out[0],
        layer_out[1],
        layer_out[2],
        layer_out[3],
        norm_out[0],
        norm_out[1],
        norm_out[2],
        norm_out[3],
        grad_norm,
        loss_total,
    )


def solution(mesh):
    return jax.shard_map(
        on_device,
        mesh=mesh,
        in_specs=(
            P(None, "dp", None, "seq"),
            P(None, "dp", "seq"),
            P(None, "dp", "seq"),
            P(),
            P(),
            P(),
            P(),
            P(("dp", "seq"), None),
            P(("dp", "seq"), None),
            P(("dp", "seq"), None),
            P(None, ("dp", "seq")),
            P(None, ("dp", "seq")),
            P(None, ("dp", "seq")),
            P(("dp", "seq")),
            P(("dp", "seq")),
            P(("dp", "seq")),
        ),
        out_specs=(
            P(("dp", "seq"), None),
            P(("dp", "seq"), None),
            P(("dp", "seq"), None),
            P(("dp", "seq"), None),
            P(None, ("dp", "seq")),
            P(None, ("dp", "seq")),
            P(None, ("dp", "seq")),
            P(None, ("dp", "seq")),
            P(("dp", "seq")),
            P(("dp", "seq")),
            P(("dp", "seq")),
            P(("dp", "seq")),
            P(),
            P(),
        ),
        check_vma=False,
    )
```

profile of v0, /device:TPU:0, one launch (start us, length us, event | category | flops | bytes accessed | tf_op | source)
XLA Modules:
  0.0 2701.3 jit_solution(3871319905073668791)
XLA Ops:
  15.4 23.1 all-gather.17
  39.3 68.0 %all-gather.50.cloned.1.call-done = bf16[2,1572,1088]{1,2,0:T(8,128)(2,1)} async-done(((bf16[1,1572,1088]{1,2,0:T(8,128)(2,1)}), bf16[2,1572,1088]{1,2,0:T(8,128)(2,1)}) %all-gather.50.cloned.1.call-update) | async-done | bytes 6841360 | tf_op jit(solution)/shard_map/all_gather | solution.py:301
  165.9 22.2 all-gather.12
  224.6 40.9 %all-reduce = bf16[6528]{0:T(1024)(128)(2,1)S(1)} all-reduce(bf16[6528]{0:T(1024)(128)(2,1)S(1)} %dynamic-update-slice.4), channel_id=1, replica_groups=mesh['dp'=2,'seq'=16] {'dp','seq'}, use_global_device_ids=true, to_apply=%add | all-reduce | flops 6528 | bytes 26112
  272.9 92.6 %all-gather.32.cloned.1.call-done = bf16[1088,13056]{0,1:T(8,128)(2,1)} async-done(((bf16[1088,408]{0,1:T(8,128)(2,1)}), bf16[1088,13056]{0,1:T(8,128)(2,1)}) %all-gather.32.cloned.1.call-update) | async-done | bytes 28409872 | tf_op jit(solution)/shard_map/all_gather | solution.py:340
  373.0 18.8 reduce-scatter.16.cloned.1.call-done
  412.0 34.9 %all-gather.40.cloned.1.call-done = bf16[2,1024,1088]{2,1,0:T(8,128)(2,1)} async-done(((bf16[2,64,1088]{2,1,0:T(8,128)(2,1)}), bf16[2,1024,1088]{2,1,0:T(8,128)(2,1)}) %all-gather.40.cloned.1.call-update) | async-done | bytes 4456464 | tf_op jit(solution)/shard_map/all_gather | solution.py:134
  455.7 45.7 %all-gather.42.cloned.1.call-done = bf16[2,1024,1088]{2,1,0:T(8,128)(2,1)} async-done(((bf16[2,64,1088]{2,1,0:T(8,128)(2,1)}), bf16[2,1024,1088]{2,1,0:T(8,128)(2,1)}) %all-gather.42.cloned.1.call-update) | async-done | bytes 4456464 | tf_op jit(solution)/shard_map/all_gather | solution.py:131
  510.0 45.8 %all-gather.34.cloned.1.call-done = bf16[2,1024,1088]{2,1,0:T(8,128)(2,1)} async-done(((bf16[2,64,1088]{2,1,0:T(8,128)(2,1)}), bf16[2,1024,1088]{2,1,0:T(8,128)(2,1)}) %all-gather.34.cloned.1.call-update) | async-done | bytes 4456464 | tf_op jit(solution)/shard_map/all_gather | solution.py:134
  684.1 18.3 all-gather.38.cloned.1.call-done
  709.7 19.5 all-gather.14
  731.5 17.5 all-gather.15
  749.0 18.8 all-gather.16
  775.0 17.6 all-gather.18
  794.9 18.8 all-gather.19
  813.7 17.5 all-gather.20
  865.1 50.1 %reduce-scatter.12.cloned.1.call-done = f32[32,1088]{1,0:T(8,128)} async-done(((f32[512,1088]{1,0:T(8,128)}), f32[32,1088]{1,0:T(8,128)}) %reduce-scatter.12.cloned.1.call-update) | async-done | bytes 139280 | tf_op jit(solution)/shard_map/reduce_scatter | solution.py:383
  917.6 64.2 %reduce-scatter.14.cloned.1.call-done = f32[32,1088]{1,0:T(8,128)} async-done(((f32[512,1088]{1,0:T(8,128)}), f32[32,1088]{1,0:T(8,128)}) %reduce-scatter.14.cloned.1.call-update) | async-done | bytes 139280 | tf_op jit(solution)/shard_map/reduce_scatter | solution.py:383
  1157.0 312.9 %all-reduce.19.cloned.1.call-done = (bf16[2,1024,1088]{2,0,1:T(2,128)(2,1)}, bf16[2,1024,1088]{2,0,1:T(2,128)(2,1)}, bf16[2,1024,1088]{2,0,1:T(2,128)(2,1)}, bf16[2,1024,1088]{2,0,1:T(2,128)(2,1)}) async-done(((bf16[2,1024,1088]{2,0,1:T(2,128)(2,1)}, bf16[2,1024,1088]{2,0,1:T(2,128)(2,1)}, bf16[2,1024,1088]{2,0,1:T(2,128)(2,1)}, bf16[2,1024,1088]{2,0,1:T(2,128)(2,1)}), (bf16[2,1024,1088]{2,0,1:T(2,128)(2,1)}, ...) | async-done | bytes 17825808
  1545.9 64.5 %concatenate.68 = f32[1088,13056]{1,0:T(8,128)} concatenate(f32[1088,3264]{1,0:T(8,128)} %fusion.254, f32[1088,1088]{1,0:T(8,128)} %fusion.177, f32[1088,4352]{1,0:T(8,128)} %fusion.260, f32[1088,4352]{1,0:T(8,128)} %fusion.180), dimensions={1} | concatenate | bytes 113639424 | tf_op jit(solution)/shard_map/concatenate | solution.py:252
  1617.8 64.3 %concatenate.69 = f32[1088,13056]{1,0:T(8,128)} concatenate(f32[1088,3264]{1,0:T(8,128)} %fusion.257, f32[1088,1088]{1,0:T(8,128)} %fusion.171, f32[1088,4352]{1,0:T(8,128)} %fusion.261, f32[1088,4352]{1,0:T(8,128)} %fusion.174), dimensions={1} | concatenate | bytes 113639424 | tf_op jit(solution)/shard_map/concatenate | solution.py:252
  1682.0 53.6 %add.883 = f32[1088,13056]{1,0:T(8,128)} add(f32[1088,13056]{1,0:T(8,128)} %concatenate.68, f32[1088,13056]{1,0:T(8,128)} %concatenate.69) | non-fusion elementwise | flops 14204928 | bytes 170459136 | tf_op jit(solution)/shard_map/add | solution.py:404
  1749.0 16.6 convolution_add_fusion
  1765.5 16.7 copy.269
  1815.7 30.5 %scatter_fusion = f32[3144,1088]{1,0:T(8,128)} fusion(f32[3144,1088]{1,0:T(8,128)} %copy.269, s32[2048]{0:T(1024)S(1)} %bitcast.457, f32[2048,1088]{1,0:T(8,128)} %copy.270), kind=kCustom, calls=%fused_computation.11 | custom fusion | flops 2228224 | bytes 26746880 | tf_op jit(solution)/shard_map/scatter-add | solution.py:399
  1846.2 31.1 %scatter_fusion.1 = f32[3144,1088]{1,0:T(8,128)} fusion(f32[3144,1088]{1,0:T(8,128)} %scatter_fusion, s32[2048]{0:T(1024)S(1)} %bitcast.456, f32[2048,1088]{1,0:T(8,128)} %copy.279), kind=kCustom, calls=%fused_computation.13 | custom fusion | flops 2228224 | bytes 26746880 | tf_op jit(solution)/shard_map/scatter-add | solution.py:399
  1877.4 255.6 %fusion = f32[1584,1088]{1,0:T(8,128)} fusion(f32[3144,1088]{1,0:T(8,128)} %scatter_fusion.1), kind=kCustom, calls=%all-reduce-scatter | all-reduce-scatter fusion | flops 3446785 | bytes 20576768
  2172.6 42.5 %all-reduce.9 = f32[6528]{0:T(1024)S(1)} all-reduce(f32[6528]{0:T(1024)S(1)} %add.884), channel_id=26, replica_groups=mesh['dp'=2,'seq'=16] {'dp','seq'}, use_global_device_ids=true, to_apply=%region_81.84.clone | all-reduce | flops 6528 | bytes 52224
  2215.7 19.4 concatenate.76
  2240.7 339.3 %all-reduce.17.cloned.1.call-done = f32[1088,13056]{1,0:T(8,128)} async-done(((f32[1088,13056]{1,0:T(8,128)}), f32[1088,13056]{1,0:T(8,128)}) %all-reduce.17.cloned.1.call-update) | async-done | bytes 56819728
  2585.0 39.3 %all-reduce.12 = (f32[]{:T(128)}, f32[]{:T(128)}) all-reduce(f32[]{:T(128)S(6)} %add.852, f32[]{:T(128)} %bitcast.128), channel_id=1, replica_groups=mesh['dp'=2,'seq'=16] {'dp','seq'}, use_global_device_ids=true, to_apply=%region_90.93 | all-reduce | flops 2 | bytes 16 | tf_op jit(solution)/shard_map/psum | solution.py:412
  2625.0 17.2 fusion.269
  (799 shorter events, 730.9 us)
Async XLA Ops:
  8.0 99.3 %all-gather.50.cloned.1.call-start = ((), (), s32[]{:S(2)}) async-start(), calls=%async_computation.15 | async-start | bytes 10862592 | tf_op jit(solution)/shard_map/all_gather | solution.py:301
  13.4 257.9 %reduce-scatter.18.cloned.1.call-start = ((), (), s32[]{:S(2)}) async-start(), calls=%async_computation.17 | async-start | bytes 5013504
  162.1 203.4 %all-gather.32.cloned.1.call-start = ((), (), s32[]{:S(2)}) async-start(), calls=%async_computation.4 | async-start | bytes 31021056 | tf_op jit(solution)/shard_map/all_gather | solution.py:340
  164.7 227.2 %reduce-scatter.16.cloned.1.call-start = ((), (), s32[]{:S(2)}) async-start(), calls=%async_computation.16 | async-start | bytes 5013504
  223.7 223.2 %all-gather.40.cloned.1.call-start = ((), (), s32[]{:S(2)}) async-start(), calls=%async_computation.8 | async-start | bytes 5013504 | tf_op jit(solution)/shard_map/all_gather | solution.py:134
  265.6 376.4 %copy-start.62 = (f32[1088]{0:T(1024)}, f32[1088]{0:T(1024)S(1)}, u32[]{:S(2)}) copy-start(f32[1088]{0:T(1024)S(1)} %get-tuple-element.621) | copy-start | bytes 13060
  272.6 311.3 %copy-start.22 = (bf16[128,1088]{0,1:T(8,128)(2,1)}, bf16[128,1088]{0,1:T(8,128)(2,1)S(1)}, u32[]{:S(2)}) copy-start(bf16[128,1088]{0,1:T(8,128)(2,1)S(1)} %copy.308) | copy-start | bytes 835588
  372.0 129.4 %all-gather.42.cloned.1.call-start = ((), (), s32[]{:S(2)}) async-start(), calls=%async_computation.9 | async-start | bytes 5013504 | tf_op jit(solution)/shard_map/all_gather | solution.py:131
  373.0 182.8 %all-gather.34.cloned.1.call-start = ((), (), s32[]{:S(2)}) async-start(), calls=%async_computation.5 | async-start | bytes 5013504 | tf_op jit(solution)/shard_map/all_gather | solution.py:134
  393.0 245.9 %copy-start.9 = (bf16[128,1088]{0,1:T(8,128)(2,1)}, bf16[128,1088]{0,1:T(8,128)(2,1)S(1)}, u32[]{:S(2)}) copy-start(bf16[128,1088]{0,1:T(8,128)(2,1)S(1)} %copy.306) | copy-start | bytes 835588
  399.9 210.5 %all-gather.36.cloned.1.call-start = ((), (), s32[]{:S(2)}) async-start(), calls=%async_computation.6 | async-start | bytes 5013504 | tf_op jit(solution)/shard_map/all_gather | solution.py:131
  411.8 290.6 %all-gather.38.cloned.1.call-start = ((), (), s32[]{:S(2)}) async-start(), calls=%async_computation.7 | async-start | bytes 1253376 | tf_op jit(solution)/shard_map/all_gather | solution.py:345
  631.8 399.0 %copy-start.98 = (f32[17,64]{1,0:T(8,128)}, f32[17,64]{1,0:T(8,128)S(1)}, u32[]{:S(2)}) copy-start(f32[17,64]{1,0:T(8,128)S(1)} %get-tuple-element.663) | copy-start | bytes 13060
  641.8 384.0 %copy-start.13 = (f32[128,1088]{0,1:T(8,128)}, f32[128,1088]{0,1:T(8,128)S(1)}, u32[]{:S(2)}) copy-start(f32[128,1088]{0,1:T(8,128)S(1)} %get-tuple-element.668) | copy-start | bytes 1671172
  641.8 384.0 %copy-start.90 = (f32[128]{0:T(128)}, f32[128]{0:T(128)S(1)}, u32[]{:S(2)}) copy-start(f32[128]{0:T(128)S(1)} %broadcast_multiply_fusion.16) | copy-start | bytes 1540
  642.0 383.8 %copy-start.104 = (f32[128]{0:T(128)}, f32[128]{0:T(128)S(1)}, u32[]{:S(2)}) copy-start(f32[128]{0:T(128)S(1)} %add_rsqrt_fusion.4) | copy-start | bytes 1540
  665.4 102.5 %all-gather.44.cloned.1.call-start = ((), (), s32[]{:S(2)}) async-start(), calls=%async_computation.10 | async-start | bytes 1253376 | tf_op jit(solution)/shard_map/all_gather | solution.py:345
  682.4 159.4 %copy-start.100 = (s32[512]{0:T(512)}, s32[512]{0:T(512)S(1)}, u32[]{:S(2)}) copy-start(s32[512]{0:T(512)S(1)} %get-tuple-element.586) | copy-start | bytes 6148
  682.5 170.8 %copy-start.76 = (s32[512]{0:T(512)}, s32[512]{0:T(512)S(1)}, u32[]{:S(2)}) copy-start(s32[512]{0:T(512)S(1)} %get-tuple-element.582) | copy-start | bytes 6148
  682.5 170.8 %copy-start.106 = (pred[512]{0:T(512)(128)(4,1)}, pred[512]{0:T(512)(128)(4,1)S(1)}, u32[]{:S(2)}) copy-start(pred[512]{0:T(512)(128)(4,1)S(1)} %get-tuple-element.583) | copy-start | bytes 1540
  684.0 231.1 %reduce-scatter.12.cloned.1.call-start = ((), (), s32[]{:S(2)}) async-start(), calls=%async_computation.11 | async-start | bytes 2506752 | tf_op jit(solution)/shard_map/reduce_scatter | solution.py:383
  853.2 128.5 %reduce-scatter.14.cloned.1.call-start = ((), (), s32[]{:S(2)}) async-start(), calls=%async_computation.12 | async-start | bytes 2506752 | tf_op jit(solution)/shard_map/reduce_scatter | solution.py:383
  865.0 605.0 %all-reduce.19.cloned.1.call-start = ((), (), s32[]{:S(2)}) async-start(), calls=%async_computation.19 | async-start | bytes 37748736
  1141.9 640.3 %all-gather.46.cloned.1.call-start = ((), (), s32[]{:S(2)}) async-start(), calls=%async_computation.13 | async-start | bytes 4734976 | tf_op jit(solution)/shard_map/all_gather | solution.py:396
  1156.6 315.8 %copy-start.38 = (bf16[128,1088]{1,0:T(8,128)(2,1)S(1)}, bf16[128,1088]{1,0:T(8,128)(2,1)}, u32[]{:S(2)}) copy-start(bf16[128,1088]{1,0:T(8,128)(2,1)} %copy.278) | copy-start | bytes 835588
  1156.8 316.1 %copy-start.23 = (bf16[128,1088]{0,1:T(8,128)(2,1)S(1)}, bf16[128,1088]{0,1:T(8,128)(2,1)}, u32[]{:S(2)}) copy-start(bf16[128,1088]{0,1:T(8,128)(2,1)} %copy-done.22) | copy-start | bytes 835588
  1156.8 316.1 %copy-start.65 = (f32[1088]{0:T(1024)S(1)}, f32[1088]{0:T(1024)}, u32[]{:S(2)}) copy-start(f32[1088]{0:T(1024)} %copy-done.64) | copy-start | bytes 13060
  1156.8 316.1 %copy-start.124 = (f32[128]{0:T(128)S(1)}, f32[128]{0:T(128)}, u32[]{:S(2)}) copy-start(f32[128]{0:T(128)} %copy-done.123) | copy-start | bytes 1540
  1156.8 316.1 %copy-start.131 = (f32[128]{0:T(128)S(1)}, f32[128]{0:T(128)}, u32[]{:S(2)}) copy-start(f32[128]{0:T(128)} %copy-done.130) | copy-start | bytes 1540
  1494.8 304.3 %all-gather.48.cloned.1.call-start = ((), (), s32[]{:S(2)}) async-start(), calls=%async_computation.14 | async-start | bytes 4734976 | tf_op jit(solution)/shard_map/all_gather | solution.py:396
  1495.3 1084.6 %all-reduce.17.cloned.1.call-start = ((), (), s32[]{:S(2)}) async-start(), calls=%async_computation.18 | async-start | bytes 113639424
  2133.8 81.9 %collective-permute-start = (f32[12,1088]{1,0:T(8,128)S(1)}, f32[12,1088]{1,0:T(8,128)S(1)}, u32[]{:S(2)}, u32[]{:S(2)}) collective-permute-start(f32[12,1088]{1,0:T(8,128)S(1)} %slice.396), channel_id=1, source_target_pairs={{0,16},{1,17},{2,18},{3,19},{4,20},{5,21},{6,22},{7,23},{8,24},{9,... | collective-permute-start | bytes 156680
  (151 other events, 2374.2 us)
Sparse Core Ops, SparseCore 0:
  13.5 93.7 all-gather.49
  162.3 109.0 reduce-scatter.17
  275.8 116.0 reduce-scatter.15
  394.6 52.3 all-gather.39
  449.7 51.6 all-gather.41
  504.1 51.6 all-gather.33
  558.6 51.6 all-gather.35
  665.5 36.8 all-gather.37
  705.2 37.2 all-gather.43
  853.4 61.7 reduce-scatter.11
  919.5 62.2 reduce-scatter.13
  1142.1 327.8 all-reduce.18
  1494.9 54.1 all-gather.45
  1551.6 52.2 all-gather.47
Sparse Core Ops, SparseCore 1:
  166.0 199.4 all-gather.31
  1735.8 844.1 all-reduce.16
where the time goes:
time: 2720 us; the launch traced here: 2700 us
  waiting for transfers between devices  1100 us (40%)
  blocking collectives  543 us (20%)
  local copies, waits for them, and re-layouts  473 us (17%)
  matrix products  312 us (11%)
  other arithmetic  235 us (9%)
  between operations  34.3 us (1%)
    unnamed x21, waiting for transfers between devices  678 us
    unnamed x4, blocking collectives  349 us
    dot_general x22, matrix products, contract(): lax.dot_general(left, right, (((left_dim,), (right_dim,)), ((), ())), pre...  189 us
    unnamed x363, local copies, waits for them, and re-layouts  139 us
    concatenate x2, local copies, waits for them, and re-layouts, layer_backward(): jnp.concatenate([qkv_grad, out_grad, up_grad, down_grad], axis=1)  129 us
    reduce_scatter x2, waiting for transfers between devices, on_device(): lax.psum_scatter(contract(logit_grad, slab, 1, 0), 'seq', scatter_dimensi...  114 us
    all_gather x6, blocking collectives, merged(): gathered = jax.tree.map(lambda a: lax.all_gather(a, axis), part)  110 us
    all_gather x1, waiting for transfers between devices, on_device(): lax.all_gather(layer_weights.astype(jnp.bfloat16), ('dp', 'seq'), axis=1,...  92.6 us
  transfers between devices with their start and end apart: 17, of which 13 were waited for; matrix products, arithmetic and copies ran while one was open for 32% of the time, Pallas kernels for 0%

commit v1 on v0

v1 whole, which is shorter than its diff:
```python
import jax
import jax.numpy as jnp
from jax import lax
from jax.sharding import PartitionSpec as P

HEADS = 17
HD = 64
FF = 4352
PICK = 32
CLEN = 512
MB = 2
STEP = 10


EPS_NORM = 1e-05
DPO_BETA = 0.05
CLIP_NORM = 1.0
LEARN_RATE = 0.03
NORM_RATE = 0.4
WEIGHT_DECAY = 0.1
MOMENT_ONE = 0.9
MOMENT_TWO = 0.999
EPS_ADAM = 1e-08
MASKED = -1e30
BF = jnp.bfloat16
F32 = jnp.float32


def contract(left, right, left_dim, right_dim):
    return lax.dot_general(
        left, right, (((left_dim,), (right_dim,)), ((), ())), preferred_element_type=F32
    )


def norm_forward(values, gain, bias):
    centred = values - jnp.mean(values, axis=-1, keepdims=True)
    inverse = lax.rsqrt(jnp.mean(centred * centred, axis=-1, keepdims=True) + EPS_NORM)
    unit = centred * inverse
    return (unit * gain + bias, unit, inverse)


def norm_backward(upstream, unit, inverse, gain):
    scaled = upstream * gain
    inner = (
        scaled
        - jnp.mean(scaled, axis=-1, keepdims=True)
        - unit * jnp.mean(scaled * unit, axis=-1, keepdims=True)
    )
    return (inverse * inner, jnp.sum(upstream * unit, axis=0), jnp.sum(upstream, axis=0))


def probabilities(queries, keys, visible):
    scores = jnp.einsum("mqhe,mkhe->mhqk", queries, keys, preferred_element_type=F32) * HD ** (-0.5)
    scores = jnp.where(visible[None, None], scores, MASKED)
    shifted = jnp.exp(scores - jnp.max(scores, axis=-1, keepdims=True))
    return shifted / jnp.sum(shifted, axis=-1, keepdims=True)


def attend_forward(queries, keys, values, visible):
    probs = probabilities(queries, keys, visible)
    return jnp.einsum("mhqk,mkhe->mqhe", probs.astype(BF), values, preferred_element_type=F32)


def attend_backward(queries, keys, values, visible, grad_out):
    probs = probabilities(queries, keys, visible)
    grad_probs = jnp.einsum("mqhe,mkhe->mhqk", grad_out, values, preferred_element_type=F32)
    grad_scores = (
        probs * (grad_probs - jnp.sum(probs * grad_probs, axis=-1, keepdims=True))
    ).astype(BF)
    scale = HD ** (-0.5)
    grad_query = (
        jnp.einsum("mhqk,mkhe->mqhe", grad_scores, keys, preferred_element_type=F32) * scale
    )
    grad_keys = (
        jnp.einsum("mhqk,mqhe->mkhe", grad_scores, queries, preferred_element_type=F32) * scale
    )
    grad_values = jnp.einsum(
        "mhqk,mqhe->mkhe", probs.astype(BF), grad_out, preferred_element_type=F32
    )
    return (grad_query, grad_keys, grad_values)


def adamw(weight, moment_a, moment_b, gradient, rate, decay):
    moment_a = MOMENT_ONE * moment_a + (1.0 - MOMENT_ONE) * gradient
    moment_b = MOMENT_TWO * moment_b + (1.0 - MOMENT_TWO) * gradient * gradient
    update = (
        moment_a
        / (1.0 - MOMENT_ONE**STEP)
        / (jnp.sqrt(moment_b / (1.0 - MOMENT_TWO**STEP)) + EPS_ADAM)
    )
    weight = weight - rate * (update + decay * weight)
    return (weight, moment_a, moment_b, weight.astype(BF))


def on_device(
    tokens,
    targets,
    counted,
    cont_label,
    pair_map,
    ref_logp,
    vocab_slot,
    embed_table,
    embed_first,
    embed_second,
    layer_weights,
    layer_first,
    layer_second,
    norm_params,
    norm_first,
    norm_second,
):
    seq_count = lax.axis_size("seq")
    group_count = lax.axis_size("dp")
    all_count = seq_count * group_count
    seq_rank = lax.axis_index("seq")
    group_rank = lax.axis_index("dp")
    device_rank = group_rank * seq_count + seq_rank
    rows_dev = tokens.shape[3]
    half = rows_dev * seq_count
    vocab_dev, width = embed_table.shape
    run_count = half // CLEN
    run_devs = CLEN // rows_dev
    own_rows = MB * 2 * rows_dev
    norm_dev = norm_params.shape[0]

    table_t = embed_table.T
    slab_t = lax.all_gather(table_t.astype(BF)[None], "dp", axis=0, tiled=True)
    weights = lax.all_gather(
        layer_weights.T.astype(BF)[None], ("dp", "seq"), axis=0, tiled=True
    ).reshape(-1, width)
    w_q, w_k, w_v, w_o = (weights[i * width : (i + 1) * width] for i in range(4))
    w_qkv = weights[: 3 * width]
    w_kv = weights[width : 3 * width]
    w_up = weights[4 * width : 4 * width + FF]
    w_dn = weights[4 * width + FF :]

    marks = counted[:, 0]
    spots = jnp.arange(rows_dev, dtype=jnp.int32)
    ranks = (
        jnp.sum(jnp.where(spots[None, :, None] <= spots[None, None, :], marks[:, :, None], 0), axis=1)
        - 1
    )
    pick_ids = jnp.arange(PICK, dtype=jnp.int32)
    pick_hit = (ranks[:, None, :] == pick_ids[None, :, None]) & (marks[:, None, :] == 1)
    pick_targets = jnp.sum(jnp.where(pick_hit, targets[:, 0][:, None, :], 0), axis=2)
    pick_low = pick_hit.astype(BF)
    slots = vocab_slot[jnp.concatenate([tokens[:, 0].reshape(-1), pick_targets.reshape(-1)])]
    small = jnp.concatenate([slots.astype(F32), norm_params])
    small = jnp.pad(small, (0, -small.shape[0] % 128)).reshape(1, -1, 128)
    small_all = lax.all_gather(small, ("dp", "seq"), axis=0, tiled=True).reshape(all_count, -1)
    slots_all = lax.dynamic_slice_in_dim(small_all, group_rank * seq_count, seq_count, 0)[
        :, : own_rows + MB * PICK
    ].astype(jnp.int32)
    gains = small_all[:, own_rows + MB * PICK :][:, :norm_dev].astype(BF).astype(F32).reshape(6, width)
    row_slots = slots_all[:, :own_rows].reshape(-1)
    target_slots = slots_all[:, own_rows:].reshape(-1)
    vocab_ids = jnp.arange(vocab_dev, dtype=jnp.int32)

    def hits(slot_ids, part):
        first = (part * seq_count + seq_rank) * vocab_dev
        return (slot_ids - first)[:, None] == vocab_ids[None, :]

    partial = jnp.zeros((row_slots.shape[0], width), F32)
    for part in range(group_count):
        partial = partial + contract(hits(row_slots, part).astype(BF), slab_t[part], 1, 1)
    stream = lax.psum_scatter(
        partial.astype(BF).reshape(seq_count, own_rows, width), "seq", scatter_dimension=0, tiled=True
    )[0].astype(F32)

    normed, unit_one, inverse_one = norm_forward(stream, gains[0], gains[3])
    hidden_one = normed.astype(BF)
    hidden_all = lax.all_gather(
        hidden_one.reshape(1, MB, 2, rows_dev, width), "seq", axis=0, tiled=True
    )
    run_dev = seq_rank // run_devs * run_devs
    prompt_hidden = hidden_all[:, :, 0].transpose(1, 0, 2, 3).reshape(MB, half, width)
    run_hidden = (
        lax.dynamic_slice_in_dim(hidden_all[:, :, 1], run_dev, run_devs, 0)
        .transpose(1, 0, 2, 3)
        .reshape(MB, CLEN, width)
    )
    key_rows = half + CLEN
    hidden_sel = jnp.concatenate([prompt_hidden, run_hidden], axis=1).reshape(MB * key_rows, width)
    keys = contract(hidden_sel, w_k, 1, 1).astype(BF).reshape(MB, key_rows, HEADS, HD)
    values = contract(hidden_sel, w_v, 1, 1).astype(BF).reshape(MB, key_rows, HEADS, HD)
    queries = contract(hidden_one, w_q, 1, 1).astype(BF).reshape(MB, 2 * rows_dev, HEADS, HD)
    start = seq_rank * rows_dev
    query_pos = jnp.concatenate([start + spots, half + (start - run_dev * rows_dev) + spots])
    key_pos = jnp.arange(key_rows, dtype=jnp.int32)
    visible = key_pos[None, :] <= query_pos[:, None]
    attended = attend_forward(queries, keys, values, visible).reshape(own_rows, width).astype(BF)
    stream_one = stream + contract(attended, w_o, 1, 0)
    normed, unit_two, inverse_two = norm_forward(stream_one, gains[1], gains[4])
    hidden_two = normed.astype(BF)
    up_proj = contract(hidden_two, w_up, 1, 1)
    activated = jax.nn.gelu(up_proj, approximate=False).astype(BF)
    stream_two = stream_one + contract(activated, w_dn, 1, 0)
    normed, unit_final, inverse_final = norm_forward(stream_two, gains[2], gains[5])
    final = normed.astype(BF).reshape(MB, 2, rows_dev, width)[:, 1]
    picked = jnp.einsum("mpr,mrd->mpd", pick_low, final, preferred_element_type=F32).astype(BF)

    head_rows = lax.all_gather(
        picked.reshape(1, MB * PICK, width), "seq", axis=0, tiled=True
    ).reshape(seq_count * MB * PICK, width)
    logits = [contract(head_rows, slab_t[part], 1, 0) for part in range(group_count)]
    target_hits = [hits(target_slots, part) for part in range(group_count)]
    highest = jnp.max(logits[0], axis=1)
    for part in range(1, group_count):
        highest = jnp.maximum(highest, jnp.max(logits[part], axis=1))
    summed = jnp.zeros_like(highest)
    target_logit = jnp.zeros_like(highest)
    for part in range(group_count):
        summed = summed + jnp.sum(jnp.exp(logits[part] - highest[:, None]), axis=1)
        target_logit = target_logit + jnp.sum(jnp.where(target_hits[part], logits[part], 0.0), axis=1)
    stats = lax.all_gather(jnp.stack([highest, summed, target_logit])[None], "seq", axis=0, tiled=True)
    overall = jnp.max(stats[:, 0], axis=0)
    total = jnp.sum(stats[:, 1] * jnp.exp(stats[:, 0] - overall[None]), axis=0)
    log_total = overall + jnp.log(total)
    token_lp = jnp.sum(stats[:, 2], axis=0) - log_total

    run_ids = jnp.arange(run_count, dtype=jnp.int32)
    run_of_dev = jnp.arange(seq_count, dtype=jnp.int32) * rows_dev // CLEN
    run_match = run_of_dev[:, None] == run_ids[None, :]
    dev_lp = jnp.sum(token_lp.reshape(seq_count, MB, PICK), axis=2)
    run_lp = jnp.sum(jnp.where(run_match[:, None, :], dev_lp[:, :, None], 0.0), axis=0)
    labels = lax.dynamic_index_in_dim(cont_label, group_rank, 1, keepdims=False)
    pairing = lax.dynamic_index_in_dim(pair_map, group_rank, 1, keepdims=False)
    reference_lp = lax.dynamic_index_in_dim(ref_logp, group_rank, 1, keepdims=False)
    label_match = labels[:, :, None] == run_ids[None, None, :]
    label_lp = jnp.sum(jnp.where(label_match, run_lp[:, :, None], 0.0), axis=1)
    margin = label_lp - reference_lp
    chosen = pairing[:, 0::2, None] == run_ids[None, None, :]
    rejected = pairing[:, 1::2, None] == run_ids[None, None, :]
    delta = jnp.sum(jnp.where(chosen, margin[:, None, :], 0.0), axis=2) - jnp.sum(
        jnp.where(rejected, margin[:, None, :], 0.0), axis=2
    )
    loss = jnp.sum(jax.nn.softplus(-DPO_BETA * delta))
    pair_grad = -DPO_BETA * jax.nn.sigmoid(-DPO_BETA * delta)
    label_grad = jnp.sum(
        jnp.where(chosen, pair_grad[:, :, None], 0.0)
        - jnp.where(rejected, pair_grad[:, :, None], 0.0),
        axis=1,
    )
    run_grad = jnp.sum(jnp.where(label_match, label_grad[:, None, :], 0.0), axis=2)
    dev_grad = jnp.sum(jnp.where(run_match[:, None, :], run_grad[None], 0.0), axis=2)
    row_grad = jnp.broadcast_to(dev_grad[:, :, None], (seq_count, MB, PICK)).reshape(-1)

    head_back = jnp.zeros((head_rows.shape[0], width), F32)
    logit_grads = []
    for part in range(group_count):
        logit_grad = (
            row_grad[:, None]
            * (target_hits[part].astype(F32) - jnp.exp(logits[part] - log_total[:, None]))
        ).astype(BF)
        logit_grads.append(logit_grad)
        head_back = head_back + contract(logit_grad, slab_t[part], 1, 1)
    row_back = lax.psum_scatter(
        head_back.astype(BF).reshape(seq_count, MB * PICK, width),
        "seq",
        scatter_dimension=0,
        tiled=True,
    )[0].reshape(MB, PICK, width)
    cont_back = jnp.einsum("mpr,mpd->mrd", pick_low, row_back, preferred_element_type=F32)
    upstream = jnp.concatenate(
        [jnp.zeros((MB, 1, rows_dev, width), F32), cont_back[:, None]], axis=1
    ).reshape(own_rows, width)

    grad_two, gain_final, bias_final = norm_backward(upstream, unit_final, inverse_final, gains[2])
    grad_ffn = grad_two.astype(BF)
    down_grad = contract(activated, grad_ffn, 0, 0).astype(BF)
    grad_act = contract(grad_ffn, w_dn, 1, 1)
    _, gelu_pull = jax.vjp(lambda pre_act: jax.nn.gelu(pre_act, approximate=False), up_proj)
    grad_up = gelu_pull(grad_act)[0].astype(BF)
    up_grad = contract(grad_up, hidden_two, 0, 0).astype(BF)
    grad_hidden = contract(grad_up, w_up, 1, 0)
    grad_mid, gain_two, bias_two = norm_backward(grad_hidden, unit_two, inverse_two, gains[1])
    grad_one = grad_two + grad_mid
    grad_branch = grad_one.astype(BF)
    out_grad = contract(attended, grad_branch, 0, 0).astype(BF)
    grad_attended = (
        contract(grad_branch, w_o, 1, 1).astype(BF).reshape(MB, 2 * rows_dev, HEADS, HD)
    )
    grad_query, grad_keys, grad_values = attend_backward(
        queries, keys, values, visible, grad_attended
    )
    grad_query = grad_query.astype(BF).reshape(own_rows, width)
    grad_keys = grad_keys.astype(BF).reshape(MB * key_rows, width)
    grad_values = grad_values.astype(BF).reshape(MB * key_rows, width)
    low_sel = (
        contract(grad_keys, w_k, 1, 0) + contract(grad_values, w_v, 1, 0)
    ).astype(BF).reshape(MB, key_rows, width)
    prompt_low = low_sel[:, :half].reshape(MB, seq_count, rows_dev, width).transpose(1, 0, 2, 3)
    run_low = low_sel[:, half:].reshape(MB, run_devs, rows_dev, width).transpose(1, 0, 2, 3)
    blank = jnp.zeros((seq_count, MB, rows_dev, width), BF)
    low_all = jnp.stack(
        [prompt_low, lax.dynamic_update_slice_in_dim(blank, run_low, run_dev, 0)], axis=2
    ).reshape(seq_count, own_rows, width)
    low_own = lax.psum_scatter(low_all, "seq", scatter_dimension=0, tiled=True)[0]
    grad_low = low_own.astype(F32) + contract(grad_query, w_q, 1, 0)
    query_grad = contract(grad_query, hidden_one, 0, 0).astype(BF)
    key_grad = contract(grad_keys, hidden_sel, 0, 0).astype(BF)
    value_grad = contract(grad_values, hidden_sel, 0, 0).astype(BF)
    grad_first, gain_one, bias_one = norm_backward(grad_low, unit_one, inverse_one, gains[0])
    weight_grad = jnp.concatenate(
        [query_grad, key_grad, value_grad, out_grad, up_grad, down_grad], axis=0
    ).reshape(all_count, -1, width)
    weight_sum = lax.psum_scatter(weight_grad, ("dp", "seq"), scatter_dimension=0, tiled=True)[
        0
    ].astype(F32)
    norm_rows = jnp.stack([gain_one, gain_two, gain_final, bias_one, bias_two, bias_final])
    pad_rows = 16
    sent = jnp.concatenate(
        [
            (grad_one + grad_first).astype(BF),
            norm_rows.astype(BF),
            jnp.zeros((pad_rows - 6, width), BF),
        ]
    )
    stream_grads = lax.all_gather(sent[None], "seq", axis=0, tiled=True)
    row_grads = stream_grads[:, :own_rows].reshape(-1, width)
    norm_sum = jnp.sum(stream_grads[:, own_rows : own_rows + 6].astype(F32), axis=0)

    blocks = []
    for part in range(group_count):
        grad_part = contract(head_rows, logit_grads[part], 0, 0) + contract(
            row_grads, hits(row_slots, part).astype(BF), 0, 0
        )
        blocks.append(jnp.concatenate([grad_part, norm_sum.T], axis=1).astype(BF))
    summed_blocks = lax.psum_scatter(jnp.stack(blocks), "dp", scatter_dimension=0, tiled=True)[
        0
    ].astype(F32)
    embed_sum = summed_blocks[:, :vocab_dev]
    norm_all = summed_blocks[:, vocab_dev:].T.reshape(-1)
    norm_own = lax.dynamic_slice_in_dim(norm_all, device_rank * norm_dev, norm_dev, 0)
    squares = (
        jnp.sum(embed_sum * embed_sum)
        + jnp.sum(weight_sum * weight_sum)
        + jnp.sum(norm_own * norm_own)
    )
    square_total, loss_total = lax.psum((squares, loss / seq_count), ("dp", "seq"))
    grad_norm = jnp.sqrt(square_total)
    factor = jnp.minimum(1.0, CLIP_NORM / grad_norm)
    embed_out = adamw(
        table_t, embed_first.T, embed_second.T, embed_sum * factor, LEARN_RATE, WEIGHT_DECAY
    )
    layer_out = adamw(
        layer_weights.T,
        layer_first.T,
        layer_second.T,
        weight_sum * factor,
        LEARN_RATE,
        WEIGHT_DECAY,
    )
    norm_out = adamw(norm_params, norm_first, norm_second, norm_own * factor, NORM_RATE, 0.0)
    return (
        embed_out[0].T,
        embed_out[1].T,
        embed_out[2].T,
        embed_out[3].T,
        layer_out[0].T,
        layer_out[1].T,
        layer_out[2].T,
        layer_out[3].T,
        norm_out[0],
        norm_out[1],
        norm_out[2],
        norm_out[3],
        grad_norm,
        loss_total,
    )


def solution(mesh):
    return jax.shard_map(
        on_device,
        mesh=mesh,
        in_specs=(
            P(None, "dp", None, "seq"),
            P(None, "dp", "seq"),
            P(None, "dp", "seq"),
            P(),
            P(),
            P(),
            P(),
            P(("dp", "seq"), None),
            P(("dp", "seq"), None),
            P(("dp", "seq"), None),
            P(None, ("dp", "seq")),
            P(None, ("dp", "seq")),
            P(None, ("dp", "seq")),
            P(("dp", "seq")),
            P(("dp", "seq")),
            P(("dp", "seq")),
        ),
        out_specs=(
            P(("dp", "seq"), None),
            P(("dp", "seq"), None),
            P(("dp", "seq"), None),
            P(("dp", "seq"), None),
            P(None, ("dp", "seq")),
            P(None, ("dp", "seq")),
            P(None, ("dp", "seq")),
            P(None, ("dp", "seq")),
            P(("dp", "seq")),
            P(("dp", "seq")),
            P(("dp", "seq")),
            P(("dp", "seq")),
            P(),
            P(),
        ),
        check_vma=False,
    )
```

time: 2720 us -> 1760 us (0.65)
  blocking collectives: 543 us -> 104 us
  waiting for transfers between devices: 1100 us -> 850 us
  local copies, waits for them, and re-layouts: 473 us -> 249 us
  other arithmetic: 235 us -> 127 us
  matrix products: 312 us -> 392 us
    unnamed x21 -> x11, waiting for transfers between devices: 678 us -> 174 us
    unnamed x4 -> x0, blocking collectives: 349 us -> none
    reduce_scatter x2 -> x4, waiting for transfers between devices: 114 us -> 344 us  [the longest x1 106 us: on_device(): lax.psum_scatter(partial.astype(BF).reshape(seq_count, own_rows, width),...]
    unnamed x363 -> x185, local copies, waits for them, and re-layouts: 139 us -> 14.6 us
    dot_general x22 -> x28, matrix products: 189 us -> 307 us  [contract(): lax.dot_general(left, right, (((left_dim,), (right_dim,)), ((), ())), pre...]
    all_gather x8 -> x2, blocking collectives: 155 us -> 64.3 us  [the longest x1 44.3 us: on_device(): lax.all_gather(small, ('dp', 'seq'), axis=0, tiled=True)]
    scatter-add x4 -> x0, other arithmetic: 64.6 us -> none  [the longest x2 61.6 us: on_device(): slab_grad.at[local_rows]]
    reshape x2 -> x10, local copies, waits for them, and re-layouts: 2.05 us -> 64 us  [the longest x1 15.9 us: on_device(): contract(hidden_sel, w_k, 1, 1).astype(BF).reshape(MB, key_rows, HEADS, HD)]
  transfers between devices with their start and end apart: 17 -> 10, of which waited for: 13 -> 9; matrix products, arithmetic and copies ran while one was open for 32% -> 14% of each run, Pallas kernels for 0% -> 0%
where the time goes in v1:
time: 1760 us; the launch traced here: 1740 us
  waiting for transfers between devices  850 us (48%)
  matrix products  392 us (22%)
  local copies, waits for them, and re-layouts  249 us (14%)
  other arithmetic  127 us (7%)
  blocking collectives  104 us (6%)
  between operations  20.3 us (1%)
    dot_general x28, matrix products, contract(): lax.dot_general(left, right, (((left_dim,), (right_dim,)), ((), ())), pre...  307 us
    unnamed x11, waiting for transfers between devices  174 us
    all_gather x1, waiting for transfers between devices, on_device(): lax.all_gather(layer_weights.T.astype(BF)[None], ('dp', 'seq'), axis=0, t...  167 us
    reduce_scatter x1, waiting for transfers between devices, on_device(): lax.psum_scatter(partial.astype(BF).reshape(seq_count, own_rows, width),...  106 us
    reduce_scatter x1, waiting for transfers between devices, on_device(): lax.psum_scatter(low_all, 'seq', scatter_dimension=0, tiled=True)[0]  90.5 us
    reduce_scatter x1, waiting for transfers between devices, on_device(): lax.psum_scatter(jnp.stack(blocks), 'dp', scatter_dimension=0, tiled=True)  87.1 us
    concatenate x2, local copies, waits for them, and re-layouts, on_device(): jnp.concatenate([query_grad, key_grad, value_grad, out_grad, up_grad, dow...  82.6 us
    all_gather x1, waiting for transfers between devices, on_device(): lax.all_gather(hidden_one.reshape(1, MB, 2, rows_dev, width), 'seq', axis...  79.2 us
  transfers between devices with their start and end apart: 10, of which 9 were waited for; matrix products, arithmetic and copies ran while one was open for 14% of the time, Pallas kernels for 0%

profile of v1, /device:TPU:0, one launch (start us, length us, event | category | flops | bytes accessed | tf_op | source)
XLA Modules:
  0.0 1744.0 jit_solution(1214689977857050925)
XLA Ops:
  16.0 44.3 %all_gather.21 = f32[32,5,128]{2,1,0:T(8,128)S(1)} all-gather(f32[1,5,128]{2,1,0:T(8,128)S(1)} %fusion.145), channel_id=1, replica_groups=mesh['dp'=2,'seq'=16] {'dp','seq'}, dimensions={0}, use_global_device_ids=true | all-gather | bytes 84480 | tf_op jit(solution)/shard_map/all_gather | solution.py:151
  60.5 46.7 %all-gather.15.cloned.1.call-done = bf16[2176,1572]{1,0:T(8,128)(2,1)} async-done(((bf16[1088,1572]{1,0:T(8,128)(2,1)}), bf16[2176,1572]{1,0:T(8,128)(2,1)}) %all-gather.15.cloned.1.call-update) | async-done | bytes 6841360 | tf_op jit(solution)/shard_map/all_gather | solution.py:128
  107.1 27.7 %fusion.2 = f32[4096,1088]{0,1:T(8,128)} fusion(s32[4096]{0:T(1024)S(1)} %bitcast.327, bf16[2176,1572]{1,0:T(8,128)(2,1)} %all-gather.15.cloned.1.call-done), kind=kOutput, calls=%fused_computation.8 | convolution fusion | flops 14017511424 | bytes 21463040 | tf_op jit(solution)/shard_map/dot_general | solution.py:30
  134.9 20.8 %fusion.7 = bf16[4096,1088]{0,1:T(8,128)(2,1)} fusion(f32[4096,1088]{0,1:T(8,128)} %fusion.2, s32[4096]{0:T(1024)S(1)} %bitcast.329, bf16[2176,1572]{1,0:T(8,128)(2,1)S(1)} %copy-done.81), kind=kOutput, calls=%fused_computation.16 | convolution fusion | flops 14026424320 | bytes 30375936 | tf_op jit(solution)/shard_map/dot_general | solution.py:30
  164.9 106.2 %reduce-scatter.8.cloned.1.call-done = bf16[1,256,1088]{1,2,0:T(8,128)(2,1)} async-done(((bf16[16,256,1088]{1,2,0:T(8,128)(2,1)}), bf16[1,256,1088]{1,2,0:T(8,128)(2,1)}) %reduce-scatter.8.cloned.1.call-update) | async-done | bytes 557072 | tf_op jit(solution)/shard_map/reduce_scatter | solution.py:167
  277.7 79.2 %all-gather.11.cloned.1.call-done = bf16[16,2,2,64,1088]{4,3,2,1,0:T(8,128)(2,1)} async-done(((bf16[1,2,2,64,1088]{4,3,2,1,0:T(8,128)(2,1)}), bf16[16,2,2,64,1088]{4,3,2,1,0:T(8,128)(2,1)}) %all-gather.11.cloned.1.call-update) | async-done | bytes 8912912 | tf_op jit(solution)/shard_map/all_gather | solution.py:173
  369.4 166.9 %all-gather.17.cloned.1.call-done = bf16[13056,1088]{1,0:T(8,128)(2,1)} async-done(((bf16[408,1088]{1,0:T(8,128)(2,1)}), bf16[13056,1088]{1,0:T(8,128)(2,1)}) %all-gather.17.cloned.1.call-update) | async-done | bytes 28409872 | tf_op jit(solution)/shard_map/all_gather | solution.py:129
  536.3 14.2 convolution_convert_fusion.3
  550.4 15.7 reshape.790
  566.2 14.2 convolution_convert_fusion.2
  580.3 15.9 reshape.792
  599.3 15.6 fusion.42
  614.9 30.3 %fusion.160 = (f32[2,17,128]{2,1,0:T(8,128)S(1)}, f32[2,17,128,1536]{3,2,1,0:T(8,128)}) fusion(f32[2,17,128,1536]{3,2,1,0:T(8,128)} %fusion.42, pred[128,1536]{1,0:T(8,128)(4,1)S(1)} %iota_compare_fusion.24), kind=kOutput, calls=%fused_computation.309 | output fusion | flops 40109568 | bytes 53691392 | tf_op jit(solution)/shard_map/sub | solution.py:55
  645.2 13.5 fusion.96
  662.7 16.6 multiply_convert_fusion.4
  693.0 39.1 %all-gather.13.cloned.1.call-done = bf16[16,64,1088]{2,1,0:T(8,128)(2,1)} async-done(((bf16[1,64,1088]{2,1,0:T(8,128)(2,1)}), bf16[16,64,1088]{2,1,0:T(8,128)(2,1)}) %all-gather.13.cloned.1.call-update) | async-done | bytes 2228240 | tf_op jit(solution)/shard_map/all_gather | solution.py:203
  751.6 20.0 %all-gather.4 = f32[16,3,1024]{2,1,0:T(4,128)S(1)} all-gather(f32[1,3,1024]{2,1,0:T(4,128)S(1)} %maximum_bitcast_fusion), channel_id=4, replica_groups=mesh['dp'=2,'seq'=16] {'seq'}, dimensions={0}, use_global_device_ids=true | all-gather | bytes 208896 | tf_op jit(solution)/shard_map/all_gather | solution.py:216
  793.9 60.6 %reduce-scatter.10.cloned.1.call-done = bf16[1,64,1088]{2,1,0:T(8,128)(2,1)} async-done(((bf16[16,64,1088]{2,1,0:T(8,128)(2,1)}), bf16[1,64,1088]{2,1,0:T(8,128)(2,1)}) %reduce-scatter.10.cloned.1.call-update) | async-done | bytes 139280 | tf_op jit(solution)/shard_map/reduce_scatter | solution.py:258
  883.1 22.8 %multiply_reduce_fusion = (f32[2,17,128]{2,1,0:T(8,128)S(1)}, f32[2,17,128,1536]{3,2,1,0:T(8,128)}) fusion(f32[2,17,128,1536]{3,2,1,0:T(8,128)} %get-tuple-element.75, f32[2,17,128]{2,1,0:T(8,128)S(1)} %copy-done.44, bf16[2,1536,17,64]{1,0,3,2:T(2,128)(2,1)} %reshape.790, bf16[2,128,17,64]{1,0,3,2:T(2,128)(2,1)S(1)} %reshape.798), kind=kOutput, calls=%fused_computation.3 | convolution fusion | flops 875687680 | bytes 60753920 | tf_op jit(solution)/shard_map/mqhe,mkhe->mhqk/dot_general | solution.py:66
  918.7 17.1 multiply_convert_fusion
  942.7 13.4 copy.281
  991.7 15.7 fusion.15
  1075.2 90.5 %reduce-scatter.12.cloned.1.call-done = bf16[1,256,1088]{1,2,0:T(8,128)(2,1)} async-done(((bf16[16,256,1088]{1,2,0:T(8,128)(2,1)}), bf16[1,256,1088]{1,2,0:T(8,128)(2,1)}) %reduce-scatter.12.cloned.1.call-update) | async-done | bytes 557072 | tf_op jit(solution)/shard_map/reduce_scatter | solution.py:299
  1205.7 13.8 convolution_convert_fusion.6
  1219.4 47.2 %concatenate.86 = bf16[13056,1088]{0,1:T(8,128)(2,1)} concatenate(bf16[1088,1088]{0,1:T(8,128)(2,1)} %convolution_convert_fusion.5, bf16[1088,1088]{0,1:T(8,128)(2,1)} %convolution_convert_fusion.7, bf16[1088,1088]{0,1:T(8,128)(2,1)} %convolution_convert_fusion.6, bf16[1088,1088]{0,1:T(8,128)(2,1)S(1)} %copy-done.12, bf16[4352,1088]{0,1:T(8,128)(2,1)} %convolution_convert_fusion.1, ...), dimensions={0} | concatenate | bytes 56819712 | tf_op jit(solution)/shard_map/concatenate | solution.py:305
  1266.6 35.4 %copy.301 = bf16[13056,1088]{1,0:T(8,128)(2,1)} copy(bf16[13056,1088]{0,1:T(8,128)(2,1)} %concatenate.86) | data formatting | bytes 56819712 | tf_op jit(solution)/shard_map/concatenate | solution.py:305
  1339.5 24.4 %fusion.35 = bf16[1,1088,1572]{2,1,0:T(8,128)(2,1)} fusion(f32[1088,1572]{1,0:T(8,128)} %fusion.154, bf16[4096,1088]{1,0:T(8,128)(2,1)} %bitcast.292, s32[4096]{0:T(1024)S(1)} %bitcast.330), kind=kOutput, calls=%fused_computation.66 | convolution fusion | flops 14020931584 | bytes 19191296 | tf_op jit(solution)/shard_map/dot_general | solution.py:30
  1364.0 22.6 %fusion.36 = bf16[1,1088,1572]{2,1,0:T(8,128)(2,1)} fusion(f32[1088,1572]{1,0:T(8,128)} %fusion.155, bf16[4096,1088]{1,0:T(8,128)(2,1)S(1)} %bitcast.293, s32[4096]{0:T(1024)S(1)} %bitcast.328), kind=kOutput, calls=%fused_computation.67 | convolution fusion | flops 14020931584 | bytes 19191296 | tf_op jit(solution)/shard_map/dot_general | solution.py:30
  1395.4 173.5 %reduce-scatter.16.cloned.1.call-done = bf16[1,408,1088]{2,1,0:T(8,128)(2,1)} async-done(((bf16[32,408,1088]{2,1,0:T(8,128)(2,1)}), bf16[1,408,1088]{2,1,0:T(8,128)(2,1)}) %reduce-scatter.16.cloned.1.call-update) | async-done | bytes 887824
  1571.2 87.1 %reduce-scatter.14.cloned.1.call-done = bf16[1,1088,1578]{2,1,0:T(8,128)(2,1)} async-done(((bf16[2,1088,1578]{2,1,0:T(8,128)(2,1)}), bf16[1,1088,1578]{2,1,0:T(8,128)(2,1)}) %reduce-scatter.14.cloned.1.call-update) | async-done | bytes 3433744 | tf_op jit(solution)/shard_map/reduce_scatter | solution.py:330
  1666.9 39.5 %all-reduce.3 = (f32[]{:T(128)}, f32[]{:T(128)}) all-reduce(f32[]{:T(128)S(6)} %add.330, f32[]{:T(128)S(6)} %div.178), channel_id=1, replica_groups=mesh['dp'=2,'seq'=16] {'dp','seq'}, use_global_device_ids=true, to_apply=%region_48.49 | all-reduce | flops 2 | bytes 16 | tf_op jit(solution)/shard_map/psum | solution.py:341
  1707.2 21.5 %convert_bitcast_fusion.1 = (bf16[1572,1088]{0,1:T(8,128)(2,1)}, f32[1088,1572]{1,0:T(8,128)}, f32[1572,1088]{0,1:T(8,128)}, f32[1572,1088]{0,1:T(8,128)}) fusion(f32[1572,1088]{0,1:T(8,128)} %param.25, f32[]{:T(128)S(6)} %min.3, f32[1088,1578]{1,0:T(8,128)} %copy-done.3, f32[1572,1088]{0,1:T(8,128)} %param.24, f32[1572,1088]{0,1:T(8,128)} %param.23), kind=kLoop, calls=%fused_computation.107 | loop fusion | flops 29075712 | bytes 51310084 | tf_op jit(solution)/shard_map/transpose | solution.py:360
  (358 shorter events, 351.8 us)
Async XLA Ops:
  7.2 99.9 %all-gather.15.cloned.1.call-start = ((), (), s32[]{:S(2)}) async-start(), calls=%async_computation.11 | async-start | bytes 10862592 | tf_op jit(solution)/shard_map/all_gather | solution.py:128
  12.6 258.6 %reduce-scatter.8.cloned.1.call-start = ((), (), s32[]{:S(2)}) async-start(), calls=%async_computation.5 | async-start | bytes 9469952 | tf_op jit(solution)/shard_map/reduce_scatter | solution.py:167
  60.4 74.5 %copy-start.33 = (s32[16,320]{1,0:T(8,128)}, s32[16,320]{1,0:T(8,128)S(1)}, u32[]{:S(2)}) copy-start(s32[16,320]{1,0:T(8,128)S(1)} %dynamic-slice_convert_fusion) | copy-start | bytes 61444
  60.4 74.4 %copy-start.57 = (s32[2,2,8,128]{3,1,2,0:T(2,128)}, s32[2,2,8,128]{3,1,2,0:T(2,128)S(1)}, u32[]{:S(2)}) copy-start(s32[2,2,8,128]{3,1,2,0:T(2,128)S(1)} %copy.316) | copy-start | bytes 49156
  60.5 74.4 %copy-start.59 = (s32[2,2,8,128]{3,1,2,0:T(2,128)}, s32[2,2,8,128]{3,1,2,0:T(2,128)S(1)}, u32[]{:S(2)}) copy-start(s32[2,2,8,128]{3,1,2,0:T(2,128)S(1)} %copy.315) | copy-start | bytes 49156
  107.1 27.7 %copy-start.81 = (bf16[2176,1572]{1,0:T(8,128)(2,1)S(1)}, bf16[2176,1572]{1,0:T(8,128)(2,1)}, u32[]{:S(2)}) copy-start(bf16[2176,1572]{1,0:T(8,128)(2,1)} %all-gather.15.cloned.1.call-done) | copy-start | bytes 20524036
  163.6 112.7 %copy-start.16 = (f32[1088,408]{0,1:T(8,128)S(1)}, f32[1088,408]{0,1:T(8,128)}, u32[]{:S(2)}) copy-start(f32[1088,408]{0,1:T(8,128)} %param.26) | copy-start | bytes 5326852
  163.6 193.4 %all-gather.11.cloned.1.call-start = ((), (), s32[]{:S(2)}) async-start(), calls=%async_computation.6 | async-start | bytes 10027008 | tf_op jit(solution)/shard_map/all_gather | solution.py:173
  164.9 431.3 %copy-start.34 = (f32[1088]{0:T(1024)}, f32[1088]{0:T(1024)S(1)}, u32[]{:S(2)}) copy-start(f32[1088]{0:T(1024)S(1)} %get-tuple-element.37) | copy-start | bytes 13060
  164.9 431.4 %copy-start.38 = (f32[1088]{0:T(1024)}, f32[1088]{0:T(1024)S(1)}, u32[]{:S(2)}) copy-start(f32[1088]{0:T(1024)S(1)} %get-tuple-element.36) | copy-start | bytes 13060
  164.9 497.7 %copy-start.36 = (f32[1088]{0:T(1024)}, f32[1088]{0:T(1024)S(1)}, u32[]{:S(2)}) copy-start(f32[1088]{0:T(1024)S(1)} %get-tuple-element.34) | copy-start | bytes 13060
  164.9 714.0 %copy-start.31 = (f32[1088]{0:T(1024)}, f32[1088]{0:T(1024)S(1)}, u32[]{:S(2)}) copy-start(f32[1088]{0:T(1024)S(1)} %get-tuple-element.35) | copy-start | bytes 13060
  272.4 323.9 %copy-start.45 = (f32[256]{0:T(256)}, f32[256]{0:T(256)S(1)}, u32[]{:S(2)}) copy-start(f32[256]{0:T(256)S(1)} %broadcast_multiply_fusion.8) | copy-start | bytes 3076
  273.8 322.5 %copy-start.61 = (f32[256]{0:T(256)}, f32[256]{0:T(256)S(1)}, u32[]{:S(2)}) copy-start(f32[256]{0:T(256)S(1)} %add_rsqrt_fusion.2) | copy-start | bytes 3076
  276.3 260.0 %all-gather.17.cloned.1.call-start = ((), (), s32[]{:S(2)}) async-start(), calls=%async_computation.12 | async-start | bytes 31021056 | tf_op jit(solution)/shard_map/all_gather | solution.py:129
  277.4 454.7 %all-gather.13.cloned.1.call-start = ((), (), s32[]{:S(2)}) async-start(), calls=%async_computation.7 | async-start | bytes 2506752 | tf_op jit(solution)/shard_map/all_gather | solution.py:203
  662.4 216.5 %copy-start.8 = (f32[256,1088]{0,1:T(8,128)}, f32[256,1088]{0,1:T(8,128)S(1)}, u32[]{:S(2)}) copy-start(f32[256,1088]{0,1:T(8,128)S(1)} %get-tuple-element.77) | copy-start | bytes 3342340
  662.4 216.5 %copy-start.41 = (f32[256]{0:T(256)}, f32[256]{0:T(256)S(1)}, u32[]{:S(2)}) copy-start(f32[256]{0:T(256)S(1)} %broadcast_multiply_fusion.7) | copy-start | bytes 3076
  662.6 216.3 %copy-start.49 = (f32[256]{0:T(256)}, f32[256]{0:T(256)S(1)}, u32[]{:S(2)}) copy-start(f32[256]{0:T(256)S(1)} %add_rsqrt_fusion.1) | copy-start | bytes 3076
  691.4 163.0 %reduce-scatter.10.cloned.1.call-start = ((), (), s32[]{:S(2)}) async-start(), calls=%async_computation.8 | async-start | bytes 2506752 | tf_op jit(solution)/shard_map/reduce_scatter | solution.py:258
  692.7 89.1 %copy-start.51 = (s32[1024]{0:T(1024)}, s32[1024]{0:T(1024)S(1)}, u32[]{:S(2)}) copy-start(s32[1024]{0:T(1024)S(1)} %sub.279) | copy-start | bytes 12292
  692.8 81.0 %copy-start.53 = (s32[1024]{0:T(1024)}, s32[1024]{0:T(1024)S(1)}, u32[]{:S(2)}) copy-start(s32[1024]{0:T(1024)S(1)} %sub.276) | copy-start | bytes 12292
  793.8 371.9 %reduce-scatter.12.cloned.1.call-start = ((), (), s32[]{:S(2)}) async-start(), calls=%async_computation.9 | async-start | bytes 9469952 | tf_op jit(solution)/shard_map/reduce_scatter | solution.py:299
  1059.0 106.7 %copy-start.15 = (bf16[1,256,1088]{1,2,0:T(8,128)(2,1)S(1)}, bf16[1,256,1088]{1,2,0:T(8,128)(2,1)}, u32[]{:S(2)}) copy-start(bf16[1,256,1088]{1,2,0:T(8,128)(2,1)} %reduce-scatter.8.cloned.1.call-done) | copy-start | bytes 1671172
  1059.0 106.7 %copy-start.35 = (f32[1088]{0:T(1024)S(1)}, f32[1088]{0:T(1024)}, u32[]{:S(2)}) copy-start(f32[1088]{0:T(1024)} %copy-done.34) | copy-start | bytes 13060
  1059.0 106.7 %copy-start.46 = (f32[256]{0:T(256)S(1)}, f32[256]{0:T(256)}, u32[]{:S(2)}) copy-start(f32[256]{0:T(256)} %copy-done.45) | copy-start | bytes 3076
  1059.1 106.6 %copy-start.62 = (f32[256]{0:T(256)S(1)}, f32[256]{0:T(256)}, u32[]{:S(2)}) copy-start(f32[256]{0:T(256)} %copy-done.61) | copy-start | bytes 3076
  1059.1 268.1 %all-gather.19.cloned.1.call-start = ((), (), s32[]{:S(2)}) async-start(), calls=%async_computation.13 | async-start | bytes 10653696 | tf_op jit(solution)/shard_map/all_gather | solution.py:320
  1072.2 97.1 %copy-start.29 = (bf16[2,128,17,64]{1,0,3,2:T(2,128)(2,1)}, bf16[2,128,17,64]{1,0,3,2:T(2,128)(2,1)S(1)}, u32[]{:S(2)}) copy-start(bf16[2,128,17,64]{1,0,3,2:T(2,128)(2,1)S(1)} %copy.291) | copy-start | bytes 1671172
  1176.4 392.5 %reduce-scatter.16.cloned.1.call-start = ((), (), s32[]{:S(2)}) async-start(), calls=%async_computation.14 | async-start | bytes 31021056
  1302.1 356.2 %reduce-scatter.14.cloned.1.call-start = ((), (), s32[]{:S(2)}) async-start(), calls=%async_computation.10 | async-start | bytes 10862592 | tf_op jit(solution)/shard_map/reduce_scatter | solution.py:330
  1339.5 24.5 %copy-start.13 = (bf16[16,256,1088]{2,1,0:T(8,128)(2,1)S(1)}, bf16[16,256,1088]{2,1,0:T(8,128)(2,1)}, u32[]{:S(2)}) copy-start(bf16[16,256,1088]{2,1,0:T(8,128)(2,1)} %slice.174) | copy-start | bytes 26738692
  (66 other events, 601.5 us)
Sparse Core Ops, SparseCore 0:
  12.7 94.3 all-gather.14
  163.7 107.4 reduce-scatter.7
  276.4 80.5 all-gather.10
  360.2 175.9 all-gather.16
  691.6 40.4 all-gather.12
  794.0 60.4 reduce-scatter.9
  1059.1 106.5 reduce-scatter.11
  1176.5 84.2 all-gather.18
  1302.2 266.6 reduce-scatter.15
  1571.6 86.6 reduce-scatter.13

commit v2 on v1

v2 whole, which is shorter than its diff:
```python
import functools

import jax
import jax.numpy as jnp
from jax import lax
from jax.experimental import pallas as pl
from jax.experimental.pallas import tpu as pltpu
from jax.sharding import PartitionSpec as P

HEADS = 17
HD = 64
FF = 4352
PICK = 32
CLEN = 512
MB = 2
STEP = 10


EPS_NORM = 1e-05
DPO_BETA = 0.05
CLIP_NORM = 1.0
LEARN_RATE = 0.03
NORM_RATE = 0.4
WEIGHT_DECAY = 0.1
MOMENT_ONE = 0.9
MOMENT_TWO = 0.999
EPS_ADAM = 1e-08
MASKED = -1e30
BF = jnp.bfloat16
F32 = jnp.float32
MESH = pl.DeviceIdType.MESH
VMEM = pltpu.VMEM


def meet(peers):
    barrier = pltpu.get_barrier_semaphore()
    for there, peer in peers:

        @pl.when(there)
        def _():
            pl.semaphore_signal(barrier, inc=1, device_id=peer, device_id_type=MESH)

    pl.semaphore_wait(barrier, sum(jnp.where(there, 1, 0) for there, _ in peers))


def direct_kernel(whole, x_ref, o_ref, send_sem, recv_sem):
    seq_count = lax.axis_size("seq")
    group_rank = lax.axis_index("dp")
    me = lax.axis_index("seq")
    count = o_ref.shape[0]
    if whole:
        me = group_rank * seq_count + me

    def peer(step):
        other = lax.rem(me + step, count)
        if whole:
            return (other // seq_count, lax.rem(other, seq_count))
        return (group_rank, other)

    barrier = pltpu.get_barrier_semaphore()

    def greet(step, carry):
        pl.semaphore_signal(barrier, inc=1, device_id=peer(step), device_id_type=MESH)
        return carry

    lax.fori_loop(1, count, greet, 0)
    o_ref[me] = x_ref[...]
    pl.semaphore_wait(barrier, count - 1)

    def copy(step):
        return pltpu.make_async_remote_copy(
            src_ref=x_ref,
            dst_ref=o_ref.at[me],
            send_sem=send_sem.at[step],
            recv_sem=recv_sem.at[step],
            device_id=peer(step),
            device_id_type=MESH,
        )

    def begin(step, carry):
        copy(step).start()
        return carry

    def finish(step, carry):
        copy(step).wait()
        return carry

    lax.fori_loop(1, count, begin, 0)
    lax.fori_loop(1, count, finish, 0)


def direct_gather(x, whole, collective_id):
    count = lax.axis_size("seq") * (lax.axis_size("dp") if whole else 1)
    return pl.pallas_call(
        functools.partial(direct_kernel, whole),
        out_shape=jax.ShapeDtypeStruct((count,) + x.shape, x.dtype),
        in_specs=[pl.BlockSpec(memory_space=VMEM)],
        out_specs=pl.BlockSpec(memory_space=VMEM),
        scratch_shapes=[pltpu.SemaphoreType.DMA((count,)), pltpu.SemaphoreType.DMA((count,))],
        compiler_params=pltpu.CompilerParams(collective_id=collective_id, has_side_effects=True),
    )(x)


def place(rank):
    return (rank // 4, lax.rem(rank, 4) // 2, lax.rem(rank, 2))


def line_peers(at, side, core, group, line):
    return [
        (at > 0, (group, 4 * (at - 1) + 2 * side + core)),
        (at < line - 1, (group, 4 * (at + 1) + 2 * side + core)),
        (at >= 0, (group, 4 * at + 2 * (1 - side) + core)),
        (at >= 0, (group, 4 * at + 2 * side + 1 - core)),
    ]


def spread_kernel(parts, count, *refs):
    given, wanted, pieces = parts
    total = len(pieces)
    x_refs, o_refs = refs[:given], refs[given : given + wanted]
    local_sem, z_send, z_recv, b_send, b_recv, c_send, c_recv = refs[given + wanted :]
    spans = [piece[0] for piece in pieces]
    ins = [piece[1](x_refs) for piece in pieces]
    line = count // 4
    group = lax.axis_index("dp")
    at, side, core = place(lax.axis_index("seq"))
    peers = line_peers(at, side, core, group, line)
    below, above, beside, sibling = (peer for _, peer in peers)
    meet(peers)

    def seq_of(where, which_side, which_core):
        return 4 * where + 2 * which_side + which_core

    def remote(src, dst, send, recv, peer):
        return pltpu.make_async_remote_copy(
            src_ref=src, dst_ref=dst, send_sem=send, recv_sem=recv, device_id=peer, device_id_type=MESH
        )

    def low_high(span):
        low = at // span * span
        return low, low + span

    def view(part, where, which_side, which_core):
        return pieces[part][2](o_refs, seq_of(where, which_side, which_core))

    def where_of(item):
        far = (item + 1) // 2
        return at - far if item % 2 else at + far

    def valid(part, item):
        low, high = low_high(spans[part])
        where = where_of(item)
        return (where >= low) & (where < high)

    def z_copy(part, item, up):
        where = where_of(item)
        far = (item + 1) // 2 + 1
        mark = 2 * far - 1 if up else 2 * far
        src = ins[part] if item == 0 else view(part, where, side, core)
        return remote(
            src,
            view(part, where, side, core),
            z_send.at[part, mark],
            z_recv.at[part, mark],
            above if up else below,
        )

    def b_copy(part, item):
        where = where_of(item)
        src = ins[part] if item == 0 else view(part, where, side, core)
        return remote(
            src, view(part, where, side, core), b_send.at[part, item], b_recv.at[part, item], beside
        )

    def b_arrived(part, item):
        where = where_of(item)
        spot = view(part, where, 1 - side, core)
        return remote(spot, spot, b_send.at[part, item], b_recv.at[part, item], beside)

    def z_arrived(part, item):
        spot = view(part, where_of(item), side, core)
        return remote(spot, spot, z_send.at[part, item], z_recv.at[part, item], beside)

    def c_copy(part, item, from_side):
        where = where_of(item)
        mine = item == 0 and not from_side
        which = 1 - side if from_side else side
        src = ins[part] if mine else view(part, where, which, core)
        index = 2 * item + from_side
        return remote(
            src, view(part, where, which, core), c_send.at[part, index], c_recv.at[part, index], sibling
        )

    def c_arrived(part, item, from_side):
        which = 1 - side if from_side else side
        spot = view(part, where_of(item), which, 1 - core)
        index = 2 * item + from_side
        return remote(spot, spot, c_send.at[part, index], c_recv.at[part, index], sibling)

    items = 2 * line - 1

    def goes_up(part, item):
        low, high = low_high(spans[part])
        return at + 1 < high

    def goes_down(part, item):
        low, high = low_high(spans[part])
        return at - 1 >= low

    def active(part, item):
        return (item + 1) // 2 < spans[part]

    for part in range(total):
        pltpu.make_async_copy(
            ins[part], view(part, at, side, core), local_sem.at[part]
        ).start()

    def launch(part, item):
        @pl.when(valid(part, item))
        def _():
            if item == 0 or item % 2 == 1:
                if (item + 1) // 2 + 1 < spans[part]:
                    @pl.when(goes_up(part, item))
                    def _():
                        z_copy(part, item, True).start()
            if item == 0 or item % 2 == 0:
                if (item + 1) // 2 + 1 < spans[part]:
                    @pl.when(goes_down(part, item))
                    def _():
                        z_copy(part, item, False).start()
            b_copy(part, item).start()
            c_copy(part, item, 0).start()

    def relay(part, item):
        @pl.when(valid(part, item))
        def _():
            b_arrived(part, item).wait_recv()
            c_copy(part, item, 1).start()

    for part in range(total):
        launch(part, 0)
    for far in range(1, line + 1):
        for item in (2 * far - 1, 2 * far):
            for part in range(total):
                if far < line and active(part, item):
                    @pl.when(valid(part, item))
                    def _():
                        z_arrived(part, item).wait_recv()
                    launch(part, item)
        last = [0] if far == 1 else [2 * far - 3, 2 * far - 2]
        for item in last:
            for part in range(total):
                if active(part, item):
                    relay(part, item)
    for part in range(total):
        pltpu.make_async_copy(ins[part], view(part, at, side, core), local_sem.at[part]).wait()
        for item in range(items):
            if not active(part, item):
                continue

            @pl.when(valid(part, item))
            def _():
                if (item == 0 or item % 2 == 1) and (item + 1) // 2 + 1 < spans[part]:
                    @pl.when(goes_up(part, item))
                    def _():
                        z_copy(part, item, True).wait_send()
                if (item == 0 or item % 2 == 0) and (item + 1) // 2 + 1 < spans[part]:
                    @pl.when(goes_down(part, item))
                    def _():
                        z_copy(part, item, False).wait_send()
                b_copy(part, item).wait_send()
                c_copy(part, item, 0).wait_send()
                c_copy(part, item, 1).wait_send()
                c_arrived(part, item, 0).wait_recv()
                c_arrived(part, item, 1).wait_recv()


def spread(blocks, out_shapes, pieces, collective_id):
    count = lax.axis_size("seq")
    total = len(pieces)
    items = 2 * (count // 4) + 1
    sem = pltpu.SemaphoreType.DMA
    return pl.pallas_call(
        functools.partial(spread_kernel, (len(blocks), len(out_shapes), pieces), count),
        out_shape=out_shapes,
        in_specs=[pl.BlockSpec(memory_space=VMEM)] * len(blocks),
        out_specs=[pl.BlockSpec(memory_space=pl.ANY)] * len(out_shapes),
        scratch_shapes=[sem((total,))] + [sem((total, items))] * 4 + [sem((total, 2 * items))] * 2,
        compiler_params=pltpu.CompilerParams(collective_id=collective_id, has_side_effects=True),
    )(*blocks)


def fold_kernel(parts, count, *refs):
    given, wanted, pieces = parts
    total = len(pieces)
    spans = [piece[0] for piece in pieces]
    x_refs, o_refs = refs[:given], refs[given : given + wanted]
    scratch = refs[given + wanted :]
    outs = [piece[3](o_refs) for piece in pieces]
    c_bufs, s_bufs, b_bufs, u_bufs, d_bufs, t_bufs = (
        scratch[i * total : (i + 1) * total] for i in range(6)
    )
    c_send, c_recv, b_send, b_recv, u_send, u_recv, d_send, d_recv = scratch[6 * total :]
    line = count // 4
    group = lax.axis_index("dp")
    at, side, core = place(lax.axis_index("seq"))
    peers = line_peers(at, side, core, group, line)
    below, above, beside, sibling = (peer for _, peer in peers)
    meet(peers)

    def remote(src, dst, send, recv, peer):
        return pltpu.make_async_remote_copy(
            src_ref=src, dst_ref=dst, send_sem=send, recv_sem=recv, device_id=peer, device_id_type=MESH
        )

    def view(part, where, which_side, which_core):
        return pieces[part][2](x_refs, 4 * where + 2 * which_side + which_core)

    def valid(part, where):
        low = at // spans[part] * spans[part]
        return (where >= low) & (where < low + spans[part])

    def slot(part, where):
        return lax.rem(where, spans[part])

    order = []
    for far in range(line - 1, 0, -1):
        order += [(far, 1), (far, -1)]
    order.append((0, 1))

    def c_copy(part, where, other):
        which = 1 - side if other else side
        index = 2 * slot(part, where) + other
        return remote(
            view(part, where, which, 1 - core),
            c_bufs[part].at[index],
            c_send.at[part, index],
            c_recv.at[part, index],
            sibling,
        )

    def b_copy(part, where):
        index = slot(part, where)
        return remote(
            s_bufs[part].at[index], b_bufs[part].at[index], b_send.at[part, index], b_recv.at[part, index], beside
        )

    def u_copy(part, where):
        index = slot(part, where)
        return remote(
            t_bufs[part].at[index], u_bufs[part].at[index], u_send.at[part, index], u_recv.at[part, index], above
        )

    def d_copy(part, where):
        index = slot(part, where)
        return remote(
            t_bufs[part].at[index], d_bufs[part].at[index], d_send.at[part, index], d_recv.at[part, index], below
        )

    def each(action):
        for far, sign in order:
            for part in range(total):
                if far >= spans[part]:
                    continue
                where = at + sign * far

                @pl.when(valid(part, where))
                def _():
                    action(part, where, far, sign)

    each(lambda part, where, far, sign: c_copy(part, where, 1).start())
    each(lambda part, where, far, sign: c_copy(part, where, 0).start())

    def aside(part, where, far, sign):
        c_copy(part, where, 1).wait_recv()
        index = slot(part, where)
        mine = view(part, where, 1 - side, core)[...]
        s_bufs[part][index] = (
            mine.astype(F32) + c_bufs[part][2 * index + 1].astype(F32)
        ).astype(BF)
        b_copy(part, where).start()

    each(aside)

    def along(part, where, far, sign):
        c_copy(part, where, 0).wait_recv()
        b_copy(part, where).wait_recv()
        index = slot(part, where)
        here = slot(part, at)
        value = (
            view(part, where, side, core)[...].astype(F32)
            + c_bufs[part][2 * index].astype(F32)
            + b_bufs[part][index].astype(F32)
        )
        if far == 0:
            outs[part][...] = value

            @pl.when(here > 0)
            def _():
                u_copy(part, where).wait_recv()
                outs[part][...] += u_bufs[part][index].astype(F32)

            @pl.when(here < spans[part] - 1)
            def _():
                d_copy(part, where).wait_recv()
                outs[part][...] += d_bufs[part][index].astype(F32)
        elif sign > 0:
            t_bufs[part][index] = value.astype(BF)

            @pl.when(here > 0)
            def _():
                u_copy(part, where).wait_recv()
                t_bufs[part][index] = (value + u_bufs[part][index].astype(F32)).astype(BF)

            u_copy(part, where).start()
        else:
            t_bufs[part][index] = value.astype(BF)

            @pl.when(here < spans[part] - 1)
            def _():
                d_copy(part, where).wait_recv()
                t_bufs[part][index] = (value + d_bufs[part][index].astype(F32)).astype(BF)

            d_copy(part, where).start()

    each(along)

    def finish(part, where, far, sign):
        c_copy(part, where, 0).wait_send()
        c_copy(part, where, 1).wait_send()
        b_copy(part, where).wait_send()
        if far > 0:
            (u_copy if sign > 0 else d_copy)(part, where).wait_send()

    each(finish)


def fold(arrays, out_shapes, pieces, collective_id):
    count = lax.axis_size("seq")
    total = len(pieces)
    sem = pltpu.SemaphoreType.DMA
    line = count // 4
    bufs = []
    for times in (2, 1, 1, 1, 1, 1):
        bufs += [VMEM((times * piece[0],) + piece[1], BF) for piece in pieces]
    return pl.pallas_call(
        functools.partial(fold_kernel, (len(arrays), len(out_shapes), pieces), count),
        out_shape=[jax.ShapeDtypeStruct(shape, F32) for shape in out_shapes],
        in_specs=[pl.BlockSpec(memory_space=VMEM)] * len(arrays),
        out_specs=[pl.BlockSpec(memory_space=VMEM)] * len(out_shapes),
        scratch_shapes=bufs + [sem((total, 2 * line))] * 2 + [sem((total, line))] * 6,
        compiler_params=pltpu.CompilerParams(
            collective_id=collective_id, has_side_effects=True, vmem_limit_bytes=60 * 2**20
        ),
    )(*arrays)


def exchange_kernel(x_ref, o_ref, own_sem, z_send, z_recv, x_send, x_recv, y_send, y_recv, c_send, c_recv):
    count = o_ref.shape[1]
    line = count // 4
    group = lax.axis_index("dp")
    me = lax.axis_index("seq")
    at, side, core = place(me)
    peers = line_peers(at, side, core, group, line)
    below, above, beside, sibling = (peer for _, peer in peers)
    across = (1 - group, me)
    meet(peers + [(at >= 0, across)])

    def remote(src, dst, send, recv, index, peer):
        return pltpu.make_async_remote_copy(
            src_ref=src, dst_ref=dst, send_sem=send.at[index], recv_sem=recv.at[index],
            device_id=peer, device_id_type=MESH,
        )

    items = [(0, 0)] + [(far, turn) for far in range(1, line) for turn in range(2)]

    def where_of(item):
        return at + item[0] * (2 * item[1] - 1)

    def number(item):
        return 2 * item[0] + item[1]

    def given(item, action):
        @pl.when((where_of(item) >= 0) & (where_of(item) < line))
        def _():
            action()

    def spot(item, other_group, other_side, other_core):
        g = 1 - group if other_group else group
        s = 1 - side if other_side else side
        c = 1 - core if other_core else core
        return o_ref.at[g, 4 * where_of(item) + 2 * s + c]

    def here(item, other_group, other_side):
        if item == (0, 0) and not other_group and not other_side:
            return x_ref
        return spot(item, other_group, other_side, False)

    def z_copy(item, turn, peer):
        far = (item[0] + 1, turn)
        return remote(here(item, 0, 0), spot(item, 0, 0, 0), z_send, z_recv, number(far), peer)

    def side_copy(item, other_group, arrived):
        dst = spot(item, other_group, arrived, 0)
        src = dst if arrived else here(item, other_group, 0)
        return remote(src, dst, x_send, x_recv, 2 * number(item) + other_group, beside)

    def cross_copy(item, other_side, arrived):
        dst = spot(item, arrived, other_side, 0)
        src = dst if arrived else here(item, 0, other_side)
        return remote(src, dst, y_send, y_recv, 2 * number(item) + other_side, across)

    def core_copy(item, other_group, other_side, arrived):
        dst = spot(item, other_group, other_side, arrived)
        src = dst if arrived else here(item, other_group, other_side)
        index = 4 * number(item) + 2 * other_group + other_side
        return remote(src, dst, c_send, c_recv, index, sibling)

    def by_side(item):
        return lax.rem(where_of(item), 2) == 0

    def z_links(item, act):
        far, turn = item
        if far + 1 < line:
            if far == 0 or turn == 0:

                @pl.when(at + 1 < line)
                def _():
                    act(z_copy(item, 0, above))

            if far == 0 or turn == 1:

                @pl.when(at > 0)
                def _():
                    act(z_copy(item, 1, below))

    def start(copy):
        copy.start()

    def launch(item):
        z_links(item, start)
        side_copy(item, 0, False).start()
        cross_copy(item, 0, False).start()
        core_copy(item, 0, 0, False).start()

    def first(item):
        z = remote(spot(item, 0, 0, 0), spot(item, 0, 0, 0), z_send, z_recv, number(item), beside)
        z.wait_recv()
        launch(item)

    def second(item):
        side_copy(item, 0, True).wait_recv()

        @pl.when(jnp.logical_not(by_side(item)))
        def _():
            cross_copy(item, 1, False).start()

        core_copy(item, 0, 1, False).start()
        cross_copy(item, 0, True).wait_recv()

        @pl.when(by_side(item))
        def _():
            side_copy(item, 1, False).start()

        core_copy(item, 1, 0, False).start()

    def third(item):
        @pl.when(by_side(item))
        def _():
            side_copy(item, 1, True).wait_recv()

        @pl.when(jnp.logical_not(by_side(item)))
        def _():
            cross_copy(item, 1, True).wait_recv()

        core_copy(item, 1, 1, False).start()

    def at_far(far):
        return [item for item in items if item[0] == far]

    own = pltpu.make_async_copy(x_ref, spot((0, 0), 0, 0, 0), own_sem.at[0])
    own.start()
    launch((0, 0))
    for step in range(1, line + 2):
        for item in at_far(step):
            given(item, functools.partial(first, item))
        for item in at_far(step - 1):
            given(item, functools.partial(second, item))
        if step >= 2:
            for item in at_far(step - 2):
                given(item, functools.partial(third, item))
    own.wait()

    def finish(item):
        z_links(item, lambda copy: copy.wait_send())
        side_copy(item, 0, False).wait_send()
        cross_copy(item, 0, False).wait_send()

        @pl.when(by_side(item))
        def _():
            side_copy(item, 1, False).wait_send()

        @pl.when(jnp.logical_not(by_side(item)))
        def _():
            cross_copy(item, 1, False).wait_send()

        for other_group in range(2):
            for other_side in range(2):
                core_copy(item, other_group, other_side, False).wait_send()
                core_copy(item, other_group, other_side, True).wait_recv()

    for item in items:
        given(item, functools.partial(finish, item))


def exchange(x, collective_id):
    count = lax.axis_size("seq")
    marks = 2 * (count // 4) + 2
    sem = pltpu.SemaphoreType.DMA
    return pl.pallas_call(
        exchange_kernel,
        out_shape=jax.ShapeDtypeStruct((2, count) + x.shape, x.dtype),
        in_specs=[pl.BlockSpec(memory_space=VMEM)],
        out_specs=pl.BlockSpec(memory_space=pl.ANY),
        scratch_shapes=[sem((1,))] + [sem((marks,))] * 2 + [sem((2 * marks,))] * 4 + [sem((4 * marks,))] * 2,
        compiler_params=pltpu.CompilerParams(collective_id=collective_id, has_side_effects=True),
    )(x)


def row_gather(line, rows, cuts):
    size = rows // cuts
    return tuple(
        (
            line,
            lambda x, h=h: x[0].at[pl.ds(h * size, size)],
            lambda o, q, h=h: o[0].at[q, pl.ds(h * size, size)],
        )
        for h in range(cuts)
    )


def row_pieces(line, rows, width, cuts):
    size = rows // cuts
    return tuple(
        (
            line,
            (size, width),
            lambda x, q, h=h: x[0].at[q, pl.ds(h * size, size)],
            lambda o, h=h: o[0].at[pl.ds(h * size, size)],
        )
        for h in range(cuts)
    )


def visible_rows(kind, run_devs, rows_dev, half, q):
    first = half + rows_dev * lax.rem(q, run_devs) if kind else rows_dev * q
    return pl.multiple_of(first, 32)


def visible_gather(line, run_devs, rows_dev, half):
    size = rows_dev // 2
    return tuple(
        (
            run_devs // 4 if kind else line,
            lambda x, m=m, kind=kind, j=j: x[0].at[m, kind, pl.ds(size * j, size)],
            lambda o, q, m=m, kind=kind, j=j: o[0].at[
                m, pl.ds(visible_rows(kind, run_devs, rows_dev, half, q) + size * j, size)
            ],
        )
        for kind in range(2)
        for m in range(MB)
        for j in range(2)
    )


def visible_sum(line, run_devs, rows_dev, half, width):
    return tuple(
        (
            run_devs // 4 if kind else line,
            (MB, rows_dev, width),
            lambda x, q, kind=kind: x[0].at[
                :, pl.ds(visible_rows(kind, run_devs, rows_dev, half, q), rows_dev)
            ],
            lambda o, kind=kind: o[0].at[:, kind],
        )
        for kind in range(2)
    )


def place_kernel(l_ref, r_ref, *refs):
    refs[-1][...] = jnp.dot(l_ref[...], r_ref[...], preferred_element_type=F32).astype(BF)


def place_product(buffer, left, right, first, rows):
    depth, width = right.shape
    block = width // 2
    given = () if buffer is None else (buffer,)
    return pl.pallas_call(
        place_kernel,
        grid=(left.shape[0] // block,),
        out_shape=jax.ShapeDtypeStruct((rows, width), BF),
        in_specs=[
            pl.BlockSpec((block, depth), lambda i: (i, 0)),
            pl.BlockSpec((depth, width), lambda i: (0, 0)),
        ]
        + [pl.BlockSpec(memory_space=pl.ANY)] * len(given),
        out_specs=pl.BlockSpec((block, width), lambda i: (first // block + i, 0)),
        input_output_aliases={2: 0} if given else {},
    )(left, right, *given)


def contract(left, right, left_dim, right_dim):
    return lax.dot_general(
        left, right, (((left_dim,), (right_dim,)), ((), ())), preferred_element_type=F32
    )


def norm_forward(values, gain, bias):
    centred = values - jnp.mean(values, axis=-1, keepdims=True)
    inverse = lax.rsqrt(jnp.mean(centred * centred, axis=-1, keepdims=True) + EPS_NORM)
    unit = centred * inverse
    return (unit * gain + bias, unit, inverse)


def norm_backward(upstream, unit, inverse, gain):
    scaled = upstream * gain
    inner = (
        scaled
        - jnp.mean(scaled, axis=-1, keepdims=True)
        - unit * jnp.mean(scaled * unit, axis=-1, keepdims=True)
    )
    return (inverse * inner, jnp.sum(upstream * unit, axis=0), jnp.sum(upstream, axis=0))


def head_probs(pos_ref, q, k):
    scores = contract(q, k, 0, 0) * HD ** (-0.5)
    key_pos = lax.broadcasted_iota(jnp.int32, scores.shape, 1)
    scores = jnp.where(key_pos <= pos_ref[...], scores, MASKED)
    shifted = jnp.exp(scores - jnp.max(scores, axis=1, keepdims=True))
    return shifted * (1.0 / jnp.sum(shifted, axis=1, keepdims=True))


def attend_kernel(pos_ref, q_ref, kv_ref, o_ref):
    probs = head_probs(pos_ref, q_ref[...], kv_ref[0]).astype(BF)
    o_ref[...] = contract(kv_ref[1], probs, 1, 1).astype(BF)


def attend_back_kernel(pos_ref, q_ref, kv_ref, g_ref, dq_ref, dkv_ref):
    q, k, v, g = q_ref[...], kv_ref[0], kv_ref[1], g_ref[...]
    probs = head_probs(pos_ref, q, k)
    grad = contract(g, v, 0, 0)
    back = (probs * (grad - jnp.sum(probs * grad, axis=1, keepdims=True))).astype(BF)
    scale = HD ** (-0.5)
    dq_ref[...] = (contract(k, back, 1, 1) * scale).astype(BF)
    dkv_ref[0] = (contract(q, back, 1, 0) * scale).astype(BF)
    dkv_ref[1] = contract(g, probs.astype(BF), 1, 0).astype(BF)


def attend(query_pos, q, kv):
    rows, keys = query_pos.shape[0], kv.shape[2] * query_pos.shape[0] // q.shape[1]
    small = pl.BlockSpec((HD, rows), lambda m, h: (h, m))
    large = pl.BlockSpec((2, HD, keys), lambda m, h: (0, h, m))
    return pl.pallas_call(
        attend_kernel,
        grid=(q.shape[1] // rows, HEADS),
        out_shape=jax.ShapeDtypeStruct(q.shape, BF),
        in_specs=[pl.BlockSpec((rows, 1), lambda m, h: (0, 0)), small, large],
        out_specs=small,
    )(query_pos, q, kv)


def attend_back(query_pos, q, kv, grad_out):
    rows, keys = query_pos.shape[0], kv.shape[2] * query_pos.shape[0] // q.shape[1]
    small = pl.BlockSpec((HD, rows), lambda m, h: (h, m))
    large = pl.BlockSpec((2, HD, keys), lambda m, h: (0, h, m))
    return pl.pallas_call(
        attend_back_kernel,
        grid=(q.shape[1] // rows, HEADS),
        out_shape=[jax.ShapeDtypeStruct(q.shape, BF), jax.ShapeDtypeStruct(kv.shape, BF)],
        in_specs=[pl.BlockSpec((rows, 1), lambda m, h: (0, 0)), small, large, small],
        out_specs=[small, large],
    )(query_pos, q, kv, grad_out)


def lookup_kernel(first_ref, slot_ref, table_ref, *refs):
    slots = slot_ref[...] - first_ref[0]
    ids = lax.broadcasted_iota(jnp.int32, (slots.shape[0], table_ref.shape[1]), 1)
    rows = contract(jnp.where(slots == ids, 1.0, 0.0).astype(BF), table_ref[...], 1, 1).astype(BF)
    refs[-1][...] = rows if len(refs) == 1 else refs[0][...] + rows


def lookup(first, slots, table, others, block):
    width, held = table.shape
    rows = pl.BlockSpec((block, width), lambda i: (i, 0))
    given = () if others is None else (others,)
    return pl.pallas_call(
        lookup_kernel,
        grid=(slots.shape[0] // block,),
        out_shape=jax.ShapeDtypeStruct((slots.shape[0], width), BF),
        in_specs=[
            pl.BlockSpec(memory_space=pltpu.SMEM),
            pl.BlockSpec((block, 1), lambda i: (i, 0)),
            pl.BlockSpec((width, held), lambda i: (0, 0)),
        ]
        + [rows] * len(given),
        out_specs=rows,
    )(first, slots, table, *given)


def adamw(weight, moment_a, moment_b, gradient, rate, decay):
    moment_a = MOMENT_ONE * moment_a + (1.0 - MOMENT_ONE) * gradient
    moment_b = MOMENT_TWO * moment_b + (1.0 - MOMENT_TWO) * gradient * gradient
    update = (
        moment_a
        / (1.0 - MOMENT_ONE**STEP)
        / (jnp.sqrt(moment_b / (1.0 - MOMENT_TWO**STEP)) + EPS_ADAM)
    )
    weight = weight - rate * (update + decay * weight)
    return (weight, moment_a, moment_b, weight.astype(BF))


def on_device(
    tokens,
    targets,
    counted,
    cont_label,
    pair_map,
    ref_logp,
    vocab_slot,
    embed_table,
    embed_first,
    embed_second,
    layer_weights,
    layer_first,
    layer_second,
    norm_params,
    norm_first,
    norm_second,
):
    seq_count = lax.axis_size("seq")
    group_count = lax.axis_size("dp")
    all_count = seq_count * group_count
    seq_rank = lax.axis_index("seq")
    group_rank = lax.axis_index("dp")
    device_rank = group_rank * seq_count + seq_rank
    rows_dev = tokens.shape[3]
    half = rows_dev * seq_count
    vocab_dev, width = embed_table.shape
    run_count = half // CLEN
    run_devs = CLEN // rows_dev
    own_rows = MB * 2 * rows_dev

    table_t = embed_table.T
    norm_dev = norm_params.shape[0]
    norm_parts = [norm_params]
    for step in range(1, group_count):
        norm_parts.append(
            lax.ppermute(
                norm_params, "dp", [(i, (i - step) % group_count) for i in range(group_count)]
            )
        )
    sent, *norm_parts = lax.optimization_barrier((table_t.astype(BF), *norm_parts))
    norm_all = jnp.zeros((group_count, norm_dev), F32)
    for step in range(group_count):
        norm_all = lax.dynamic_update_index_in_dim(
            norm_all, norm_parts[step], lax.rem(group_rank + step, group_count), 0
        )
    slab_t = [sent]
    for step in range(1, group_count):
        slab_t.append(
            lax.ppermute(
                slab_t[0], "dp", [(i, (i - step) % group_count) for i in range(group_count)]
            )
        )
    weights = lax.all_gather(
        layer_weights.T.astype(BF)[None], ("dp", "seq"), axis=0, tiled=True
    ).reshape(-1, width)
    w_q = weights[:width]
    w_o = weights[3 * width : 4 * width]
    w_kv = weights[width : 3 * width]
    w_up = weights[4 * width : 4 * width + FF]
    w_dn = weights[4 * width + FF :]

    marks = counted[:, 0]
    spots = jnp.arange(rows_dev, dtype=jnp.int32)
    ranks = (
        jnp.sum(jnp.where(spots[None, :, None] <= spots[None, None, :], marks[:, :, None], 0), axis=1)
        - 1
    )
    pick_ids = jnp.arange(PICK, dtype=jnp.int32)
    pick_hit = (ranks[:, None, :] == pick_ids[None, :, None]) & (marks[:, None, :] == 1)
    pick_targets = jnp.sum(jnp.where(pick_hit, targets[:, 0][:, None, :], 0), axis=2)
    pick_low = pick_hit.astype(BF)
    slots = vocab_slot[jnp.concatenate([tokens[:, 0].reshape(-1), pick_targets.reshape(-1)])]
    small = jnp.concatenate([slots.astype(F32), norm_all.reshape(-1)])
    small = jnp.pad(small, (0, -small.shape[0] % 1024)).reshape(-1, 128)
    small_all = direct_gather(small, False, 1).reshape(seq_count, -1)
    slots_all = small_all[:, : own_rows + MB * PICK].astype(jnp.int32)
    gains = (
        small_all[:, own_rows + MB * PICK :][:, : group_count * norm_dev]
        .reshape(seq_count, group_count, norm_dev)
        .transpose(1, 0, 2)
        .astype(BF)
        .astype(F32)
        .reshape(6, width)
    )
    row_slots = slots_all[:, :own_rows].reshape(-1)
    target_slots = slots_all[:, own_rows:].reshape(-1)
    vocab_ids = jnp.arange(vocab_dev, dtype=jnp.int32)

    def hits(slot_ids, step):
        part = lax.rem(group_rank + step, group_count)
        first = (part * seq_count + seq_rank) * vocab_dev
        return (slot_ids - first)[:, None] == vocab_ids[None, :]

    partial = None
    for step in range(group_count):
        part = lax.rem(group_rank + step, group_count)
        first = (part * seq_count + seq_rank) * vocab_dev
        partial = lookup(first[None], row_slots[:, None], slab_t[step], partial, own_rows)
    line = seq_count // 4
    (stream,) = fold(
        [partial.reshape(seq_count, own_rows, width)],
        [(own_rows, width)],
        row_pieces(line, own_rows, width, 2),
        2,
    )

    normed, unit_one, inverse_one = norm_forward(stream, gains[0], gains[3])
    hidden_one = normed.astype(BF)
    run_dev = seq_rank // run_devs * run_devs
    key_rows = half + CLEN
    (hidden_sel,) = spread(
        [hidden_one.reshape(MB, 2, rows_dev, width)],
        [jax.ShapeDtypeStruct((MB, key_rows, width), BF)],
        visible_gather(line, run_devs, rows_dev, half),
        3,
    )
    hidden_sel = hidden_sel.reshape(MB * key_rows, width)
    pairs = contract(w_kv, hidden_sel, 1, 1).astype(BF).reshape(2, width, MB * key_rows)
    queries = contract(w_q, hidden_one, 1, 1).astype(BF)
    start = seq_rank * rows_dev
    query_pos = jnp.concatenate([start + spots, half + (start - run_dev * rows_dev) + spots])[:, None]
    attended = attend(query_pos, queries, pairs)
    stream_one = stream + contract(attended, w_o, 0, 0)
    normed, unit_two, inverse_two = norm_forward(stream_one, gains[1], gains[4])
    hidden_two = normed.astype(BF)
    up_proj = contract(w_up, hidden_two, 1, 1)
    activated = jax.nn.gelu(up_proj, approximate=False).astype(BF)
    stream_two = stream_one + contract(activated, w_dn, 0, 0)
    normed, unit_final, inverse_final = norm_forward(stream_two, gains[2], gains[5])
    final = normed.astype(BF).reshape(MB, 2, rows_dev, width)[:, 1]
    picked = jnp.einsum("mpr,mrd->mpd", pick_low, final, preferred_element_type=F32).astype(BF)

    (head_rows,) = spread(
        [picked.reshape(MB * PICK, width)],
        [jax.ShapeDtypeStruct((seq_count, MB * PICK, width), BF)],
        row_gather(line, MB * PICK, 1),
        4,
    )
    head_rows = head_rows.reshape(seq_count * MB * PICK, width)
    logits = [contract(head_rows, slab_t[part], 1, 0) for part in range(group_count)]
    target_hits = [hits(target_slots, part) for part in range(group_count)]
    highest = jnp.max(logits[0], axis=1)
    for part in range(1, group_count):
        highest = jnp.maximum(highest, jnp.max(logits[part], axis=1))
    summed = jnp.zeros_like(highest)
    target_logit = jnp.zeros_like(highest)
    for part in range(group_count):
        summed = summed + jnp.sum(jnp.exp(logits[part] - highest[:, None]), axis=1)
        target_logit = target_logit + jnp.sum(jnp.where(target_hits[part], logits[part], 0.0), axis=1)
    stats = direct_gather(
        jnp.stack([highest, summed, target_logit]).reshape(-1, 128), False, 5
    ).reshape(seq_count, 3, -1)
    overall = jnp.max(stats[:, 0], axis=0)
    total = jnp.sum(stats[:, 1] * jnp.exp(stats[:, 0] - overall[None]), axis=0)
    log_total = overall + jnp.log(total)
    token_lp = jnp.sum(stats[:, 2], axis=0) - log_total

    run_ids = jnp.arange(run_count, dtype=jnp.int32)
    run_of_dev = jnp.arange(seq_count, dtype=jnp.int32) * rows_dev // CLEN
    run_match = run_of_dev[:, None] == run_ids[None, :]
    dev_lp = jnp.sum(token_lp.reshape(seq_count, MB, PICK), axis=2)
    run_lp = jnp.sum(jnp.where(run_match[:, None, :], dev_lp[:, :, None], 0.0), axis=0)
    labels = lax.dynamic_index_in_dim(cont_label, group_rank, 1, keepdims=False)
    pairing = lax.dynamic_index_in_dim(pair_map, group_rank, 1, keepdims=False)
    reference_lp = lax.dynamic_index_in_dim(ref_logp, group_rank, 1, keepdims=False)
    label_match = labels[:, :, None] == run_ids[None, None, :]
    label_lp = jnp.sum(jnp.where(label_match, run_lp[:, :, None], 0.0), axis=1)
    margin = label_lp - reference_lp
    chosen = pairing[:, 0::2, None] == run_ids[None, None, :]
    rejected = pairing[:, 1::2, None] == run_ids[None, None, :]
    delta = jnp.sum(jnp.where(chosen, margin[:, None, :], 0.0), axis=2) - jnp.sum(
        jnp.where(rejected, margin[:, None, :], 0.0), axis=2
    )
    loss = jnp.sum(jax.nn.softplus(-DPO_BETA * delta))
    pair_grad = -DPO_BETA * jax.nn.sigmoid(-DPO_BETA * delta)
    label_grad = jnp.sum(
        jnp.where(chosen, pair_grad[:, :, None], 0.0)
        - jnp.where(rejected, pair_grad[:, :, None], 0.0),
        axis=1,
    )
    run_grad = jnp.sum(jnp.where(label_match, label_grad[:, None, :], 0.0), axis=2)
    dev_grad = jnp.sum(jnp.where(run_match[:, None, :], run_grad[None], 0.0), axis=2)
    row_grad = jnp.broadcast_to(dev_grad[:, :, None], (seq_count, MB, PICK)).reshape(-1)

    head_back = 0.0
    logit_grads = []
    for part in range(group_count):
        logit_grad = (
            row_grad[:, None]
            * (target_hits[part].astype(F32) - jnp.exp(logits[part] - log_total[:, None]))
        ).astype(BF)
        logit_grads.append(logit_grad)
        head_back = head_back + contract(logit_grad, slab_t[part], 1, 1)
    head_back = head_back.astype(BF)
    moved = [(i, (i + 1) % group_count) for i in range(group_count)]
    if group_count == 2:
        head_back, head_part = lax.optimization_barrier(
            (head_back, contract(head_rows, logit_grads[1], 0, 0).astype(BF))
        )
        head_other = lax.ppermute(head_part, "dp", moved)
    (row_back,) = fold(
        [head_back.reshape(seq_count, MB * PICK, width)],
        [(MB * PICK, width)],
        row_pieces(line, MB * PICK, width, 1),
        6,
    )
    row_back = row_back.astype(BF).reshape(MB, PICK, width)
    cont_back = jnp.einsum("mpr,mpd->mrd", pick_low, row_back, preferred_element_type=F32)
    upstream = jnp.concatenate(
        [jnp.zeros((MB, 1, rows_dev, width), F32), cont_back[:, None]], axis=1
    ).reshape(own_rows, width)

    grad_two, gain_final, bias_final = norm_backward(upstream, unit_final, inverse_final, gains[2])
    grad_ffn = grad_two.astype(BF)
    columns = weights.shape[0]
    weight_grad = place_product(None, activated, grad_ffn, 4 * width + FF, columns)
    grad_act = contract(w_dn, grad_ffn, 1, 1)
    _, gelu_pull = jax.vjp(lambda pre_act: jax.nn.gelu(pre_act, approximate=False), up_proj)
    grad_up = gelu_pull(grad_act)[0].astype(BF)
    weight_grad = place_product(weight_grad, grad_up, hidden_two, 4 * width, columns)
    grad_hidden = contract(grad_up, w_up, 0, 0)
    grad_mid, gain_two, bias_two = norm_backward(grad_hidden, unit_two, inverse_two, gains[1])
    grad_one = grad_two + grad_mid
    grad_branch = grad_one.astype(BF)
    weight_grad = place_product(weight_grad, attended, grad_branch, 3 * width, columns)
    grad_attended = contract(w_o, grad_branch, 1, 1).astype(BF)
    grad_query, grad_pairs = attend_back(query_pos, queries, pairs, grad_attended)
    grad_pairs = grad_pairs.reshape(2 * width, MB * key_rows)
    weight_grad = place_product(weight_grad, grad_query, hidden_one, 0, columns)
    weight_grad = place_product(weight_grad, grad_pairs, hidden_sel, width, columns)
    low_sel = contract(grad_pairs, w_kv, 0, 0).astype(BF).reshape(MB, key_rows, width)
    weight_sum = lax.psum_scatter(
        weight_grad.reshape(all_count, -1, width), ("dp", "seq"), scatter_dimension=0, tiled=True
    )[0].astype(F32)
    (low_own,) = fold(
        [low_sel],
        [(MB, 2, rows_dev, width)],
        visible_sum(line, run_devs, rows_dev, half, width),
        7,
    )
    grad_low = low_own.reshape(own_rows, width) + contract(grad_query, w_q, 0, 0)
    grad_first, gain_one, bias_one = norm_backward(grad_low, unit_one, inverse_one, gains[0])
    norm_rows = jnp.stack([gain_one, gain_two, gain_final, bias_one, bias_two, bias_final])
    if group_count == 2:
        head_own = contract(head_rows, logit_grads[0], 0, 0)
        pad_rows = 8
        all_rows = exchange(
            jnp.concatenate(
                [grad_one + grad_first, norm_rows, jnp.zeros((pad_rows - 6, width), F32)]
            ).astype(BF),
            8,
        )
        other_slots = lax.ppermute(row_slots, "dp", moved)
        all_slots = jnp.where(
            group_rank == 0,
            jnp.stack([row_slots, other_slots]),
            jnp.stack([other_slots, row_slots]),
        ).reshape(all_count, own_rows)
        all_slots = jnp.pad(all_slots, ((0, 0), (0, pad_rows)), constant_values=-1).reshape(-1)
        embed_sum = (
            contract(all_rows.reshape(-1, width), hits(all_slots, 0).astype(BF), 0, 0)
            + head_own
            + head_other.astype(F32)
        )
        norm_all = jnp.sum(
            all_rows.reshape(all_count, own_rows + pad_rows, width)[
                :, own_rows : own_rows + 6
            ].astype(F32),
            axis=0,
        )
    else:
        row_grads, norm_grads = spread(
            [
                (grad_one + grad_first).astype(BF),
                jnp.concatenate([norm_rows, jnp.zeros((10, width), F32)]).astype(BF),
            ],
            [
                jax.ShapeDtypeStruct((seq_count, own_rows, width), BF),
                jax.ShapeDtypeStruct((seq_count, 16, width), BF),
            ],
            row_gather(line, own_rows, 2)
            + ((line, lambda x: x[1], lambda o, q: o[1].at[q]),),
            8,
        )
        row_grads = row_grads.reshape(-1, width)
        norm_sum = jnp.sum(norm_grads[:, :6].astype(F32), axis=0)
        norm_all = norm_sum
        for step in range(1, group_count):
            norm_all = norm_all + lax.ppermute(
                norm_sum, "dp", [(i, (i + step) % group_count) for i in range(group_count)]
            )

        def table_grad(step):
            return contract(head_rows, logit_grads[step], 0, 0) + contract(
                row_grads, hits(row_slots, step).astype(BF), 0, 0
            )

        arrived = [
            lax.ppermute(
                table_grad(step).astype(BF),
                "dp",
                [(i, (i + step) % group_count) for i in range(group_count)],
            )
            for step in range(1, group_count)
        ]
        embed_sum = table_grad(0)
        for block in arrived:
            embed_sum = embed_sum + block.astype(F32)
    norm_own = lax.dynamic_slice_in_dim(norm_all.reshape(-1), device_rank * norm_dev, norm_dev, 0)
    squares = (
        jnp.sum(embed_sum * embed_sum)
        + jnp.sum(weight_sum * weight_sum)
        + jnp.sum(norm_own * norm_own)
    )
    lanes = lax.broadcasted_iota(jnp.int32, (8, 128), 1)
    scalars = direct_gather(
        jnp.where(lanes == 0, squares, jnp.where(lanes == 1, loss, 0.0)), True, 9
    )
    square_total = jnp.sum(scalars[:, 0, 0])
    loss_total = jnp.sum(scalars[::seq_count, 0, 1])
    grad_norm = jnp.sqrt(square_total)
    factor = jnp.minimum(1.0, CLIP_NORM / grad_norm)
    embed_out = adamw(
        table_t, embed_first.T, embed_second.T, embed_sum * factor, LEARN_RATE, WEIGHT_DECAY
    )
    layer_out = adamw(
        layer_weights.T,
        layer_first.T,
        layer_second.T,
        weight_sum * factor,
        LEARN_RATE,
        WEIGHT_DECAY,
    )
    norm_out = adamw(norm_params, norm_first, norm_second, norm_own * factor, NORM_RATE, 0.0)
    return (
        embed_out[0].T,
        embed_out[1].T,
        embed_out[2].T,
        embed_out[3].T,
        layer_out[0].T,
        layer_out[1].T,
        layer_out[2].T,
        layer_out[3].T,
        norm_out[0],
        norm_out[1],
        norm_out[2],
        norm_out[3],
        grad_norm,
        loss_total,
    )


def solution(mesh):
    return jax.shard_map(
        on_device,
        mesh=mesh,
        in_specs=(
            P(None, "dp", None, "seq"),
            P(None, "dp", "seq"),
            P(None, "dp", "seq"),
            P(),
            P(),
            P(),
            P(),
            P(("dp", "seq"), None),
            P(("dp", "seq"), None),
            P(("dp", "seq"), None),
            P(None, ("dp", "seq")),
            P(None, ("dp", "seq")),
            P(None, ("dp", "seq")),
            P(("dp", "seq")),
            P(("dp", "seq")),
            P(("dp", "seq")),
        ),
        out_specs=(
            P(("dp", "seq"), None),
            P(("dp", "seq"), None),
            P(("dp", "seq"), None),
            P(("dp", "seq"), None),
            P(None, ("dp", "seq")),
            P(None, ("dp", "seq")),
            P(None, ("dp", "seq")),
            P(None, ("dp", "seq")),
            P(("dp", "seq")),
            P(("dp", "seq")),
            P(("dp", "seq")),
            P(("dp", "seq")),
            P(),
            P(),
        ),
        check_vma=False,
    )
```

time: 1760 us -> 1080 us (0.61)
  waiting for transfers between devices: 850 us -> 67.5 us
  Pallas kernels: 0 us -> 610 us
  local copies, waits for them, and re-layouts: 249 us -> 30.2 us
  matrix products: 392 us -> 268 us
  blocking collectives: 104 us -> 0 us
  other arithmetic: 127 us -> 65.6 us
    pallas_call x0 -> x18, Pallas kernels: none -> 610 us  [the longest x3 184 us: fold(): pl.pallas_call(functools.partial(fold_kernel, (len(arrays), len(out_shape...]
    reduce_scatter x4 -> x0, waiting for transfers between devices: 344 us -> none  [the longest x1 106 us: on_device(): lax.psum_scatter(partial.astype(BF).reshape(seq_count, own_rows, width),...]
    unnamed x11 -> x3, waiting for transfers between devices: 174 us -> 0.03 us
    all_gather x1, waiting for transfers between devices: 167 us -> 0.02 us  [on_device(): lax.all_gather(layer_weights.T.astype(BF)[None], ('dp', 'seq'), axis=0, t...]
    all_gather x4 -> x0, waiting for transfers between devices: 165 us -> none  [the longest x1 79.2 us: on_device(): lax.all_gather(hidden_one.reshape(1, MB, 2, rows_dev, width), 'seq', axis...]
    concatenate x4 -> x1, local copies, waits for them, and re-layouts: 86.5 us -> 2.77 us  [on_device(): jnp.concatenate([grad_one + grad_first, norm_rows, jnp.zeros((pad_rows -...]
    dot_general x6 -> x0, matrix products: 81.8 us -> none  [the longest x1 22.8 us: attend_backward(): jnp.einsum('mqhe,mkhe->mhqk', grad_out, values, preferred_element_type=F32)]
    ppermute x0 -> x4, waiting for transfers between devices: none -> 67.5 us  [the longest x1 65.1 us: on_device(): lax.ppermute(slab_t[0], 'dp', [(i, (i - step) % group_count) for i in ran...]
  transfers between devices with their start and end apart: 10 -> 6, of which waited for: 9 -> 2; matrix products, arithmetic and copies ran while one was open for 14% -> 17% of each run, Pallas kernels for 0% -> 39%
where the time goes in v2:
time: 1080 us; the launch traced here: 1070 us
  Pallas kernels  610 us (56%)
  matrix products  268 us (25%)
  waiting for transfers between devices  67.5 us (6%)
  other arithmetic  65.6 us (6%)
  local copies, waits for them, and re-layouts  30.2 us (3%)
  between operations  19.1 us (2%)
    dot_general x17, matrix products, contract(): lax.dot_general(left, right, (((left_dim,), (right_dim,)), ((), ())), pre...  267 us
    pallas_call x3, Pallas kernels, fold(): pl.pallas_call(functools.partial(fold_kernel, (len(arrays), len(out_shape...  184 us
    pallas_call x1, Pallas kernels, exchange(): pl.pallas_call(exchange_kernel, out_shape=jax.ShapeDtypeStruct((2, count)...  151 us
    pallas_call x2, Pallas kernels, spread(): pl.pallas_call(functools.partial(spread_kernel, (len(blocks), len(out_sha...  72.7 us
    ppermute x1, waiting for transfers between devices, on_device(): lax.ppermute(slab_t[0], 'dp', [(i, (i - step) % group_count) for i in ran...  65.1 us
    pallas_call x2, Pallas kernels, lookup(): pl.pallas_call(lookup_kernel, grid=(slots.shape[0] // block,), out_shape=...  51.4 us
    pallas_call x5, Pallas kernels, place_product(): pl.pallas_call(place_kernel, grid=(left.shape[0] // block,), out_shape=ja...  47.7 us
    pallas_call x1, Pallas kernels, attend_back(): pl.pallas_call(attend_back_kernel, grid=(q.shape[1] // rows, HEADS), out_...  39.6 us
  transfers between devices with their start and end apart: 6, of which 2 were waited for; matrix products, arithmetic and copies ran while one was open for 17% of the time, Pallas kernels for 39%

profile of v2, /device:TPU:0, one launch (start us, length us, event | category | flops | bytes accessed | tf_op | source)
XLA Modules:
  0.0 1066.4 jit_solution(14275382026012683528)
XLA Ops:
  23.0 9.7 shard_map.263
  36.6 25.6 %shard_map.264.refs_0_ = bf16[4096,1088]{1,0:T(8,128)(2,1)} custom-call(s32[1]{0:T(128)} %bitcast.8.first_ref, s32[4096,1]{1,0:T(8,128)} %bitcast.281, bf16[1088,1572]{1,0:T(8,128)(2,1)} %bitcast_convert_fusion.table_ref), custom_call_target="tpu_custom_call" | custom-call | tf_op jit(solution)/shard_map/pallas_call | solution.py:796
  62.3 65.1 %collective-permute-done.1.table_ref = bf16[1088,1572]{1,0:T(8,128)(2,1)} collective-permute-done((bf16[1088,1572]{1,0:T(8,128)(2,1)}, bf16[1088,1572]{1,0:T(8,128)(2,1)}, u32[]{:S(2)}, u32[]{:S(2)}) %collective-permute-start.1) | collective-permute-done | bytes 3420704 | tf_op jit(solution)/shard_map/ppermute | solution.py:871
  127.4 25.9 %shard_map.265 = bf16[4096,1088]{1,0:T(8,128)(2,1)} custom-call(s32[1]{0:T(128)} %bitcast.2.first_ref, s32[4096,1]{1,0:T(8,128)} %bitcast.282, bf16[1088,1572]{1,0:T(8,128)(2,1)} %collective-permute-done.1.table_ref, bf16[4096,1088]{1,0:T(8,128)(2,1)} %shard_map.264.refs_0_), custom_call_target="tpu_custom_call" | custom-call | tf_op jit(solution)/shard_map/pallas_call | solution.py:796
  153.3 86.2 %shard_map.266 = f32[256,1088]{1,0:T(8,128)} custom-call(bf16[16,256,1088]{2,1,0:T(8,128)(2,1)} %bitcast.275), custom_call_target="tpu_custom_call" | custom-call | tf_op jit(solution)/shard_map/pallas_call | solution.py:446
  244.8 48.3 %shard_map.267 = bf16[2,1536,1088]{2,1,0:T(8,128)(2,1)} custom-call(bf16[2,2,64,1088]{3,2,1,0:T(8,128)(2,1)} %bitcast.289), custom_call_target="tpu_custom_call" | custom-call | tf_op jit(solution)/shard_map/pallas_call | solution.py:283
  296.6 23.4 %convolution_convert_fusion = bf16[3072,2176]{0,1:T(8,128)(2,1)} fusion(bf16[3072,1088]{1,0:T(8,128)(2,1)} %bitcast.276, bf16[13056,1088]{1,0:T(8,128)(2,1)} %all-gather.3.cloned.1.call-done), kind=kOutput, calls=%fused_computation.4 | convolution fusion | flops 14552530944 | bytes 25460736 | tf_op jit(solution)/shard_map/dot_general | solution.py:713
  320.1 34.5 %shard_map.268.l_ref = bf16[1088,256]{1,0:T(8,128)(2,1)} custom-call(s32[128,1]{1,0:T(8,128)} %copy.150.pos_ref, bf16[1088,256]{1,0:T(8,128)(2,1)} %fusion.46.q_ref, bf16[2,1088,3072]{2,1,0:T(8,128)(2,1)} %bitcast.273), custom_call_target="tpu_custom_call" | custom-call | tf_op jit(solution)/shard_map/pallas_call | solution.py:763
  358.2 16.2 %fusion.19 = (bf16[4352,256]{1,0:T(8,128)(2,1)S(1)}, f32[4352,256]{1,0:T(8,128)}, f32[256,4352]{0,1:T(8,128)}) fusion(bf16[256,1088]{1,0:T(8,128)(2,1)S(1)} %add_convert_fusion.2.r_ref, bf16[13056,1088]{1,0:T(8,128)(2,1)} %all-gather.3.cloned.1.call-done), kind=kOutput, calls=%fused_computation.45 | convolution fusion | flops 2496724992 | bytes 21725184 | tf_op jit(solution)/shard_map/dot_general | solution.py:713
  374.4 7.9 fusion.93
  383.7 24.4 %shard_map.269 = bf16[16,64,1088]{2,1,0:T(8,128)(2,1)} custom-call(bf16[64,1088]{1,0:T(8,128)(2,1)} %bitcast.298), custom_call_target="tpu_custom_call" | custom-call | tf_op jit(solution)/shard_map/pallas_call | solution.py:283
  408.2 7.3 fusion.94
  415.5 8.8 fusion.95
  428.8 8.4 shard_map.270
  440.3 10.2 convolution_convert_fusion.2
  450.4 8.1 fusion.82
  458.6 7.8 fusion.42
  470.7 24.9 %shard_map.271 = f32[64,1088]{1,0:T(8,128)} custom-call(bf16[16,64,1088]{2,1,0:T(8,128)(2,1)} %bitcast.285), custom_call_target="tpu_custom_call" | custom-call | tf_op jit(solution)/shard_map/pallas_call | solution.py:446
  499.4 9.0 shard_map.275.refs_0_
  508.3 10.6 fusion.25.l_ref
  518.9 9.6 fusion.96
  537.1 39.6 %shard_map.272 = (bf16[1088,256]{1,0:T(8,128)(2,1)}, bf16[2,1088,3072]{2,1,0:T(8,128)(2,1)}) custom-call(s32[128,1]{1,0:T(8,128)} %copy.150.pos_ref, bf16[1088,256]{1,0:T(8,128)(2,1)} %fusion.46.q_ref, bf16[2,1088,3072]{2,1,0:T(8,128)(2,1)} %bitcast.274, bf16[1088,256]{1,0:T(8,128)(2,1)} %fusion.47.g_ref), custom_call_target="tpu_custom_call" | custom-call | tf_op jit(solution)/shard_map/pallas_call | solution.py:776
  576.7 9.0 shard_map.276.refs_0_
  592.4 23.0 %shard_map.279 = bf16[13056,1088]{1,0:T(8,128)(2,1)} custom-call(bf16[2176,3072]{1,0:T(8,128)(2,1)} %bitcast.283, bf16[3072,1088]{1,0:T(8,128)(2,1)} %bitcast.277, bf16[13056,1088]{1,0:T(8,128)(2,1)} %shard_map.278.refs_0_), custom_call_target="tpu_custom_call", output_to_operand_aliasing={{}: (2, {})} | custom-call | tf_op jit(solution)/shard_map/pallas_call | solution.py:698
  621.7 22.7 %convolution_convert_fusion.1 = bf16[3072,1088]{0,1:T(8,128)(2,1)} fusion(bf16[2176,3072]{1,0:T(8,128)(2,1)} %bitcast.284, bf16[13056,1088]{1,0:T(8,128)(2,1)} %all-gather.3.cloned.1.call-done), kind=kOutput, calls=%fused_computation.5 | convolution fusion | flops 14549188608 | bytes 25067520 | tf_op jit(solution)/shard_map/dot_general | solution.py:713
  644.4 10.7 %copy.166 = bf16[3072,1088]{1,0:T(8,128)(2,1)} copy(bf16[3072,1088]{0,1:T(8,128)(2,1)} %convolution_convert_fusion.1) | data formatting | bytes 13369344 | tf_op jit(solution)/shard_map/convert_element_type | solution.py:1053
  655.2 73.4 %shard_map.273 = f32[2,2,64,1088]{3,2,1,0:T(8,128)} custom-call(bf16[2,1536,1088]{2,1,0:T(8,128)(2,1)} %bitcast.278), custom_call_target="tpu_custom_call" | custom-call | tf_op jit(solution)/shard_map/pallas_call | solution.py:446
  735.9 151.4 %shard_map.274 = bf16[2,16,264,1088]{3,2,1,0:T(8,128)(2,1)} custom-call(bf16[264,1088]{1,0:T(8,128)(2,1)} %concatenate.45.x_ref), custom_call_target="tpu_custom_call" | custom-call | tf_op jit(solution)/shard_map/pallas_call | solution.py:620
  890.0 10.7 %fusion.81 = f32[1088,1572]{1,0:T(8,128)} fusion(bf16[1024,1088]{1,0:T(8,128)(2,1)S(1)} %bitcast.294, f32[1024,1572]{0,1:T(8,128)} %copy-done.5, f32[1024]{0:T(1024)S(1)} %copy-done.29, f32[1024]{0:T(1024)S(1)} %copy-done.31, s32[1024]{0:T(1024)S(1)} %copy-done.27), kind=kOutput, calls=%fused_computation.221 | convolution fusion | flops 3512426496 | bytes 15520768 | tf_op jit(solution)/shard_map/dot_general | solution.py:713
  900.7 109.6 %multiply_reduce_fusion = (f32[]{:T(128)}, f32[1088,1572]{1,0:T(8,128)}) fusion(bf16[1088,1572]{1,0:T(8,128)(2,1)} %collective-permute-done.3, f32[1088,1572]{1,0:T(8,128)} %fusion.81, bf16[8448,1088]{1,0:T(8,128)(2,1)} %bitcast.280, s32[8448]{0:T(1024)S(1)} %sub.240), kind=kOutput, calls=%fused_computation.24 | convolution fusion | flops 28919666688 | bytes 35520004 | tf_op jit(solution)/shard_map/dot_general | solution.py:713
  1015.1 10.0 shard_map.280
  1036.2 21.9 %convert_bitcast_fusion = (bf16[1572,1088]{0,1:T(8,128)(2,1)}, f32[1088,1572]{1,0:T(8,128)}, f32[1572,1088]{0,1:T(8,128)}, f32[1572,1088]{0,1:T(8,128)}) fusion(f32[1572,1088]{0,1:T(8,128)} %param.25, f32[]{:T(128)S(6)} %min.3, f32[1088,1572]{1,0:T(8,128)} %get-tuple-element.100, bf16[1088,1572]{1,0:T(8,128)(2,1)} %collective-permute-done.3, ...), kind=kLoop, calls=%fused_computation.68 | loop fusion | flops 32496384 | bytes 54730756 | tf_op jit(solution)/shard_map/transpose | solution.py:1161
  (231 shorter events, 93.5 us)
Async XLA Ops:
  7.2 286.0 %all-gather.3.cloned.1.call-start = ((), (), s32[]{:S(2)}) async-start(), calls=%async_computation.1 | async-start | bytes 31021056 | tf_op jit(solution)/shard_map/all_gather | solution.py:875
  9.9 12.2 %copy-start.32 = (f32[204]{0:T(256)S(1)}, f32[204]{0:T(256)}, u32[]{:S(2)}) copy-start(f32[204]{0:T(256)} %param.29) | copy-start | bytes 2452
  9.9 1000.4 %reduce-scatter.4.cloned.1.call-start = ((), (), s32[]{:S(2)}) async-start(), calls=%async_computation.2 | async-start | bytes 31021056
  10.0 8.3 collective-permute-start
  18.3 109.1 %collective-permute-start.1 = (bf16[1088,1572]{1,0:T(8,128)(2,1)}, bf16[1088,1572]{1,0:T(8,128)(2,1)}, u32[]{:S(2)}, u32[]{:S(2)}) collective-permute-start(bf16[1088,1572]{1,0:T(8,128)(2,1)} %bitcast_convert_fusion.table_ref), channel_id=1, source_target_pairs={{0,16},{16,0},{1,17},{17,1},{2,18},{18,2},{3,19},{19,3},{4,20},{20... | collective-permute-start | bytes 10262024 | tf_op jit(solution)/shard_map/ppermute | solution.py:871
  33.9 424.6 %copy-start.26 = (s32[1024]{0:T(1024)}, s32[1024]{0:T(1024)S(1)}, u32[]{:S(2)}) copy-start(s32[1024]{0:T(1024)S(1)} %sub.213) | copy-start | bytes 12292
  62.3 180.2 %copy-start.17 = (f32[1088]{0:T(1024)}, f32[1088]{0:T(1024)S(1)}, u32[]{:S(2)}) copy-start(f32[1088]{0:T(1024)S(1)} %get-tuple-element.50) | copy-start | bytes 13060
  240.9 52.2 %copy-start.21 = (f32[256]{0:T(256)}, f32[256]{0:T(256)S(1)}, u32[]{:S(2)}) copy-start(f32[256]{0:T(256)S(1)} %broadcast_multiply_fusion.8) | copy-start | bytes 3076
  242.5 50.7 %copy-start.24 = (f32[256]{0:T(256)}, f32[256]{0:T(256)S(1)}, u32[]{:S(2)}) copy-start(f32[256]{0:T(256)S(1)} %add_rsqrt_fusion.2) | copy-start | bytes 3076
  244.8 48.3 %copy-start.7 = (bf16[256,1088]{1,0:T(8,128)(2,1)S(1)}, bf16[256,1088]{1,0:T(8,128)(2,1)}, u32[]{:S(2)}) copy-start(bf16[256,1088]{1,0:T(8,128)(2,1)} %add_convert_fusion.3.r_ref) | copy-start | bytes 1671172
  320.1 34.5 %copy-start.2 = (f32[256,1088]{1,0:T(8,128)S(1)}, f32[256,1088]{1,0:T(8,128)}, u32[]{:S(2)}) copy-start(f32[256,1088]{1,0:T(8,128)} %shard_map.266) | copy-start | bytes 3342340
  358.2 16.2 %copy-start.9 = (bf16[256,1088]{1,0:T(8,128)(2,1)}, bf16[256,1088]{1,0:T(8,128)(2,1)S(1)}, u32[]{:S(2)}) copy-start(bf16[256,1088]{1,0:T(8,128)(2,1)S(1)} %add_convert_fusion.2.r_ref) | copy-start | bytes 1671172
  438.4 20.1 %copy-start.28 = (f32[1024]{0:T(1024)}, f32[1024]{0:T(1024)S(1)}, u32[]{:S(2)}) copy-start(f32[1024]{0:T(1024)S(1)} %get-tuple-element.70) | copy-start | bytes 12292
  440.3 18.3 %copy-start.30 = (f32[1024]{0:T(1024)}, f32[1024]{0:T(1024)S(1)}, u32[]{:S(2)}) copy-start(f32[1024]{0:T(1024)S(1)} %mul.450) | copy-start | bytes 12292
  440.3 18.3 %slice-start = ((s8[6455296]{0:T(1024)(128)(4,1)}), s8[4194304]{0:T(1024)(128)(4,1)S(1)}, s32[]{:S(2)}) async-start(s8[6455296]{0:T(1024)(128)(4,1)} %bitcast.287), calls=%async_computation.3 | async-start | bytes 8388608
  533.5 43.2 %copy-start.13 = (bf16[256,1088]{1,0:T(8,128)(2,1)}, bf16[256,1088]{1,0:T(8,128)(2,1)S(1)}, u32[]{:S(2)}) copy-start(bf16[256,1088]{1,0:T(8,128)(2,1)S(1)} %get-tuple-element.65.r_ref) | copy-start | bytes 1671172
  616.2 3.8 collective-permute-start.2
  620.2 280.5 %collective-permute-start.3 = (bf16[1088,1572]{1,0:T(8,128)(2,1)}, bf16[1088,1572]{1,0:T(8,128)(2,1)}, u32[]{:S(2)}, u32[]{:S(2)}) collective-permute-start(bf16[1088,1572]{1,0:T(8,128)(2,1)} %convolution_convert_fusion.2), channel_id=1, source_target_pairs={{0,16},{16,0},{1,17},{17,1},{2,18},{18,2},{3,19},{19,3},{4,20},{20... | collective-permute-start | bytes 10262024 | tf_op jit(solution)/shard_map/ppermute | solution.py:1022
  655.2 73.4 %copy-start.3 = (f32[256,1088]{1,0:T(8,128)S(1)}, f32[256,1088]{1,0:T(8,128)}, u32[]{:S(2)}) copy-start(f32[256,1088]{1,0:T(8,128)} %shard_map.266) | copy-start | bytes 3342340
  655.2 73.4 %copy-start.16 = (bf16[1088,256]{1,0:T(8,128)(2,1)S(1)}, bf16[1088,256]{1,0:T(8,128)(2,1)}, u32[]{:S(2)}) copy-start(bf16[1088,256]{1,0:T(8,128)(2,1)} %get-tuple-element.26.l_ref) | copy-start | bytes 1671172
  655.2 73.4 %copy-start.18 = (f32[1088]{0:T(1024)S(1)}, f32[1088]{0:T(1024)}, u32[]{:S(2)}) copy-start(f32[1088]{0:T(1024)} %copy-done.17) | copy-start | bytes 13060
  655.2 73.5 %copy-start.22 = (f32[256]{0:T(256)S(1)}, f32[256]{0:T(256)}, u32[]{:S(2)}) copy-start(f32[256]{0:T(256)} %copy-done.21) | copy-start | bytes 3076
  655.2 73.5 %copy-start.25 = (f32[256]{0:T(256)S(1)}, f32[256]{0:T(256)}, u32[]{:S(2)}) copy-start(f32[256]{0:T(256)} %copy-done.24) | copy-start | bytes 3076
  735.9 154.1 %copy-start.11 = (bf16[16,64,1088]{2,1,0:T(8,128)(2,1)S(1)}, bf16[16,64,1088]{2,1,0:T(8,128)(2,1)}, u32[]{:S(2)}) copy-start(bf16[16,64,1088]{2,1,0:T(8,128)(2,1)} %shard_map.269) | copy-start | bytes 6684676
  735.9 154.1 %copy-start.27 = (s32[1024]{0:T(1024)S(1)}, s32[1024]{0:T(1024)}, u32[]{:S(2)}) copy-start(s32[1024]{0:T(1024)} %copy-done.26) | copy-start | bytes 12292
  735.9 154.1 %copy-start.29 = (f32[1024]{0:T(1024)S(1)}, f32[1024]{0:T(1024)}, u32[]{:S(2)}) copy-start(f32[1024]{0:T(1024)} %copy-done.28) | copy-start | bytes 12292
  735.9 154.1 %copy-start.31 = (f32[1024]{0:T(1024)S(1)}, f32[1024]{0:T(1024)}, u32[]{:S(2)}) copy-start(f32[1024]{0:T(1024)} %copy-done.30) | copy-start | bytes 12292
  900.7 128.1 %copy-start.33 = (f32[204]{0:T(256)S(1)}, f32[204]{0:T(256)}, u32[]{:S(2)}) copy-start(f32[204]{0:T(256)} %param.29) | copy-start | bytes 2452
  900.7 128.1 %copy-start.37 = (f32[204]{0:T(256)S(1)}, f32[204]{0:T(256)}, u32[]{:S(2)}) copy-start(f32[204]{0:T(256)} %param.30) | copy-start | bytes 2452
  900.7 128.1 %copy-start.38 = (f32[204]{0:T(256)S(1)}, f32[204]{0:T(256)}, u32[]{:S(2)}) copy-start(f32[204]{0:T(256)} %param.31) | copy-start | bytes 2452
  900.7 128.8 %copy-start.4 = (f32[1088,408]{0,1:T(8,128)S(1)}, f32[1088,408]{0,1:T(8,128)}, u32[]{:S(2)}) copy-start(f32[1088,408]{0,1:T(8,128)} %param.26) | copy-start | bytes 5326852
  1036.2 21.9 %copy-start.1 = (s32[50304]{0:T(1024)S(1)}, s32[50304]{0:T(1024)}, u32[]{:S(2)}) copy-start(s32[50304]{0:T(1024)} %param.22) | copy-start | bytes 603652
  (18 other events, 139.2 us)
Sparse Core Ops, SparseCore 0:
  11.4 215.6 all-gather.2
  615.6 331.7 reduce-scatter.3

commit v3 on v2

--- a/solution.py
+++ b/solution.py
@@ -6,6 +6,7 @@
 from jax.experimental import pallas as pl
 from jax.experimental.pallas import tpu as pltpu
 from jax.sharding import PartitionSpec as P
+
 
 HEADS = 17
 HD = 64
@@ -199,12 +200,12 @@
 
     items = 2 * line - 1
 
-    def goes_up(part, item):
-        low, high = low_high(spans[part])
+    def goes_up(part):
+        _, high = low_high(spans[part])
         return at + 1 < high
 
-    def goes_down(part, item):
-        low, high = low_high(spans[part])
+    def goes_down(part):
+        low, _ = low_high(spans[part])
         return at - 1 >= low
 
     def active(part, item):
@@ -220,12 +221,12 @@
         def _():
             if item == 0 or item % 2 == 1:
                 if (item + 1) // 2 + 1 < spans[part]:
-                    @pl.when(goes_up(part, item))
+                    @pl.when(goes_up(part))
                     def _():
                         z_copy(part, item, True).start()
             if item == 0 or item % 2 == 0:
                 if (item + 1) // 2 + 1 < spans[part]:
-                    @pl.when(goes_down(part, item))
+                    @pl.when(goes_down(part))
                     def _():
                         z_copy(part, item, False).start()
             b_copy(part, item).start()
@@ -246,6 +247,7 @@
                     @pl.when(valid(part, item))
                     def _():
                         z_arrived(part, item).wait_recv()
+
                     launch(part, item)
         last = [0] if far == 1 else [2 * far - 3, 2 * far - 2]
         for item in last:
@@ -261,11 +263,11 @@
             @pl.when(valid(part, item))
             def _():
                 if (item == 0 or item % 2 == 1) and (item + 1) // 2 + 1 < spans[part]:
-                    @pl.when(goes_up(part, item))
+                    @pl.when(goes_up(part))
                     def _():
                         z_copy(part, item, True).wait_send()
                 if (item == 0 or item % 2 == 0) and (item + 1) // 2 + 1 < spans[part]:
-                    @pl.when(goes_down(part, item))
+                    @pl.when(goes_down(part))
                     def _():
                         z_copy(part, item, False).wait_send()
                 b_copy(part, item).wait_send()
@@ -805,6 +807,24 @@
         + [rows] * len(given),
         out_specs=rows,
     )(first, slots, table, *given)
+
+
+def own_columns(early, late, rank, count):
+    size = early.shape[0]
+    pieces = []
+    for turn in range(3):
+        units = [(3 * owner + turn, owner) for owner in range(count)]
+        from_early = lax.ppermute(
+            early, ("dp", "seq"), [(unit, owner) for unit, owner in units if unit < count]
+        )
+        first = lax.rem(2 * rank + 3 * count + count - turn, 3) == 0
+        from_late = lax.ppermute(
+            jnp.where(first, late[:size], late[size:]),
+            ("dp", "seq"),
+            [((unit - count) // 2, owner) for unit, owner in units if unit >= count],
+        )
+        pieces.append(jnp.where(3 * rank + turn < count, from_early, from_late))
+    return jnp.concatenate(pieces)
 
 
 def adamw(weight, moment_a, moment_b, gradient, rate, decay):
@@ -1034,26 +1054,33 @@
 
     grad_two, gain_final, bias_final = norm_backward(upstream, unit_final, inverse_final, gains[2])
     grad_ffn = grad_two.astype(BF)
-    columns = weights.shape[0]
-    weight_grad = place_product(None, activated, grad_ffn, 4 * width + FF, columns)
+    weight_late = place_product(None, activated, grad_ffn, FF, 2 * FF)
     grad_act = contract(w_dn, grad_ffn, 1, 1)
     _, gelu_pull = jax.vjp(lambda pre_act: jax.nn.gelu(pre_act, approximate=False), up_proj)
     grad_up = gelu_pull(grad_act)[0].astype(BF)
-    weight_grad = place_product(weight_grad, grad_up, hidden_two, 4 * width, columns)
+    weight_late = place_product(weight_late, grad_up, hidden_two, 0, 2 * FF)
     grad_hidden = contract(grad_up, w_up, 0, 0)
     grad_mid, gain_two, bias_two = norm_backward(grad_hidden, unit_two, inverse_two, gains[1])
     grad_one = grad_two + grad_mid
     grad_branch = grad_one.astype(BF)
-    weight_grad = place_product(weight_grad, attended, grad_branch, 3 * width, columns)
     grad_attended = contract(w_o, grad_branch, 1, 1).astype(BF)
+    weight_late, grad_attended = lax.optimization_barrier((weight_late, grad_attended))
+    late_sum = lax.psum_scatter(
+        weight_late.reshape(all_count, -1, width), ("dp", "seq"), scatter_dimension=0, tiled=True
+    )[0]
     grad_query, grad_pairs = attend_back(query_pos, queries, pairs, grad_attended)
+    if group_count == 2:
+        grad_query, head_other = lax.optimization_barrier((grad_query, head_other))
     grad_pairs = grad_pairs.reshape(2 * width, MB * key_rows)
-    weight_grad = place_product(weight_grad, grad_query, hidden_one, 0, columns)
-    weight_grad = place_product(weight_grad, grad_pairs, hidden_sel, width, columns)
+    weight_early = place_product(None, attended, grad_branch, 3 * width, 4 * width)
+    weight_early = place_product(weight_early, grad_query, hidden_one, 0, 4 * width)
+    weight_early = place_product(weight_early, grad_pairs, hidden_sel, width, 4 * width)
     low_sel = contract(grad_pairs, w_kv, 0, 0).astype(BF).reshape(MB, key_rows, width)
-    weight_sum = lax.psum_scatter(
-        weight_grad.reshape(all_count, -1, width), ("dp", "seq"), scatter_dimension=0, tiled=True
-    )[0].astype(F32)
+    low_sel, late_sum, weight_early = lax.optimization_barrier((low_sel, late_sum, weight_early))
+    early_sum = lax.psum_scatter(
+        weight_early.reshape(all_count, -1, width), ("dp", "seq"), scatter_dimension=0, tiled=True
+    )[0]
+    weight_sum = own_columns(early_sum, late_sum, device_rank, all_count).astype(F32)
     (low_own,) = fold(
         [low_sel],
         [(MB, 2, rows_dev, width)],
@@ -1073,17 +1100,15 @@
             8,
         )
         other_slots = lax.ppermute(row_slots, "dp", moved)
-        all_slots = jnp.where(
-            group_rank == 0,
-            jnp.stack([row_slots, other_slots]),
-            jnp.stack([other_slots, row_slots]),
-        ).reshape(all_count, own_rows)
-        all_slots = jnp.pad(all_slots, ((0, 0), (0, pad_rows)), constant_values=-1).reshape(-1)
-        embed_sum = (
-            contract(all_rows.reshape(-1, width), hits(all_slots, 0).astype(BF), 0, 0)
-            + head_own
-            + head_other.astype(F32)
-        )
+        embed_sum = lax.optimization_barrier(head_own + head_other.astype(F32))
+        for part in range(group_count):
+            part_slots = jnp.where(group_rank == part, row_slots, other_slots)
+            part_slots = jnp.pad(
+                part_slots.reshape(seq_count, own_rows), ((0, 0), (0, pad_rows)), constant_values=-1
+            ).reshape(-1)
+            embed_sum = embed_sum + contract(
+                all_rows[part].reshape(-1, width), hits(part_slots, 0).astype(BF), 0, 0
+            )
         norm_all = jnp.sum(
             all_rows.reshape(all_count, own_rows + pad_rows, width)[
                 :, own_rows : own_rows + 6
@@ -1131,7 +1156,8 @@
     norm_own = lax.dynamic_slice_in_dim(norm_all.reshape(-1), device_rank * norm_dev, norm_dev, 0)
     squares = (
         jnp.sum(embed_sum * embed_sum)
-        + jnp.sum(weight_sum * weight_sum)
+        + jnp.sum(jnp.square(early_sum.astype(F32)))
+        + jnp.sum(jnp.square(late_sum.astype(F32)))
         + jnp.sum(norm_own * norm_own)
     )
     lanes = lax.broadcasted_iota(jnp.int32, (8, 128), 1)

time: 1080 us -> 1130 us (1.046); the launches traced: 1070 us -> 1100 us
  waiting for transfers between devices: 67.5 us -> 183 us
  matrix products: 268 us -> 207 us
  Pallas kernels: 610 us -> 555 us
  starting transfers between devices: 6.12 us -> 20.9 us
  local copies, waits for them, and re-layouts: 30.2 us -> 42.3 us
    ppermute x1, waiting for transfers between devices: 0.01 us -> 68.7 us  [on_device(): head_other = lax.ppermute(head_part, 'dp', moved)]
    dot_general x17 -> x18, matrix products: 267 us -> 206 us  [contract(): lax.dot_general(left, right, (((left_dim,), (right_dim,)), ((), ())), pre...]
    reduce_scatter x0 -> x1, waiting for transfers between devices: none -> 47.4 us  [on_device(): lax.psum_scatter(weight_late.reshape(all_count, -1, width), ('dp', 'seq')...]
    pallas_call x1, Pallas kernels: 151 us -> 116 us  [exchange(): pl.pallas_call(exchange_kernel, out_shape=jax.ShapeDtypeStruct((2, count)...]
    pallas_call x3, Pallas kernels: 184 us -> 158 us  [fold(): pl.pallas_call(functools.partial(fold_kernel, (len(arrays), len(out_shape...]
    ppermute x0 -> x6, starting transfers between devices: none -> 14.6 us  [the longest x3 11.3 us: own_columns(): lax.ppermute(jnp.where(first, late[:size], late[size:]), ('dp', 'seq'), [...]
    slice x1 -> x2, local copies, waits for them, and re-layouts: 0.18 us -> 12.2 us  [the longest x1 12 us: on_device(): all_rows[part].reshape(-1, width)]
  transfers between devices with their start and end apart: 6 -> 13, of which waited for: 2 -> 4; matrix products, arithmetic and copies ran while one was open for 17% -> 15% of each run, Pallas kernels for 39% -> 40%
where the time goes in v3:
time: 1130 us; the launch traced here: 1100 us
  Pallas kernels  555 us (49%)
  matrix products  207 us (18%)
  waiting for transfers between devices  183 us (16%)
  other arithmetic  76.6 us (7%)
  local copies, waits for them, and re-layouts  42.3 us (4%)
  starting transfers between devices  20.9 us (2%)
  between operations  19.7 us (2%)
    dot_general x18, matrix products, contract(): lax.dot_general(left, right, (((left_dim,), (right_dim,)), ((), ())), pre...  206 us
    pallas_call x3, Pallas kernels, fold(): pl.pallas_call(functools.partial(fold_kernel, (len(arrays), len(out_shape...  158 us
    pallas_call x1, Pallas kernels, exchange(): pl.pallas_call(exchange_kernel, out_shape=jax.ShapeDtypeStruct((2, count)...  116 us
    pallas_call x2, Pallas kernels, spread(): pl.pallas_call(functools.partial(spread_kernel, (len(blocks), len(out_sha...  72.7 us
    ppermute x1, waiting for transfers between devices, on_device(): head_other = lax.ppermute(head_part, 'dp', moved)  68.7 us
    ppermute x1, waiting for transfers between devices, on_device(): lax.ppermute(slab_t[0], 'dp', [(i, (i - step) % group_count) for i in ran...  65.2 us
    pallas_call x2, Pallas kernels, lookup(): pl.pallas_call(lookup_kernel, grid=(slots.shape[0] // block,), out_shape=...  51.4 us
    pallas_call x5, Pallas kernels, place_product(): pl.pallas_call(place_kernel, grid=(left.shape[0] // block,), out_shape=ja...  48.2 us
  transfers between devices with their start and end apart: 13, of which 4 were waited for; matrix products, arithmetic and copies ran while one was open for 15% of the time, Pallas kernels for 40%

profile of v3, /device:TPU:0, one launch (start us, length us, event | category | flops | bytes accessed | tf_op | source)
XLA Modules:
  0.0 1104.3 jit_solution(17585833081092901383)
XLA Ops:
  23.0 9.6 shard_map.263
  36.6 25.6 %shard_map.264.refs_0_ = bf16[4096,1088]{1,0:T(8,128)(2,1)} custom-call(s32[1]{0:T(128)} %bitcast.8.first_ref, s32[4096,1]{1,0:T(8,128)} %bitcast.264, bf16[1088,1572]{1,0:T(8,128)(2,1)} %bitcast_convert_fusion.table_ref), custom_call_target="tpu_custom_call" | custom-call | tf_op jit(solution)/shard_map/pallas_call | solution.py:798
  62.2 65.2 %collective-permute-done.1.table_ref = bf16[1088,1572]{1,0:T(8,128)(2,1)} collective-permute-done((bf16[1088,1572]{1,0:T(8,128)(2,1)}, bf16[1088,1572]{1,0:T(8,128)(2,1)}, u32[]{:S(2)}, u32[]{:S(2)}) %collective-permute-start.1) | collective-permute-done | bytes 3420704 | tf_op jit(solution)/shard_map/ppermute | solution.py:891
  127.4 25.9 %shard_map.265 = bf16[4096,1088]{1,0:T(8,128)(2,1)} custom-call(s32[1]{0:T(128)} %bitcast.3.first_ref, s32[4096,1]{1,0:T(8,128)} %bitcast.265, bf16[1088,1572]{1,0:T(8,128)(2,1)} %collective-permute-done.1.table_ref, bf16[4096,1088]{1,0:T(8,128)(2,1)} %shard_map.264.refs_0_), custom_call_target="tpu_custom_call" | custom-call | tf_op jit(solution)/shard_map/pallas_call | solution.py:798
  153.3 86.3 %shard_map.266 = f32[256,1088]{1,0:T(8,128)} custom-call(bf16[16,256,1088]{2,1,0:T(8,128)(2,1)} %bitcast.260), custom_call_target="tpu_custom_call" | custom-call | tf_op jit(solution)/shard_map/pallas_call | solution.py:448
  244.9 48.3 %shard_map.267 = bf16[2,1536,1088]{2,1,0:T(8,128)(2,1)} custom-call(bf16[2,2,64,1088]{3,2,1,0:T(8,128)(2,1)} %bitcast.274), custom_call_target="tpu_custom_call" | custom-call | tf_op jit(solution)/shard_map/pallas_call | solution.py:285
  296.6 23.7 %convolution_convert_fusion = bf16[3072,2176]{0,1:T(8,128)(2,1)} fusion(bf16[3072,1088]{1,0:T(8,128)(2,1)} %bitcast.261, bf16[13056,1088]{1,0:T(8,128)(2,1)} %all-gather.3.cloned.1.call-done), kind=kOutput, calls=%fused_computation.5 | convolution fusion | flops 14552530944 | bytes 25460736 | tf_op jit(solution)/shard_map/dot_general | solution.py:715
  320.3 34.5 %shard_map.268.l_ref = bf16[1088,256]{1,0:T(8,128)(2,1)} custom-call(s32[128,1]{1,0:T(8,128)} %copy.171.pos_ref, bf16[1088,256]{1,0:T(8,128)(2,1)} %fusion.49.q_ref, bf16[2,1088,3072]{2,1,0:T(8,128)(2,1)} %bitcast.258), custom_call_target="tpu_custom_call" | custom-call | tf_op jit(solution)/shard_map/pallas_call | solution.py:765
  358.5 16.1 %fusion.22 = (bf16[4352,256]{1,0:T(8,128)(2,1)S(1)}, f32[4352,256]{1,0:T(8,128)}, f32[256,4352]{0,1:T(8,128)}) fusion(bf16[256,1088]{1,0:T(8,128)(2,1)S(1)} %add_convert_fusion.2.r_ref, bf16[13056,1088]{1,0:T(8,128)(2,1)} %all-gather.3.cloned.1.call-done), kind=kOutput, calls=%fused_computation.49 | convolution fusion | flops 2496724992 | bytes 21725184 | tf_op jit(solution)/shard_map/dot_general | solution.py:715
  384.0 24.4 %shard_map.269 = bf16[16,64,1088]{2,1,0:T(8,128)(2,1)} custom-call(bf16[64,1088]{1,0:T(8,128)(2,1)} %bitcast.285), custom_call_target="tpu_custom_call" | custom-call | tf_op jit(solution)/shard_map/pallas_call | solution.py:285
  415.7 8.8 fusion.95
  428.9 8.4 shard_map.270
  440.4 10.2 convolution_convert_fusion.2
  470.8 24.9 %shard_map.271 = f32[64,1088]{1,0:T(8,128)} custom-call(bf16[16,64,1088]{2,1,0:T(8,128)(2,1)} %bitcast.270), custom_call_target="tpu_custom_call" | custom-call | tf_op jit(solution)/shard_map/pallas_call | solution.py:448
  501.7 9.0 shard_map.272.refs_0_
  510.8 12.0 %fusion.28.l_ref = bf16[4352,256]{1,0:T(8,128)(2,1)} fusion(f32[4352,256]{1,0:T(8,128)} %get-tuple-element.86, bf16[256,1088]{1,0:T(8,128)(2,1)S(1)} %copy-done.11, bf16[13056,1088]{1,0:T(8,128)(2,1)} %all-gather.3.cloned.1.call-done, f32[256,4352]{0,1:T(8,128)} %get-tuple-element.110), kind=kOutput, calls=%fused_computation.55 | convolution fusion | flops 2439905280 | bytes 21725184 | tf_op jit(solution)/shard_map/dot_general | solution.py:715
  522.7 8.8 shard_map.273
  531.5 9.4 fusion.96
  558.1 40.3 %shard_map.274 = (bf16[1088,256]{1,0:T(8,128)(2,1)}, bf16[2,1088,3072]{2,1,0:T(8,128)(2,1)}) custom-call(s32[128,1]{1,0:T(8,128)} %copy.171.pos_ref, bf16[1088,256]{1,0:T(8,128)(2,1)} %fusion.49.q_ref, bf16[2,1088,3072]{2,1,0:T(8,128)(2,1)} %bitcast.259, bf16[1088,256]{1,0:T(8,128)(2,1)} %fusion.50.g_ref), custom_call_target="tpu_custom_call" | custom-call | tf_op jit(solution)/shard_map/pallas_call | solution.py:778
  600.1 21.5 %convolution_convert_fusion.1 = bf16[3072,1088]{0,1:T(8,128)(2,1)} fusion(bf16[2176,3072]{1,0:T(8,128)(2,1)} %bitcast.266, bf16[13056,1088]{1,0:T(8,128)(2,1)} %all-gather.3.cloned.1.call-done), kind=kOutput, calls=%fused_computation.8 | convolution fusion | flops 14549188608 | bytes 25067520 | tf_op jit(solution)/shard_map/dot_general | solution.py:715
  621.6 9.8 copy.187
  632.1 10.8 fusion.82
  642.9 68.7 %collective-permute-done.2 = bf16[1088,1572]{1,0:T(8,128)(2,1)} collective-permute-done((bf16[1088,1572]{1,0:T(8,128)(2,1)}, bf16[1088,1572]{1,0:T(8,128)(2,1)}, u32[]{:S(2)}, u32[]{:S(2)}) %collective-permute-start.2) | collective-permute-done | bytes 3420704 | tf_op jit(solution)/shard_map/ppermute | solution.py:1042
  715.1 23.0 %shard_map.277 = bf16[4352,1088]{1,0:T(8,128)(2,1)} custom-call(bf16[2176,3072]{1,0:T(8,128)(2,1)} %bitcast.267, bf16[3072,1088]{1,0:T(8,128)(2,1)} %bitcast.262, bf16[4352,1088]{1,0:T(8,128)(2,1)} %shard_map.276.refs_0_), custom_call_target="tpu_custom_call", output_to_operand_aliasing={{}: (2, {})} | custom-call | tf_op jit(solution)/shard_map/pallas_call | solution.py:700
  738.2 47.4 %reduce-scatter.5.cloned.1.call-done = bf16[1,272,1088]{2,1,0:T(8,128)(2,1)} async-done(((bf16[32,272,1088]{2,1,0:T(8,128)(2,1)}), bf16[1,272,1088]{2,1,0:T(8,128)(2,1)}) %reduce-scatter.5.cloned.1.call-update) | async-done | bytes 591888 | tf_op jit(solution)/shard_map/reduce_scatter | solution.py:1068
  793.3 47.3 %shard_map.278 = f32[2,2,64,1088]{3,2,1,0:T(8,128)} custom-call(bf16[2,1536,1088]{2,1,0:T(8,128)(2,1)} %bitcast.263), custom_call_target="tpu_custom_call" | custom-call | tf_op jit(solution)/shard_map/pallas_call | solution.py:448
  847.6 116.2 %shard_map.279 = bf16[2,16,264,1088]{3,2,1,0:T(8,128)(2,1)} custom-call(bf16[264,1088]{1,0:T(8,128)(2,1)} %concatenate.48.x_ref), custom_call_target="tpu_custom_call" | custom-call | tf_op jit(solution)/shard_map/pallas_call | solution.py:622
  978.0 12.0 %fusion.90 = (bf16[1,16,264,1088]{3,2,1,0:T(8,128)(2,1)S(1)}, bf16[1,16,264,1088]{3,2,1,0:T(8,128)(2,1)}) fusion(bf16[2,16,264,1088]{3,2,1,0:T(8,128)(2,1)} %shard_map.279), kind=kLoop, calls=%fused_computation.240 | loop fusion | bytes 36765696 | tf_op jit(solution)/shard_map/slice | solution.py:1110
  990.0 24.1 %fusion.5 = f32[1088,1572]{1,0:T(8,128)} fusion(f32[1088,1572]{1,0:T(8,128)} %convert_add_fusion, bf16[4224,1088]{1,0:T(8,128)(2,1)} %bitcast.269, s32[4224]{0:T(1024)S(1)} %sub.257), kind=kOutput, calls=%fused_computation.11 | convolution fusion | flops 14457268224 | bytes 22891008 | tf_op jit(solution)/shard_map/dot_general | solution.py:715
  1014.2 24.5 %multiply_reduce_fusion = (f32[]{:T(128)}, f32[1088,1572]{1,0:T(8,128)}) fusion(f32[1088,1572]{1,0:T(8,128)} %fusion.5, bf16[4224,1088]{1,0:T(8,128)(2,1)S(1)} %bitcast.268, s32[4224]{0:T(1024)S(1)} %sub.259), kind=kOutput, calls=%fused_computation.28 | convolution fusion | flops 14460688384 | bytes 22891012 | tf_op jit(solution)/shard_map/dot_general | solution.py:715
  1046.2 14.9 %shard_map.280 = f32[32,8,128]{2,1,0:T(8,128)} custom-call(f32[8,128]{1,0:T(8,128)} %broadcast_select_fusion.8.x_ref), custom_call_target="tpu_custom_call" | custom-call | tf_op jit(solution)/shard_map/pallas_call | solution.py:95
  1063.4 21.3 %convert_bitcast_fusion = (bf16[1572,1088]{0,1:T(8,128)(2,1)}, f32[1088,1572]{1,0:T(8,128)}, f32[1572,1088]{0,1:T(8,128)}, f32[1572,1088]{0,1:T(8,128)}) fusion(f32[1572,1088]{0,1:T(8,128)} %param.25, f32[1088,1572]{1,0:T(8,128)} %get-tuple-element.121, f32[]{:T(128)S(6)} %min.3, f32[1572,1088]{0,1:T(8,128)} %param.24, f32[1572,1088]{0,1:T(8,128)} %param.23), kind=kLoop, calls=%fused_computation.72 | loop fusion | flops 29075712 | bytes 51310084 | tf_op jit(solution)/shard_map/transpose | solution.py:1187
  (246 shorter events, 151.6 us)
Async XLA Ops:
  7.2 286.0 %all-gather.3.cloned.1.call-start = ((), (), s32[]{:S(2)}) async-start(), calls=%async_computation.3 | async-start | bytes 31021056 | tf_op jit(solution)/shard_map/all_gather | solution.py:895
  9.9 775.7 %reduce-scatter.5.cloned.1.call-start = ((), (), s32[]{:S(2)}) async-start(), calls=%async_computation.2 | async-start | bytes 20680704 | tf_op jit(solution)/shard_map/reduce_scatter | solution.py:1068
  10.0 8.3 collective-permute-start
  18.3 109.1 %collective-permute-start.1 = (bf16[1088,1572]{1,0:T(8,128)(2,1)}, bf16[1088,1572]{1,0:T(8,128)(2,1)}, u32[]{:S(2)}, u32[]{:S(2)}) collective-permute-start(bf16[1088,1572]{1,0:T(8,128)(2,1)} %bitcast_convert_fusion.table_ref), channel_id=1, source_target_pairs={{0,16},{16,0},{1,17},{17,1},{2,18},{18,2},{3,19},{19,3},{4,20},{20... | collective-permute-start | bytes 10262024 | tf_op jit(solution)/shard_map/ppermute | solution.py:891
  62.2 180.3 %copy-start.19 = (f32[1088]{0:T(1024)}, f32[1088]{0:T(1024)S(1)}, u32[]{:S(2)}) copy-start(f32[1088]{0:T(1024)S(1)} %get-tuple-element.64) | copy-start | bytes 13060
  240.9 52.2 %copy-start.21 = (f32[256]{0:T(256)}, f32[256]{0:T(256)S(1)}, u32[]{:S(2)}) copy-start(f32[256]{0:T(256)S(1)} %broadcast_multiply_fusion.8) | copy-start | bytes 3076
  242.5 50.7 %copy-start.24 = (f32[256]{0:T(256)}, f32[256]{0:T(256)S(1)}, u32[]{:S(2)}) copy-start(f32[256]{0:T(256)S(1)} %add_rsqrt_fusion.2) | copy-start | bytes 3076
  244.9 48.3 %copy-start.8 = (bf16[256,1088]{1,0:T(8,128)(2,1)S(1)}, bf16[256,1088]{1,0:T(8,128)(2,1)}, u32[]{:S(2)}) copy-start(bf16[256,1088]{1,0:T(8,128)(2,1)} %add_convert_fusion.3.r_ref) | copy-start | bytes 1671172
  320.3 34.6 %copy-start.2 = (f32[256,1088]{1,0:T(8,128)S(1)}, f32[256,1088]{1,0:T(8,128)}, u32[]{:S(2)}) copy-start(f32[256,1088]{1,0:T(8,128)} %shard_map.266) | copy-start | bytes 3342340
  358.5 16.1 %copy-start.15 = (bf16[256,1088]{1,0:T(8,128)(2,1)}, bf16[256,1088]{1,0:T(8,128)(2,1)S(1)}, u32[]{:S(2)}) copy-start(bf16[256,1088]{1,0:T(8,128)(2,1)S(1)} %add_convert_fusion.2.r_ref) | copy-start | bytes 1671172
  440.4 18.2 %slice-start = ((s8[6455296]{0:T(1024)(128)(4,1)}), s8[4194304]{0:T(1024)(128)(4,1)S(1)}, s32[]{:S(2)}) async-start(s8[6455296]{0:T(1024)(128)(4,1)} %bitcast.272), calls=%async_computation.5 | async-start | bytes 8388608
  549.6 489.0 %reduce-scatter.7.cloned.1.call-start = ((), (), s32[]{:S(2)}) async-start(), calls=%async_computation.4 | async-start | bytes 10340352
  550.3 3.8 collective-permute-start.3
  598.4 113.2 %collective-permute-start.2 = (bf16[1088,1572]{1,0:T(8,128)(2,1)}, bf16[1088,1572]{1,0:T(8,128)(2,1)}, u32[]{:S(2)}, u32[]{:S(2)}) collective-permute-start(bf16[1088,1572]{1,0:T(8,128)(2,1)} %convolution_convert_fusion.2), channel_id=1, source_target_pairs={{0,16},{16,0},{1,17},{17,1},{2,18},{18,2},{3,19},{19,3},{4,20},{20... | collective-permute-start | bytes 10262024 | tf_op jit(solution)/shard_map/ppermute | solution.py:1042
  793.3 47.4 %copy-start.3 = (f32[256,1088]{1,0:T(8,128)S(1)}, f32[256,1088]{1,0:T(8,128)}, u32[]{:S(2)}) copy-start(f32[256,1088]{1,0:T(8,128)} %shard_map.266) | copy-start | bytes 3342340
  793.3 47.4 %copy-start.17 = (bf16[1088,256]{1,0:T(8,128)(2,1)S(1)}, bf16[1088,256]{1,0:T(8,128)(2,1)}, u32[]{:S(2)}) copy-start(bf16[1088,256]{1,0:T(8,128)(2,1)} %get-tuple-element.38.l_ref) | copy-start | bytes 1671172
  793.3 47.4 %copy-start.20 = (f32[1088]{0:T(1024)S(1)}, f32[1088]{0:T(1024)}, u32[]{:S(2)}) copy-start(f32[1088]{0:T(1024)} %copy-done.19) | copy-start | bytes 13060
  793.3 47.4 %copy-start.22 = (f32[256]{0:T(256)S(1)}, f32[256]{0:T(256)}, u32[]{:S(2)}) copy-start(f32[256]{0:T(256)} %copy-done.21) | copy-start | bytes 3076
  793.3 47.4 %copy-start.25 = (f32[256]{0:T(256)S(1)}, f32[256]{0:T(256)}, u32[]{:S(2)}) copy-start(f32[256]{0:T(256)} %copy-done.24) | copy-start | bytes 3076
  847.6 117.5 %copy-start.10 = (bf16[1,272,1088]{2,1,0:T(8,128)(2,1)S(1)}, bf16[1,272,1088]{2,1,0:T(8,128)(2,1)}, u32[]{:S(2)}) copy-start(bf16[1,272,1088]{2,1,0:T(8,128)(2,1)} %reduce-scatter.5.cloned.1.call-done) | copy-start | bytes 1775620
  965.1 121.7 %collective-permute-start.9 = (bf16[136,1088]{1,0:T(8,128)(2,1)S(1)}, bf16[136,1088]{1,0:T(8,128)(2,1)}, u32[]{:S(2)}, u32[]{:S(2)}) collective-permute-start(bf16[136,1088]{1,0:T(8,128)(2,1)S(1)} %get-tuple-element.94), channel_id=1, source_target_pairs={{0,10},{1,11},{3,12},{4,13},{6,14},{7,15},{9,16},{10,17},{12,18},{... | collective-permute-start | bytes 887816 | tf_op jit(solution)/shard_map/ppermute | solution.py:821
  973.0 115.5 %collective-permute-start.7 = (bf16[136,1088]{1,0:T(8,128)(2,1)S(1)}, bf16[136,1088]{1,0:T(8,128)(2,1)}, u32[]{:S(2)}, u32[]{:S(2)}) collective-permute-start(bf16[136,1088]{1,0:T(8,128)(2,1)S(1)} %get-tuple-element.95), channel_id=1, source_target_pairs={{1,11},{2,12},{4,13},{5,14},{7,15},{8,16},{10,17},{11,18},{13,19},... | collective-permute-start | bytes 887816 | tf_op jit(solution)/shard_map/ppermute | solution.py:821
  974.4 115.2 %collective-permute-start.5 = (bf16[136,1088]{1,0:T(8,128)(2,1)S(1)}, bf16[136,1088]{1,0:T(8,128)(2,1)}, u32[]{:S(2)}, u32[]{:S(2)}) collective-permute-start(bf16[136,1088]{1,0:T(8,128)(2,1)S(1)} %get-tuple-element.93), channel_id=1, source_target_pairs={{0,11},{2,12},{3,13},{5,14},{6,15},{8,16},{9,17},{11,18},{12,19},{... | collective-permute-start | bytes 887816 | tf_op jit(solution)/shard_map/ppermute | solution.py:821
  1014.2 31.4 %copy-start.36 = (pred[128]{0:T(512)(128)(4,1)S(1)}, pred[128]{0:T(512)(128)(4,1)}, u32[]{:S(2)}) copy-start(pred[128]{0:T(512)(128)(4,1)} %iota_compare_fusion.15) | copy-start | bytes 388
  1038.7 48.8 %collective-permute-start.8 = (bf16[136,1088]{1,0:T(8,128)(2,1)}, bf16[136,1088]{1,0:T(8,128)(2,1)}, u32[]{:S(2)}, u32[]{:S(2)}) collective-permute-start(bf16[136,1088]{1,0:T(8,128)(2,1)} %bitcast.286), channel_id=1, source_target_pairs={{2,0},{5,1},{8,2},{11,3},{14,4},{17,5},{20,6},{23,7},{26,8},{29,9}} | collective-permute-start | bytes 887816 | tf_op jit(solution)/shard_map/ppermute | solution.py:817
  1040.0 48.6 %collective-permute-start.6 = (bf16[136,1088]{1,0:T(8,128)(2,1)}, bf16[136,1088]{1,0:T(8,128)(2,1)}, u32[]{:S(2)}, u32[]{:S(2)}) collective-permute-start(bf16[136,1088]{1,0:T(8,128)(2,1)} %bitcast.287), channel_id=1, source_target_pairs={{1,0},{4,1},{7,2},{10,3},{13,4},{16,5},{19,6},{22,7},{25,8},{28,9}... | collective-permute-start | bytes 887816 | tf_op jit(solution)/shard_map/ppermute | solution.py:817
  1063.4 22.8 %copy-start.27 = (f32[204]{0:T(256)S(1)}, f32[204]{0:T(256)}, u32[]{:S(2)}) copy-start(f32[204]{0:T(256)} %param.29) | copy-start | bytes 2452
  1063.4 22.7 %copy-start.31 = (f32[204]{0:T(256)S(1)}, f32[204]{0:T(256)}, u32[]{:S(2)}) copy-start(f32[204]{0:T(256)} %param.30) | copy-start | bytes 2452
  1063.4 22.7 %copy-start.32 = (f32[204]{0:T(256)S(1)}, f32[204]{0:T(256)}, u32[]{:S(2)}) copy-start(f32[204]{0:T(256)} %param.31) | copy-start | bytes 2452
  1063.4 23.4 %copy-start.18 = (bf16[1,136,1088]{2,1,0:T(8,128)(2,1)S(1)}, bf16[1,136,1088]{2,1,0:T(8,128)(2,1)}, u32[]{:S(2)}) copy-start(bf16[1,136,1088]{2,1,0:T(8,128)(2,1)} %reduce-scatter.7.cloned.1.call-done) | copy-start | bytes 887812
  1063.4 26.2 %copy-start.5 = (f32[1088,408]{0,1:T(8,128)S(1)}, f32[1088,408]{0,1:T(8,128)}, u32[]{:S(2)}) copy-start(f32[1088,408]{0,1:T(8,128)} %param.26) | copy-start | bytes 5326852
  1086.8 2.8 collective-permute-start.4
  (20 other events, 156.7 us)
Sparse Core Ops, SparseCore 0:
  11.4 215.6 all-gather.2
  549.7 235.8 reduce-scatter.4
  791.7 160.0 reduce-scatter.6

commit v4 on v2

--- a/solution.py
+++ b/solution.py
@@ -6,6 +6,7 @@
 from jax.experimental import pallas as pl
 from jax.experimental.pallas import tpu as pltpu
 from jax.sharding import PartitionSpec as P
+
 
 HEADS = 17
 HD = 64
@@ -199,12 +200,12 @@
 
     items = 2 * line - 1
 
-    def goes_up(part, item):
-        low, high = low_high(spans[part])
+    def goes_up(part):
+        _, high = low_high(spans[part])
         return at + 1 < high
 
-    def goes_down(part, item):
-        low, high = low_high(spans[part])
+    def goes_down(part):
+        low, _ = low_high(spans[part])
         return at - 1 >= low
 
     def active(part, item):
@@ -220,12 +221,12 @@
         def _():
             if item == 0 or item % 2 == 1:
                 if (item + 1) // 2 + 1 < spans[part]:
-                    @pl.when(goes_up(part, item))
+                    @pl.when(goes_up(part))
                     def _():
                         z_copy(part, item, True).start()
             if item == 0 or item % 2 == 0:
                 if (item + 1) // 2 + 1 < spans[part]:
-                    @pl.when(goes_down(part, item))
+                    @pl.when(goes_down(part))
                     def _():
                         z_copy(part, item, False).start()
             b_copy(part, item).start()
@@ -246,6 +247,7 @@
                     @pl.when(valid(part, item))
                     def _():
                         z_arrived(part, item).wait_recv()
+
                     launch(part, item)
         last = [0] if far == 1 else [2 * far - 3, 2 * far - 2]
         for item in last:
@@ -261,11 +263,11 @@
             @pl.when(valid(part, item))
             def _():
                 if (item == 0 or item % 2 == 1) and (item + 1) // 2 + 1 < spans[part]:
-                    @pl.when(goes_up(part, item))
+                    @pl.when(goes_up(part))
                     def _():
                         z_copy(part, item, True).wait_send()
                 if (item == 0 or item % 2 == 0) and (item + 1) // 2 + 1 < spans[part]:
-                    @pl.when(goes_down(part, item))
+                    @pl.when(goes_down(part))
                     def _():
                         z_copy(part, item, False).wait_send()
                 b_copy(part, item).wait_send()
@@ -1047,6 +1049,8 @@
     weight_grad = place_product(weight_grad, attended, grad_branch, 3 * width, columns)
     grad_attended = contract(w_o, grad_branch, 1, 1).astype(BF)
     grad_query, grad_pairs = attend_back(query_pos, queries, pairs, grad_attended)
+    if group_count == 2:
+        grad_query, head_other = lax.optimization_barrier((grad_query, head_other))
     grad_pairs = grad_pairs.reshape(2 * width, MB * key_rows)
     weight_grad = place_product(weight_grad, grad_query, hidden_one, 0, columns)
     weight_grad = place_product(weight_grad, grad_pairs, hidden_sel, width, columns)
@@ -1073,17 +1077,15 @@
             8,
         )
         other_slots = lax.ppermute(row_slots, "dp", moved)
-        all_slots = jnp.where(
-            group_rank == 0,
-            jnp.stack([row_slots, other_slots]),
-            jnp.stack([other_slots, row_slots]),
-        ).reshape(all_count, own_rows)
-        all_slots = jnp.pad(all_slots, ((0, 0), (0, pad_rows)), constant_values=-1).reshape(-1)
-        embed_sum = (
-            contract(all_rows.reshape(-1, width), hits(all_slots, 0).astype(BF), 0, 0)
-            + head_own
-            + head_other.astype(F32)
-        )
+        embed_sum = lax.optimization_barrier(head_own + head_other.astype(F32))
+        for part in range(group_count):
+            part_slots = jnp.where(group_rank == part, row_slots, other_slots)
+            part_slots = jnp.pad(
+                part_slots.reshape(seq_count, own_rows), ((0, 0), (0, pad_rows)), constant_values=-1
+            ).reshape(-1)
+            embed_sum = embed_sum + contract(
+                all_rows[part].reshape(-1, width), hits(part_slots, 0).astype(BF), 0, 0
+            )
         norm_all = jnp.sum(
             all_rows.reshape(all_count, own_rows + pad_rows, width)[
                 :, own_rows : own_rows + 6

time: 1080 us -> 1030 us (0.954)
  matrix products: 268 us -> 203 us
  local copies, waits for them, and re-layouts: 30.2 us -> 41.7 us
    dot_general x17 -> x18, matrix products: 267 us -> 202 us  [contract(): lax.dot_general(left, right, (((left_dim,), (right_dim,)), ((), ())), pre...]
    slice x1 -> x2, local copies, waits for them, and re-layouts: 0.18 us -> 12.2 us  [the longest x1 12.1 us: on_device(): all_rows[part].reshape(-1, width)]
    pallas_call x1, Pallas kernels: 151 us -> 139 us  [exchange(): pl.pallas_call(exchange_kernel, out_shape=jax.ShapeDtypeStruct((2, count)...]
  transfers between devices with their start and end apart: 6 -> 6, of which waited for: 2 -> 2; matrix products, arithmetic and copies ran while one was open for 17% -> 16% of each run, Pallas kernels for 39% -> 47%
where the time goes in v4:
time: 1030 us; the launch traced here: 1010 us
  Pallas kernels  604 us (59%)
  matrix products  203 us (20%)
  other arithmetic  71.1 us (7%)
  waiting for transfers between devices  68.3 us (7%)
  local copies, waits for them, and re-layouts  41.7 us (4%)
  between operations  19.2 us (2%)
    dot_general x18, matrix products, contract(): lax.dot_general(left, right, (((left_dim,), (right_dim,)), ((), ())), pre...  202 us
    pallas_call x3, Pallas kernels, fold(): pl.pallas_call(functools.partial(fold_kernel, (len(arrays), len(out_shape...  189 us
    pallas_call x1, Pallas kernels, exchange(): pl.pallas_call(exchange_kernel, out_shape=jax.ShapeDtypeStruct((2, count)...  139 us
    pallas_call x2, Pallas kernels, spread(): pl.pallas_call(functools.partial(spread_kernel, (len(blocks), len(out_sha...  72.7 us
    ppermute x1, waiting for transfers between devices, on_device(): lax.ppermute(slab_t[0], 'dp', [(i, (i - step) % group_count) for i in ran...  65.1 us
    pallas_call x2, Pallas kernels, lookup(): pl.pallas_call(lookup_kernel, grid=(slots.shape[0] // block,), out_shape=...  51.4 us
    pallas_call x5, Pallas kernels, place_product(): pl.pallas_call(place_kernel, grid=(left.shape[0] // block,), out_shape=ja...  47.7 us
    pallas_call x1, Pallas kernels, attend_back(): pl.pallas_call(attend_back_kernel, grid=(q.shape[1] // rows, HEADS), out_...  39.6 us
  transfers between devices with their start and end apart: 6, of which 2 were waited for; matrix products, arithmetic and copies ran while one was open for 16% of the time, Pallas kernels for 47%

profile of v4, /device:TPU:0, one launch (start us, length us, event | category | flops | bytes accessed | tf_op | source)
XLA Modules:
  0.0 1012.6 jit_solution(17240932890810146961)
XLA Ops:
  23.0 9.7 shard_map.263
  36.6 25.6 %shard_map.264.refs_0_ = bf16[4096,1088]{1,0:T(8,128)(2,1)} custom-call(s32[1]{0:T(128)} %bitcast.8.first_ref, s32[4096,1]{1,0:T(8,128)} %bitcast.278, bf16[1088,1572]{1,0:T(8,128)(2,1)} %bitcast_convert_fusion.table_ref), custom_call_target="tpu_custom_call" | custom-call | tf_op jit(solution)/shard_map/pallas_call | solution.py:798
  62.2 65.1 %collective-permute-done.1.table_ref = bf16[1088,1572]{1,0:T(8,128)(2,1)} collective-permute-done((bf16[1088,1572]{1,0:T(8,128)(2,1)}, bf16[1088,1572]{1,0:T(8,128)(2,1)}, u32[]{:S(2)}, u32[]{:S(2)}) %collective-permute-start.1) | collective-permute-done | bytes 3420704 | tf_op jit(solution)/shard_map/ppermute | solution.py:873
  127.4 25.8 %shard_map.265 = bf16[4096,1088]{1,0:T(8,128)(2,1)} custom-call(s32[1]{0:T(128)} %bitcast.3.first_ref, s32[4096,1]{1,0:T(8,128)} %bitcast.279, bf16[1088,1572]{1,0:T(8,128)(2,1)} %collective-permute-done.1.table_ref, bf16[4096,1088]{1,0:T(8,128)(2,1)} %shard_map.264.refs_0_), custom_call_target="tpu_custom_call" | custom-call | tf_op jit(solution)/shard_map/pallas_call | solution.py:798
  153.2 86.2 %shard_map.266 = f32[256,1088]{1,0:T(8,128)} custom-call(bf16[16,256,1088]{2,1,0:T(8,128)(2,1)} %bitcast.274), custom_call_target="tpu_custom_call" | custom-call | tf_op jit(solution)/shard_map/pallas_call | solution.py:448
  244.8 48.3 %shard_map.267 = bf16[2,1536,1088]{2,1,0:T(8,128)(2,1)} custom-call(bf16[2,2,64,1088]{3,2,1,0:T(8,128)(2,1)} %bitcast.288), custom_call_target="tpu_custom_call" | custom-call | tf_op jit(solution)/shard_map/pallas_call | solution.py:285
  296.6 23.4 %convolution_convert_fusion = bf16[3072,2176]{0,1:T(8,128)(2,1)} fusion(bf16[3072,1088]{1,0:T(8,128)(2,1)} %bitcast.275, bf16[13056,1088]{1,0:T(8,128)(2,1)} %all-gather.3.cloned.1.call-done), kind=kOutput, calls=%fused_computation.5 | convolution fusion | flops 14552530944 | bytes 25460736 | tf_op jit(solution)/shard_map/dot_general | solution.py:715
  320.0 34.5 %shard_map.268.l_ref = bf16[1088,256]{1,0:T(8,128)(2,1)} custom-call(s32[128,1]{1,0:T(8,128)} %copy.172.pos_ref, bf16[1088,256]{1,0:T(8,128)(2,1)} %fusion.49.q_ref, bf16[2,1088,3072]{2,1,0:T(8,128)(2,1)} %bitcast.272), custom_call_target="tpu_custom_call" | custom-call | tf_op jit(solution)/shard_map/pallas_call | solution.py:765
  358.2 16.2 %fusion.22 = (bf16[4352,256]{1,0:T(8,128)(2,1)S(1)}, f32[4352,256]{1,0:T(8,128)}, f32[256,4352]{0,1:T(8,128)}) fusion(bf16[256,1088]{1,0:T(8,128)(2,1)S(1)} %add_convert_fusion.2.r_ref, bf16[13056,1088]{1,0:T(8,128)(2,1)} %all-gather.3.cloned.1.call-done), kind=kOutput, calls=%fused_computation.49 | convolution fusion | flops 2496724992 | bytes 21725184 | tf_op jit(solution)/shard_map/dot_general | solution.py:715
  374.4 7.9 fusion.97
  383.6 24.5 %shard_map.269 = bf16[16,64,1088]{2,1,0:T(8,128)(2,1)} custom-call(bf16[64,1088]{1,0:T(8,128)(2,1)} %bitcast.297), custom_call_target="tpu_custom_call" | custom-call | tf_op jit(solution)/shard_map/pallas_call | solution.py:285
  415.5 8.9 fusion.99
  428.9 8.4 shard_map.270
  440.4 10.0 convolution_convert_fusion.2
  450.5 8.1 fusion.87
  470.7 25.0 %shard_map.271 = f32[64,1088]{1,0:T(8,128)} custom-call(bf16[16,64,1088]{2,1,0:T(8,128)(2,1)} %bitcast.284), custom_call_target="tpu_custom_call" | custom-call | tf_op jit(solution)/shard_map/pallas_call | solution.py:448
  501.9 9.0 shard_map.275.refs_0_
  510.9 10.6 %fusion.28.l_ref = bf16[4352,256]{1,0:T(8,128)(2,1)S(1)} fusion(f32[4352,256]{1,0:T(8,128)} %get-tuple-element.76, bf16[256,1088]{1,0:T(8,128)(2,1)S(1)} %copy-done.12, bf16[13056,1088]{1,0:T(8,128)(2,1)} %all-gather.3.cloned.1.call-done, f32[256,4352]{0,1:T(8,128)} %get-tuple-element.97), kind=kOutput, calls=%fused_computation.55 | convolution fusion | flops 2439905280 | bytes 21725184 | tf_op jit(solution)/shard_map/dot_general | solution.py:715
  521.5 9.3 fusion.100
  538.2 39.6 %shard_map.272 = (bf16[1088,256]{1,0:T(8,128)(2,1)}, bf16[2,1088,3072]{2,1,0:T(8,128)(2,1)}) custom-call(s32[128,1]{1,0:T(8,128)} %copy.172.pos_ref, bf16[1088,256]{1,0:T(8,128)(2,1)} %fusion.49.q_ref, bf16[2,1088,3072]{2,1,0:T(8,128)(2,1)} %bitcast.273, bf16[1088,256]{1,0:T(8,128)(2,1)} %fusion.50.g_ref), custom_call_target="tpu_custom_call" | custom-call | tf_op jit(solution)/shard_map/pallas_call | solution.py:778
  577.7 9.0 shard_map.276.refs_0_
  593.5 23.0 %shard_map.279 = bf16[13056,1088]{1,0:T(8,128)(2,1)} custom-call(bf16[2176,3072]{1,0:T(8,128)(2,1)} %bitcast.280, bf16[3072,1088]{1,0:T(8,128)(2,1)} %bitcast.276, bf16[13056,1088]{1,0:T(8,128)(2,1)} %shard_map.278.refs_0_), custom_call_target="tpu_custom_call", output_to_operand_aliasing={{}: (2, {})} | custom-call | tf_op jit(solution)/shard_map/pallas_call | solution.py:700
  621.3 22.5 %convolution_convert_fusion.1 = bf16[3072,1088]{0,1:T(8,128)(2,1)} fusion(bf16[2176,3072]{1,0:T(8,128)(2,1)} %bitcast.281, bf16[13056,1088]{1,0:T(8,128)(2,1)} %all-gather.3.cloned.1.call-done), kind=kOutput, calls=%fused_computation.8 | convolution fusion | flops 14549188608 | bytes 25067520 | tf_op jit(solution)/shard_map/dot_general | solution.py:715
  643.8 10.6 %copy.188 = bf16[3072,1088]{1,0:T(8,128)(2,1)} copy(bf16[3072,1088]{0,1:T(8,128)(2,1)} %convolution_convert_fusion.1) | data formatting | bytes 13369344 | tf_op jit(solution)/shard_map/convert_element_type | solution.py:1057
  654.4 78.2 %shard_map.273 = f32[2,2,64,1088]{3,2,1,0:T(8,128)} custom-call(bf16[2,1536,1088]{2,1,0:T(8,128)(2,1)} %bitcast.277), custom_call_target="tpu_custom_call" | custom-call | tf_op jit(solution)/shard_map/pallas_call | solution.py:448
  733.4 8.2 fusion.86
  753.9 139.4 %shard_map.274 = bf16[2,16,264,1088]{3,2,1,0:T(8,128)(2,1)} custom-call(bf16[264,1088]{1,0:T(8,128)(2,1)} %concatenate.45.x_ref), custom_call_target="tpu_custom_call" | custom-call | tf_op jit(solution)/shard_map/pallas_call | solution.py:622
  895.3 12.1 %fusion.94 = (bf16[1,16,264,1088]{3,2,1,0:T(8,128)(2,1)S(1)}, bf16[1,16,264,1088]{3,2,1,0:T(8,128)(2,1)}) fusion(bf16[2,16,264,1088]{3,2,1,0:T(8,128)(2,1)} %shard_map.274), kind=kLoop, calls=%fused_computation.235 | loop fusion | bytes 36765696 | tf_op jit(solution)/shard_map/slice | solution.py:1087
  907.4 24.4 %fusion.5 = f32[1088,1572]{1,0:T(8,128)} fusion(f32[1088,1572]{1,0:T(8,128)} %convert_add_fusion, bf16[4224,1088]{1,0:T(8,128)(2,1)} %bitcast.283, s32[4224]{0:T(1024)S(1)} %sub.251), kind=kOutput, calls=%fused_computation.11 | convolution fusion | flops 14457268224 | bytes 22891008 | tf_op jit(solution)/shard_map/dot_general | solution.py:715
  931.7 24.4 %multiply_reduce_fusion = (f32[]{:T(128)}, f32[1088,1572]{1,0:T(8,128)}) fusion(f32[1088,1572]{1,0:T(8,128)} %fusion.5, bf16[4224,1088]{1,0:T(8,128)(2,1)S(1)} %bitcast.282, s32[4224]{0:T(1024)S(1)} %sub.253), kind=kOutput, calls=%fused_computation.28 | convolution fusion | flops 14460688384 | bytes 22891012 | tf_op jit(solution)/shard_map/dot_general | solution.py:715
  960.9 11.1 %shard_map.280 = f32[32,8,128]{2,1,0:T(8,128)} custom-call(f32[8,128]{1,0:T(8,128)} %broadcast_select_fusion.2.x_ref), custom_call_target="tpu_custom_call" | custom-call | tf_op jit(solution)/shard_map/pallas_call | solution.py:95
  976.4 21.6 %convert_bitcast_fusion = (bf16[1572,1088]{0,1:T(8,128)(2,1)}, f32[1088,1572]{1,0:T(8,128)}, f32[1572,1088]{0,1:T(8,128)}, f32[1572,1088]{0,1:T(8,128)}) fusion(f32[1572,1088]{0,1:T(8,128)} %param.25, f32[1088,1572]{1,0:T(8,128)} %get-tuple-element.108, f32[]{:T(128)S(6)} %min.3, f32[1572,1088]{0,1:T(8,128)} %param.24, f32[1572,1088]{0,1:T(8,128)} %param.23), kind=kLoop, calls=%fused_computation.72 | loop fusion | flops 29075712 | bytes 51310084 | tf_op jit(solution)/shard_map/transpose | solution.py:1163
  (240 shorter events, 113.2 us)
Async XLA Ops:
  7.2 11.6 %copy-start = (s32[50304]{0:T(1024)S(1)}, s32[50304]{0:T(1024)}, u32[]{:S(2)}) copy-start(s32[50304]{0:T(1024)} %param.22) | copy-start | bytes 603652
  7.2 285.9 %all-gather.3.cloned.1.call-start = ((), (), s32[]{:S(2)}) async-start(), calls=%async_computation.1 | async-start | bytes 31021056 | tf_op jit(solution)/shard_map/all_gather | solution.py:877
  9.9 12.0 %copy-start.41 = (f32[2,2,2]{2,1,0:T(2,128)S(1)}, f32[2,2,2]{2,1,0:T(2,128)}, u32[]{:S(2)}) copy-start(f32[2,2,2]{2,1,0:T(2,128)} %param.21) | copy-start | bytes 100
  9.9 12.0 %copy-start.42 = (s32[2,2,2]{2,1,0:T(2,128)S(1)}, s32[2,2,2]{2,1,0:T(2,128)}, u32[]{:S(2)}) copy-start(s32[2,2,2]{2,1,0:T(2,128)} %param.20) | copy-start | bytes 100
  9.9 12.0 %copy-start.43 = (s32[2,2,2]{2,1,0:T(2,128)S(1)}, s32[2,2,2]{2,1,0:T(2,128)}, u32[]{:S(2)}) copy-start(s32[2,2,2]{2,1,0:T(2,128)} %param.19) | copy-start | bytes 100
  9.9 12.2 %copy-start.33 = (f32[204]{0:T(256)S(1)}, f32[204]{0:T(256)}, u32[]{:S(2)}) copy-start(f32[204]{0:T(256)} %param.29) | copy-start | bytes 2452
  9.9 946.2 %reduce-scatter.4.cloned.1.call-start = ((), (), s32[]{:S(2)}) async-start(), calls=%async_computation.2 | async-start | bytes 31021056
  10.0 8.3 collective-permute-start
  18.3 109.1 %collective-permute-start.1 = (bf16[1088,1572]{1,0:T(8,128)(2,1)}, bf16[1088,1572]{1,0:T(8,128)(2,1)}, u32[]{:S(2)}, u32[]{:S(2)}) collective-permute-start(bf16[1088,1572]{1,0:T(8,128)(2,1)} %bitcast_convert_fusion.table_ref), channel_id=1, source_target_pairs={{0,16},{16,0},{1,17},{17,1},{2,18},{18,2},{3,19},{19,3},{4,20},{20... | collective-permute-start | bytes 10262024 | tf_op jit(solution)/shard_map/ppermute | solution.py:873
  33.9 424.6 %copy-start.24 = (s32[1024]{0:T(1024)}, s32[1024]{0:T(1024)S(1)}, u32[]{:S(2)}) copy-start(s32[1024]{0:T(1024)S(1)} %sub.224) | copy-start | bytes 12292
  62.2 180.2 %copy-start.17 = (f32[1088]{0:T(1024)}, f32[1088]{0:T(1024)S(1)}, u32[]{:S(2)}) copy-start(f32[1088]{0:T(1024)S(1)} %get-tuple-element.54) | copy-start | bytes 13060
  240.9 52.2 %copy-start.19 = (f32[256]{0:T(256)}, f32[256]{0:T(256)S(1)}, u32[]{:S(2)}) copy-start(f32[256]{0:T(256)S(1)} %broadcast_multiply_fusion.8) | copy-start | bytes 3076
  242.4 50.7 %copy-start.22 = (f32[256]{0:T(256)}, f32[256]{0:T(256)S(1)}, u32[]{:S(2)}) copy-start(f32[256]{0:T(256)S(1)} %add_rsqrt_fusion.2) | copy-start | bytes 3076
  244.8 48.3 %copy-start.7 = (bf16[256,1088]{1,0:T(8,128)(2,1)S(1)}, bf16[256,1088]{1,0:T(8,128)(2,1)}, u32[]{:S(2)}) copy-start(bf16[256,1088]{1,0:T(8,128)(2,1)} %add_convert_fusion.3.r_ref) | copy-start | bytes 1671172
  320.0 34.5 %copy-start.2 = (f32[256,1088]{1,0:T(8,128)S(1)}, f32[256,1088]{1,0:T(8,128)}, u32[]{:S(2)}) copy-start(f32[256,1088]{1,0:T(8,128)} %shard_map.266) | copy-start | bytes 3342340
  358.1 16.2 %copy-start.10 = (bf16[256,1088]{1,0:T(8,128)(2,1)}, bf16[256,1088]{1,0:T(8,128)(2,1)S(1)}, u32[]{:S(2)}) copy-start(bf16[256,1088]{1,0:T(8,128)(2,1)S(1)} %add_convert_fusion.2.r_ref) | copy-start | bytes 1671172
  438.5 20.0 %copy-start.29 = (f32[1024]{0:T(1024)}, f32[1024]{0:T(1024)S(1)}, u32[]{:S(2)}) copy-start(f32[1024]{0:T(1024)S(1)} %get-tuple-element.74) | copy-start | bytes 12292
  440.4 18.1 %copy-start.31 = (f32[1024]{0:T(1024)}, f32[1024]{0:T(1024)S(1)}, u32[]{:S(2)}) copy-start(f32[1024]{0:T(1024)S(1)} %mul.452) | copy-start | bytes 12292
  440.4 18.1 %slice-start = ((s8[6455296]{0:T(1024)(128)(4,1)}), s8[4194304]{0:T(1024)(128)(4,1)S(1)}, s32[]{:S(2)}) async-start(s8[6455296]{0:T(1024)(128)(4,1)} %bitcast.286), calls=%async_computation.3 | async-start | bytes 8388608
  498.9 91.3 %collective-permute-start.2 = (bf16[1088,1572]{1,0:T(8,128)(2,1)}, bf16[1088,1572]{1,0:T(8,128)(2,1)}, u32[]{:S(2)}, u32[]{:S(2)}) collective-permute-start(bf16[1088,1572]{1,0:T(8,128)(2,1)} %convolution_convert_fusion.2), channel_id=1, source_target_pairs={{0,16},{16,0},{1,17},{17,1},{2,18},{18,2},{3,19},{19,3},{4,20},{20... | collective-permute-start | bytes 10262024 | tf_op jit(solution)/shard_map/ppermute | solution.py:1024
  501.9 9.0 copy-start.12
  521.5 9.3 copy-start.15
  617.2 3.8 collective-permute-start.3
  654.4 78.9 %copy-start.25 = (s32[1024]{0:T(1024)S(1)}, s32[1024]{0:T(1024)}, u32[]{:S(2)}) copy-start(s32[1024]{0:T(1024)} %copy-done.24) | copy-start | bytes 12292
  654.4 78.9 %copy-start.30 = (f32[1024]{0:T(1024)S(1)}, f32[1024]{0:T(1024)}, u32[]{:S(2)}) copy-start(f32[1024]{0:T(1024)} %copy-done.29) | copy-start | bytes 12292
  654.4 78.9 %copy-start.32 = (f32[1024]{0:T(1024)S(1)}, f32[1024]{0:T(1024)}, u32[]{:S(2)}) copy-start(f32[1024]{0:T(1024)} %copy-done.31) | copy-start | bytes 12292
  931.7 44.0 %copy-start.34 = (f32[204]{0:T(256)S(1)}, f32[204]{0:T(256)}, u32[]{:S(2)}) copy-start(f32[204]{0:T(256)} %param.29) | copy-start | bytes 2452
  931.7 44.0 %copy-start.39 = (f32[204]{0:T(256)S(1)}, f32[204]{0:T(256)}, u32[]{:S(2)}) copy-start(f32[204]{0:T(256)} %param.30) | copy-start | bytes 2452
  931.7 44.0 %copy-start.40 = (f32[204]{0:T(256)S(1)}, f32[204]{0:T(256)}, u32[]{:S(2)}) copy-start(f32[204]{0:T(256)} %param.31) | copy-start | bytes 2452
  976.4 21.6 %copy-start.4 = (f32[1088,408]{0,1:T(8,128)S(1)}, f32[1088,408]{0,1:T(8,128)}, u32[]{:S(2)}) copy-start(f32[1088,408]{0,1:T(8,128)} %param.26) | copy-start | bytes 5326852
  976.4 21.6 %copy-start.9 = (bf16[1,408,1088]{2,1,0:T(8,128)(2,1)S(1)}, bf16[1,408,1088]{2,1,0:T(8,128)(2,1)}, u32[]{:S(2)}) copy-start(bf16[1,408,1088]{2,1,0:T(8,128)(2,1)} %reduce-scatter.4.cloned.1.call-done) | copy-start | bytes 2663428
  976.4 28.0 %copy-start.1 = (s32[50304]{0:T(1024)S(1)}, s32[50304]{0:T(1024)}, u32[]{:S(2)}) copy-start(s32[50304]{0:T(1024)} %param.22) | copy-start | bytes 603652
  (20 other events, 117.7 us)
Sparse Core Ops, SparseCore 0:
  11.4 215.6 all-gather.2
  616.6 331.1 reduce-scatter.3

commit v5 on v4

--- a/solution.py
+++ b/solution.py
@@ -457,8 +457,8 @@
     )(*arrays)
 
 
-def exchange_kernel(x_ref, o_ref, own_sem, z_send, z_recv, x_send, x_recv, y_send, y_recv, c_send, c_recv):
-    count = o_ref.shape[1]
+def exchange_kernel(x_ref, own_ref, other_ref, own_sem, z_send, z_recv, x_send, x_recv, y_send, y_recv, c_send, c_recv):
+    count = own_ref.shape[0]
     line = count // 4
     group = lax.axis_index("dp")
     me = lax.axis_index("seq")
@@ -488,10 +488,10 @@
             action()
 
     def spot(item, other_group, other_side, other_core):
-        g = 1 - group if other_group else group
+        ref = other_ref if other_group else own_ref
         s = 1 - side if other_side else side
         c = 1 - core if other_core else core
-        return o_ref.at[g, 4 * where_of(item) + 2 * s + c]
+        return ref.at[4 * where_of(item) + 2 * s + c]
 
     def here(item, other_group, other_side):
         if item == (0, 0) and not other_group and not other_side:
@@ -508,7 +508,7 @@
         return remote(src, dst, x_send, x_recv, 2 * number(item) + other_group, beside)
 
     def cross_copy(item, other_side, arrived):
-        dst = spot(item, arrived, other_side, 0)
+        dst = spot(item, 1, other_side, 0)
         src = dst if arrived else here(item, 0, other_side)
         return remote(src, dst, y_send, y_recv, 2 * number(item) + other_side, across)
 
@@ -552,19 +552,18 @@
 
     def second(item):
         side_copy(item, 0, True).wait_recv()
+        core_copy(item, 0, 1, False).start()
+        cross_copy(item, 0, True).wait_recv()
+        core_copy(item, 1, 0, False).start()
+
+    def diagonal(item):
+        @pl.when(by_side(item))
+        def _():
+            side_copy(item, 1, False).start()
 
         @pl.when(jnp.logical_not(by_side(item)))
         def _():
             cross_copy(item, 1, False).start()
-
-        core_copy(item, 0, 1, False).start()
-        cross_copy(item, 0, True).wait_recv()
-
-        @pl.when(by_side(item))
-        def _():
-            side_copy(item, 1, False).start()
-
-        core_copy(item, 1, 0, False).start()
 
     def third(item):
         @pl.when(by_side(item))
@@ -583,14 +582,17 @@
     own = pltpu.make_async_copy(x_ref, spot((0, 0), 0, 0, 0), own_sem.at[0])
     own.start()
     launch((0, 0))
-    for step in range(1, line + 2):
+    for step in range(1, line + 1):
         for item in at_far(step):
             given(item, functools.partial(first, item))
         for item in at_far(step - 1):
             given(item, functools.partial(second, item))
-        if step >= 2:
-            for item in at_far(step - 2):
-                given(item, functools.partial(third, item))
+        if step >= line - 1:
+            for far in range(line - 1) if step == line - 1 else [line - 1]:
+                for item in at_far(far):
+                    given(item, functools.partial(diagonal, item))
+    for item in items:
+        given(item, functools.partial(third, item))
     own.wait()
 
     def finish(item):
@@ -621,9 +623,9 @@
     sem = pltpu.SemaphoreType.DMA
     return pl.pallas_call(
         exchange_kernel,
-        out_shape=jax.ShapeDtypeStruct((2, count) + x.shape, x.dtype),
+        out_shape=[jax.ShapeDtypeStruct((count,) + x.shape, x.dtype)] * 2,
         in_specs=[pl.BlockSpec(memory_space=VMEM)],
-        out_specs=pl.BlockSpec(memory_space=pl.ANY),
+        out_specs=[pl.BlockSpec(memory_space=pl.ANY)] * 2,
         scratch_shapes=[sem((1,))] + [sem((marks,))] * 2 + [sem((2 * marks,))] * 4 + [sem((4 * marks,))] * 2,
         compiler_params=pltpu.CompilerParams(collective_id=collective_id, has_side_effects=True),
     )(x)
@@ -652,6 +654,25 @@
         )
         for h in range(cuts)
     )
+
+
+def turned_kernel(l_ref, r_ref, o_ref):
+    o_ref[...] = contract(l_ref[...], r_ref[...], 0, 0).astype(BF)
+
+
+def turned_product(left, right, block):
+    depth, rows = left.shape
+    width = right.shape[1]
+    return pl.pallas_call(
+        turned_kernel,
+        grid=(rows // block,),
+        out_shape=jax.ShapeDtypeStruct((rows, width), BF),
+        in_specs=[
+            pl.BlockSpec((depth, block), lambda i: (0, i)),
+            pl.BlockSpec((depth, width), lambda i: (0, 0)),
+        ],
+        out_specs=pl.BlockSpec((block, width), lambda i: (i, 0)),
+    )(left, right)
 
 
 def visible_rows(kind, run_devs, rows_dev, half, q):
@@ -1054,7 +1075,7 @@
     grad_pairs = grad_pairs.reshape(2 * width, MB * key_rows)
     weight_grad = place_product(weight_grad, grad_query, hidden_one, 0, columns)
     weight_grad = place_product(weight_grad, grad_pairs, hidden_sel, width, columns)
-    low_sel = contract(grad_pairs, w_kv, 0, 0).astype(BF).reshape(MB, key_rows, width)
+    low_sel = turned_product(grad_pairs, w_kv, 2 * 2 * rows_dev).reshape(MB, key_rows, width)
     weight_sum = lax.psum_scatter(
         weight_grad.reshape(all_count, -1, width), ("dp", "seq"), scatter_dimension=0, tiled=True
     )[0].astype(F32)
@@ -1070,7 +1091,7 @@
     if group_count == 2:
         head_own = contract(head_rows, logit_grads[0], 0, 0)
         pad_rows = 8
-        all_rows = exchange(
+        own_grads, other_grads = exchange(
             jnp.concatenate(
                 [grad_one + grad_first, norm_rows, jnp.zeros((pad_rows - 6, width), F32)]
             ).astype(BF),
@@ -1078,20 +1099,17 @@
         )
         other_slots = lax.ppermute(row_slots, "dp", moved)
         embed_sum = lax.optimization_barrier(head_own + head_other.astype(F32))
-        for part in range(group_count):
-            part_slots = jnp.where(group_rank == part, row_slots, other_slots)
+        norm_all = 0.0
+        for grads, part_slots in ((own_grads, row_slots), (other_grads, other_slots)):
             part_slots = jnp.pad(
                 part_slots.reshape(seq_count, own_rows), ((0, 0), (0, pad_rows)), constant_values=-1
             ).reshape(-1)
             embed_sum = embed_sum + contract(
-                all_rows[part].reshape(-1, width), hits(part_slots, 0).astype(BF), 0, 0
+                grads.reshape(-1, width), hits(part_slots, 0).astype(BF), 0, 0
             )
-        norm_all = jnp.sum(
-            all_rows.reshape(all_count, own_rows + pad_rows, width)[
-                :, own_rows : own_rows + 6
-            ].astype(F32),
-            axis=0,
-        )
+            norm_all = norm_all + jnp.sum(
+                grads[:, own_rows : own_rows + 6].astype(F32), axis=0
+            )
     else:
         row_grads, norm_grads = spread(
             [

time: 1030 us -> 1010 us (0.981)
  Pallas kernels: 604 us -> 630 us
  matrix products: 203 us -> 181 us
  local copies, waits for them, and re-layouts: 41.7 us -> 25 us
    dot_general x18 -> x17, matrix products: 202 us -> 180 us  [contract(): lax.dot_general(left, right, (((left_dim,), (right_dim,)), ((), ())), pre...]
    pallas_call x1 -> x2, Pallas kernels: 139 us -> 161 us  [the longest x1 136 us: exchange(): pl.pallas_call(exchange_kernel, out_shape=[jax.ShapeDtypeStruct((count,)...]
    convert_element_type x1 -> x0, local copies, waits for them, and re-layouts: 10.6 us -> none  [on_device(): contract(grad_pairs, w_kv, 0, 0).astype(BF).reshape(MB, key_rows, width)]
  transfers between devices with their start and end apart: 6 -> 6, of which waited for: 2 -> 2; matrix products, arithmetic and copies ran while one was open for 16% -> 13% of each run, Pallas kernels for 47% -> 50%
where the time goes in v5:
time: 1010 us; the launch traced here: 1000 us
  Pallas kernels  630 us (62%)
  matrix products  181 us (18%)
  other arithmetic  71.6 us (7%)
  waiting for transfers between devices  68.4 us (7%)
  local copies, waits for them, and re-layouts  25 us (2%)
  between operations  19.1 us (2%)
    pallas_call x3, Pallas kernels, fold(): pl.pallas_call(functools.partial(fold_kernel, (len(arrays), len(out_shape...  195 us
    dot_general x17, matrix products, contract(): lax.dot_general(left, right, (((left_dim,), (right_dim,)), ((), ())), pre...  180 us
    pallas_call x1, Pallas kernels, exchange(): pl.pallas_call(exchange_kernel, out_shape=[jax.ShapeDtypeStruct((count,)...  136 us
    pallas_call x2, Pallas kernels, spread(): pl.pallas_call(functools.partial(spread_kernel, (len(blocks), len(out_sha...  72.7 us
    ppermute x1, waiting for transfers between devices, on_device(): lax.ppermute(slab_t[0], 'dp', [(i, (i - step) % group_count) for i in ran...  65.1 us
    pallas_call x2, Pallas kernels, lookup(): pl.pallas_call(lookup_kernel, grid=(slots.shape[0] // block,), out_shape=...  51.4 us
    pallas_call x5, Pallas kernels, place_product(): pl.pallas_call(place_kernel, grid=(left.shape[0] // block,), out_shape=ja...  47.7 us
    pallas_call x1, Pallas kernels, attend_back(): pl.pallas_call(attend_back_kernel, grid=(q.shape[1] // rows, HEADS), out_...  39.6 us
  transfers between devices with their start and end apart: 6, of which 2 were waited for; matrix products, arithmetic and copies ran while one was open for 13% of the time, Pallas kernels for 50%

profile of v5, /device:TPU:0, one launch (start us, length us, event | category | flops | bytes accessed | tf_op | source)
XLA Modules:
  0.0 1000.5 jit_solution(3638932736225983048)
XLA Ops:
  23.0 9.7 shard_map.263
  36.6 25.6 %shard_map.264.refs_0_ = bf16[4096,1088]{1,0:T(8,128)(2,1)} custom-call(s32[1]{0:T(128)} %bitcast.8.first_ref, s32[4096,1]{1,0:T(8,128)} %bitcast.277, bf16[1088,1572]{1,0:T(8,128)(2,1)} %bitcast_convert_fusion.table_ref), custom_call_target="tpu_custom_call" | custom-call | tf_op jit(solution)/shard_map/pallas_call | solution.py:819
  62.3 65.1 %collective-permute-done.1.table_ref = bf16[1088,1572]{1,0:T(8,128)(2,1)} collective-permute-done((bf16[1088,1572]{1,0:T(8,128)(2,1)}, bf16[1088,1572]{1,0:T(8,128)(2,1)}, u32[]{:S(2)}, u32[]{:S(2)}) %collective-permute-start.1) | collective-permute-done | bytes 3420704 | tf_op jit(solution)/shard_map/ppermute | solution.py:894
  127.4 25.8 %shard_map.265 = bf16[4096,1088]{1,0:T(8,128)(2,1)} custom-call(s32[1]{0:T(128)} %bitcast.3.first_ref, s32[4096,1]{1,0:T(8,128)} %bitcast.278, bf16[1088,1572]{1,0:T(8,128)(2,1)} %collective-permute-done.1.table_ref, bf16[4096,1088]{1,0:T(8,128)(2,1)} %shard_map.264.refs_0_), custom_call_target="tpu_custom_call" | custom-call | tf_op jit(solution)/shard_map/pallas_call | solution.py:819
  153.2 86.3 %shard_map.266 = f32[256,1088]{1,0:T(8,128)} custom-call(bf16[16,256,1088]{2,1,0:T(8,128)(2,1)} %bitcast.273), custom_call_target="tpu_custom_call" | custom-call | tf_op jit(solution)/shard_map/pallas_call | solution.py:448
  244.8 48.2 %shard_map.267 = bf16[2,1536,1088]{2,1,0:T(8,128)(2,1)} custom-call(bf16[2,2,64,1088]{3,2,1,0:T(8,128)(2,1)} %bitcast.283), custom_call_target="tpu_custom_call" | custom-call | tf_op jit(solution)/shard_map/pallas_call | solution.py:285
  296.6 23.4 %convolution_convert_fusion = bf16[3072,2176]{0,1:T(8,128)(2,1)} fusion(bf16[3072,1088]{1,0:T(8,128)(2,1)} %bitcast.274, bf16[13056,1088]{1,0:T(8,128)(2,1)} %all-gather.3.cloned.1.call-done), kind=kOutput, calls=%fused_computation.5 | convolution fusion | flops 14552530944 | bytes 25460736 | tf_op jit(solution)/shard_map/dot_general | solution.py:736
  320.1 34.5 %shard_map.268.l_ref = bf16[1088,256]{1,0:T(8,128)(2,1)} custom-call(s32[128,1]{1,0:T(8,128)} %copy.165.pos_ref, bf16[1088,256]{1,0:T(8,128)(2,1)} %fusion.47.q_ref, bf16[2,1088,3072]{2,1,0:T(8,128)(2,1)} %bitcast.271), custom_call_target="tpu_custom_call" | custom-call | tf_op jit(solution)/shard_map/pallas_call | solution.py:786
  358.2 16.2 %fusion.22 = (bf16[4352,256]{1,0:T(8,128)(2,1)S(1)}, f32[4352,256]{1,0:T(8,128)}, f32[256,4352]{0,1:T(8,128)}) fusion(bf16[256,1088]{1,0:T(8,128)(2,1)S(1)} %add_convert_fusion.2.r_ref, bf16[13056,1088]{1,0:T(8,128)(2,1)} %all-gather.3.cloned.1.call-done), kind=kOutput, calls=%fused_computation.48 | convolution fusion | flops 2496724992 | bytes 21725184 | tf_op jit(solution)/shard_map/dot_general | solution.py:736
  374.4 7.9 fusion.96
  383.7 24.4 %shard_map.269 = bf16[16,64,1088]{2,1,0:T(8,128)(2,1)} custom-call(bf16[64,1088]{1,0:T(8,128)(2,1)} %bitcast.292), custom_call_target="tpu_custom_call" | custom-call | tf_op jit(solution)/shard_map/pallas_call | solution.py:285
  408.2 7.3 fusion.97
  415.5 8.7 fusion.98
  428.7 8.4 shard_map.270
  440.2 10.0 %convolution_convert_fusion.1 = bf16[1088,1572]{1,0:T(8,128)(2,1)} fusion(bf16[1024,1088]{1,0:T(8,128)(2,1)} %bitcast.286, f32[1024,1572]{0,1:T(8,128)} %copy-done.6, f32[1024]{0:T(1024)S(1)} %get-tuple-element.78, f32[1024]{0:T(1024)S(1)} %mul.452, s32[1024]{0:T(1024)S(1)} %sub.227), kind=kOutput, calls=%fused_computation.19 | convolution fusion | flops 3514136832 | bytes 12100096 | tf_op jit(solution)/shard_map/dot_general | solution.py:736
  450.3 8.1 fusion.86
  458.3 7.8 fusion.43
  470.5 24.9 %shard_map.271 = f32[64,1088]{1,0:T(8,128)} custom-call(bf16[16,64,1088]{2,1,0:T(8,128)(2,1)} %bitcast.279), custom_call_target="tpu_custom_call" | custom-call | tf_op jit(solution)/shard_map/pallas_call | solution.py:448
  500.7 9.0 shard_map.276.refs_0_
  509.7 10.6 %fusion.28.l_ref = bf16[4352,256]{1,0:T(8,128)(2,1)S(1)} fusion(f32[4352,256]{1,0:T(8,128)} %get-tuple-element.80, bf16[256,1088]{1,0:T(8,128)(2,1)S(1)} %copy-done.14, bf16[13056,1088]{1,0:T(8,128)(2,1)} %all-gather.3.cloned.1.call-done, f32[256,4352]{0,1:T(8,128)} %get-tuple-element.97), kind=kOutput, calls=%fused_computation.54 | convolution fusion | flops 2439905280 | bytes 21725184 | tf_op jit(solution)/shard_map/dot_general | solution.py:736
  520.3 9.6 fusion.99
  538.5 39.6 %shard_map.272 = (bf16[1088,256]{1,0:T(8,128)(2,1)}, bf16[2,1088,3072]{2,1,0:T(8,128)(2,1)}) custom-call(s32[128,1]{1,0:T(8,128)} %copy.165.pos_ref, bf16[1088,256]{1,0:T(8,128)(2,1)} %fusion.47.q_ref, bf16[2,1088,3072]{2,1,0:T(8,128)(2,1)} %bitcast.272, bf16[1088,256]{1,0:T(8,128)(2,1)} %fusion.48.g_ref), custom_call_target="tpu_custom_call" | custom-call | tf_op jit(solution)/shard_map/pallas_call | solution.py:799
  578.1 9.0 shard_map.277.refs_0_
  593.8 23.0 %shard_map.280 = bf16[13056,1088]{1,0:T(8,128)(2,1)} custom-call(bf16[2176,3072]{1,0:T(8,128)(2,1)} %bitcast.269, bf16[3072,1088]{1,0:T(8,128)(2,1)} %bitcast.275, bf16[13056,1088]{1,0:T(8,128)(2,1)} %shard_map.279.refs_0_), custom_call_target="tpu_custom_call", output_to_operand_aliasing={{}: (2, {})} | custom-call | tf_op jit(solution)/shard_map/pallas_call | solution.py:721
  627.2 25.4 %shard_map.273 = bf16[3072,1088]{1,0:T(8,128)(2,1)} custom-call(bf16[2176,3072]{1,0:T(8,128)(2,1)} %bitcast.270, bf16[2176,1088]{1,0:T(8,128)(2,1)} %slice.125.r_ref), custom_call_target="tpu_custom_call" | custom-call | tf_op jit(solution)/shard_map/pallas_call | solution.py:666
  652.6 83.4 %shard_map.274 = f32[2,2,64,1088]{3,2,1,0:T(8,128)} custom-call(bf16[2,1536,1088]{2,1,0:T(8,128)(2,1)} %bitcast.276), custom_call_target="tpu_custom_call" | custom-call | tf_op jit(solution)/shard_map/pallas_call | solution.py:448
  736.6 7.7 fusion.85
  756.7 135.5 %shard_map.275 = (bf16[16,264,1088]{2,1,0:T(8,128)(2,1)}, bf16[16,264,1088]{2,1,0:T(8,128)(2,1)}) custom-call(bf16[264,1088]{1,0:T(8,128)(2,1)} %concatenate.45.x_ref), custom_call_target="tpu_custom_call" | custom-call | tf_op jit(solution)/shard_map/pallas_call | solution.py:624
  895.0 24.4 %fusion.5 = f32[1088,1572]{1,0:T(8,128)} fusion(f32[1088,1572]{1,0:T(8,128)} %convert_add_fusion, bf16[4224,1088]{1,0:T(8,128)(2,1)} %bitcast.306, s32[4224]{0:T(1024)S(1)} %sub.251), kind=kOutput, calls=%fused_computation.10 | convolution fusion | flops 14457268224 | bytes 22891008 | tf_op jit(solution)/shard_map/dot_general | solution.py:736
  919.5 24.6 %multiply_reduce_fusion = (f32[]{:T(128)}, f32[1088,1572]{1,0:T(8,128)}) fusion(f32[1088,1572]{1,0:T(8,128)} %fusion.5, bf16[4224,1088]{1,0:T(8,128)(2,1)S(1)} %bitcast.305, s32[4224]{0:T(1024)S(1)} %sub.253), kind=kOutput, calls=%fused_computation.27 | convolution fusion | flops 14460688384 | bytes 22891012 | tf_op jit(solution)/shard_map/dot_general | solution.py:736
  948.9 10.9 %shard_map.281 = f32[32,8,128]{2,1,0:T(8,128)} custom-call(f32[8,128]{1,0:T(8,128)} %broadcast_select_fusion.x_ref), custom_call_target="tpu_custom_call" | custom-call | tf_op jit(solution)/shard_map/pallas_call | solution.py:95
  964.2 21.6 %convert_bitcast_fusion = (bf16[1572,1088]{0,1:T(8,128)(2,1)}, f32[1088,1572]{1,0:T(8,128)}, f32[1572,1088]{0,1:T(8,128)}, f32[1572,1088]{0,1:T(8,128)}) fusion(f32[1572,1088]{0,1:T(8,128)} %param.25, f32[1088,1572]{1,0:T(8,128)} %get-tuple-element.108, f32[]{:T(128)S(6)} %min.3, f32[1572,1088]{0,1:T(8,128)} %param.24, f32[1572,1088]{0,1:T(8,128)} %param.23), kind=kLoop, calls=%fused_computation.69 | loop fusion | flops 29075712 | bytes 51310084 | tf_op jit(solution)/shard_map/transpose | solution.py:1181
  (231 shorter events, 104.8 us)
Async XLA Ops:
  7.2 11.6 %copy-start = (s32[50304]{0:T(1024)S(1)}, s32[50304]{0:T(1024)}, u32[]{:S(2)}) copy-start(s32[50304]{0:T(1024)} %param.22) | copy-start | bytes 603652
  7.2 286.0 %all-gather.3.cloned.1.call-start = ((), (), s32[]{:S(2)}) async-start(), calls=%async_computation.1 | async-start | bytes 31021056 | tf_op jit(solution)/shard_map/all_gather | solution.py:898
  9.9 8.7 copy-start.33
  9.9 12.0 %copy-start.37 = (f32[2,2,2]{2,1,0:T(2,128)S(1)}, f32[2,2,2]{2,1,0:T(2,128)}, u32[]{:S(2)}) copy-start(f32[2,2,2]{2,1,0:T(2,128)} %param.21) | copy-start | bytes 100
  9.9 12.0 %copy-start.38 = (s32[2,2,2]{2,1,0:T(2,128)S(1)}, s32[2,2,2]{2,1,0:T(2,128)}, u32[]{:S(2)}) copy-start(s32[2,2,2]{2,1,0:T(2,128)} %param.20) | copy-start | bytes 100
  9.9 12.0 %copy-start.39 = (s32[2,2,2]{2,1,0:T(2,128)S(1)}, s32[2,2,2]{2,1,0:T(2,128)}, u32[]{:S(2)}) copy-start(s32[2,2,2]{2,1,0:T(2,128)} %param.19) | copy-start | bytes 100
  9.9 12.2 %copy-start.29 = (f32[204]{0:T(256)S(1)}, f32[204]{0:T(256)}, u32[]{:S(2)}) copy-start(f32[204]{0:T(256)} %param.29) | copy-start | bytes 2452
  9.9 934.1 %reduce-scatter.4.cloned.1.call-start = ((), (), s32[]{:S(2)}) async-start(), calls=%async_computation.2 | async-start | bytes 31021056
  10.0 8.3 collective-permute-start
  18.3 109.1 %collective-permute-start.1 = (bf16[1088,1572]{1,0:T(8,128)(2,1)}, bf16[1088,1572]{1,0:T(8,128)(2,1)}, u32[]{:S(2)}, u32[]{:S(2)}) collective-permute-start(bf16[1088,1572]{1,0:T(8,128)(2,1)} %bitcast_convert_fusion.table_ref), channel_id=1, source_target_pairs={{0,16},{16,0},{1,17},{17,1},{2,18},{18,2},{3,19},{19,3},{4,20},{20... | collective-permute-start | bytes 10262024 | tf_op jit(solution)/shard_map/ppermute | solution.py:894
  33.8 28.3 %copy-start.19 = (s32[16,320]{1,0:T(8,128)}, s32[16,320]{1,0:T(8,128)S(1)}, u32[]{:S(2)}) copy-start(s32[16,320]{1,0:T(8,128)S(1)} %slice_convert_fusion.1) | copy-start | bytes 61444
  62.2 180.2 %copy-start.21 = (f32[1088]{0:T(1024)}, f32[1088]{0:T(1024)S(1)}, u32[]{:S(2)}) copy-start(f32[1088]{0:T(1024)S(1)} %get-tuple-element.58) | copy-start | bytes 13060
  240.9 52.2 %copy-start.23 = (f32[256]{0:T(256)}, f32[256]{0:T(256)S(1)}, u32[]{:S(2)}) copy-start(f32[256]{0:T(256)S(1)} %broadcast_multiply_fusion.8) | copy-start | bytes 3076
  242.5 50.7 %copy-start.26 = (f32[256]{0:T(256)}, f32[256]{0:T(256)S(1)}, u32[]{:S(2)}) copy-start(f32[256]{0:T(256)S(1)} %add_rsqrt_fusion.2) | copy-start | bytes 3076
  244.8 48.3 %copy-start.7 = (bf16[256,1088]{1,0:T(8,128)(2,1)S(1)}, bf16[256,1088]{1,0:T(8,128)(2,1)}, u32[]{:S(2)}) copy-start(bf16[256,1088]{1,0:T(8,128)(2,1)} %add_convert_fusion.3.r_ref) | copy-start | bytes 1671172
  320.1 34.5 %copy-start.2 = (f32[256,1088]{1,0:T(8,128)S(1)}, f32[256,1088]{1,0:T(8,128)}, u32[]{:S(2)}) copy-start(f32[256,1088]{1,0:T(8,128)} %shard_map.266) | copy-start | bytes 3342340
  358.2 16.2 %copy-start.11 = (bf16[256,1088]{1,0:T(8,128)(2,1)}, bf16[256,1088]{1,0:T(8,128)(2,1)S(1)}, u32[]{:S(2)}) copy-start(bf16[256,1088]{1,0:T(8,128)(2,1)S(1)} %add_convert_fusion.2.r_ref) | copy-start | bytes 1671172
  415.4 8.8 copy-start.5
  440.2 18.1 %slice-start = ((s8[6455296]{0:T(1024)(128)(4,1)}), s8[4194304]{0:T(1024)(128)(4,1)S(1)}, s32[]{:S(2)}) async-start(s8[6455296]{0:T(1024)(128)(4,1)} %bitcast.281), calls=%async_computation.3 | async-start | bytes 8388608
  497.6 93.0 %collective-permute-start.2 = (bf16[1088,1572]{1,0:T(8,128)(2,1)}, bf16[1088,1572]{1,0:T(8,128)(2,1)}, u32[]{:S(2)}, u32[]{:S(2)}) collective-permute-start(bf16[1088,1572]{1,0:T(8,128)(2,1)} %convolution_convert_fusion.1), channel_id=1, source_target_pairs={{0,16},{16,0},{1,17},{17,1},{2,18},{18,2},{3,19},{19,3},{4,20},{20... | collective-permute-start | bytes 10262024 | tf_op jit(solution)/shard_map/ppermute | solution.py:1045
  500.7 9.0 copy-start.14
  520.3 9.6 copy-start.17
  534.9 43.2 %copy-start.15 = (bf16[256,1088]{1,0:T(8,128)(2,1)}, bf16[256,1088]{1,0:T(8,128)(2,1)S(1)}, u32[]{:S(2)}) copy-start(bf16[256,1088]{1,0:T(8,128)(2,1)S(1)} %get-tuple-element.73.r_ref) | copy-start | bytes 1671172
  617.5 3.8 collective-permute-start.3
  652.5 84.0 %copy-start.13 = (bf16[16,64,1088]{2,1,0:T(8,128)(2,1)S(1)}, bf16[16,64,1088]{2,1,0:T(8,128)(2,1)}, u32[]{:S(2)}) copy-start(bf16[16,64,1088]{2,1,0:T(8,128)(2,1)} %shard_map.269) | copy-start | bytes 6684676
  895.0 24.4 %copy-start.28 = (bf16[16,264,1088]{2,1,0:T(8,128)(2,1)S(1)}, bf16[16,264,1088]{2,1,0:T(8,128)(2,1)}, u32[]{:S(2)}) copy-start(bf16[16,264,1088]{2,1,0:T(8,128)(2,1)} %get-tuple-element.35) | copy-start | bytes 27574276
  919.4 44.1 %copy-start.30 = (f32[204]{0:T(256)S(1)}, f32[204]{0:T(256)}, u32[]{:S(2)}) copy-start(f32[204]{0:T(256)} %param.29) | copy-start | bytes 2452
  919.4 44.1 %copy-start.34 = (f32[204]{0:T(256)S(1)}, f32[204]{0:T(256)}, u32[]{:S(2)}) copy-start(f32[204]{0:T(256)} %param.30) | copy-start | bytes 2452
  919.4 44.1 %copy-start.35 = (f32[204]{0:T(256)S(1)}, f32[204]{0:T(256)}, u32[]{:S(2)}) copy-start(f32[204]{0:T(256)} %param.31) | copy-start | bytes 2452
  964.2 21.6 %copy-start.4 = (f32[1088,408]{0,1:T(8,128)S(1)}, f32[1088,408]{0,1:T(8,128)}, u32[]{:S(2)}) copy-start(f32[1088,408]{0,1:T(8,128)} %param.26) | copy-start | bytes 5326852
  964.2 21.6 %copy-start.10 = (bf16[1,408,1088]{2,1,0:T(8,128)(2,1)S(1)}, bf16[1,408,1088]{2,1,0:T(8,128)(2,1)}, u32[]{:S(2)}) copy-start(bf16[1,408,1088]{2,1,0:T(8,128)(2,1)} %reduce-scatter.4.cloned.1.call-done) | copy-start | bytes 2663428
  964.2 28.1 %copy-start.1 = (s32[50304]{0:T(1024)S(1)}, s32[50304]{0:T(1024)}, u32[]{:S(2)}) copy-start(s32[50304]{0:T(1024)} %param.22) | copy-start | bytes 603652
  (16 other events, 92.4 us)
Sparse Core Ops, SparseCore 0:
  11.4 215.6 all-gather.2
  617.0 327.0 reduce-scatter.3

commit v6 on v5

--- a/solution.py
+++ b/solution.py
@@ -457,6 +457,149 @@
     )(*arrays)
 
 
+def settle_kernel(parts, count, *refs):
+    given, wanted, pieces = parts
+    total = len(pieces)
+    spans = [piece[0] for piece in pieces]
+    x_refs, o_refs = refs[:given], refs[given : given + wanted]
+    scratch = refs[given + wanted :]
+    outs = [piece[3](o_refs) for piece in pieces]
+    c_bufs, u_bufs, d_bufs, t_bufs, s_bufs, b_bufs = (
+        scratch[i * total : (i + 1) * total] for i in range(6)
+    )
+    c_send, c_recv, u_send, u_recv, d_send, d_recv, b_send, b_recv = scratch[6 * total :]
+    line = count // 4
+    group = lax.axis_index("dp")
+    at, side, core = place(lax.axis_index("seq"))
+    peers = line_peers(at, side, core, group, line)
+    below, above, beside, sibling = (peer for _, peer in peers)
+    meet(peers)
+
+    def remote(src, dst, send, recv, peer):
+        return pltpu.make_async_remote_copy(
+            src_ref=src, dst_ref=dst, send_sem=send, recv_sem=recv, device_id=peer, device_id_type=MESH
+        )
+
+    def view(part, where, other, which_core):
+        which = 1 - side if other else side
+        return pieces[part][2](x_refs, 4 * where + 2 * which + which_core)
+
+    def slot(part, where):
+        return lax.rem(where, spans[part])
+
+    def index_of(part, where, other):
+        return 2 * slot(part, where) + other
+
+    order = []
+    for far in range(line - 1, 0, -1):
+        order += [(far, 1), (far, -1)]
+    order.append((0, 1))
+
+    def c_copy(part, where, other):
+        index = index_of(part, where, other)
+        return remote(
+            view(part, where, other, 1 - core),
+            c_bufs[part].at[index],
+            c_send.at[part, index],
+            c_recv.at[part, index],
+            sibling,
+        )
+
+    def u_copy(part, where, other):
+        index = index_of(part, where, other)
+        return remote(
+            t_bufs[part].at[index], u_bufs[part].at[index], u_send.at[part, index], u_recv.at[part, index], above
+        )
+
+    def d_copy(part, where, other):
+        index = index_of(part, where, other)
+        return remote(
+            t_bufs[part].at[index], d_bufs[part].at[index], d_send.at[part, index], d_recv.at[part, index], below
+        )
+
+    def b_copy(part):
+        return remote(s_bufs[part], b_bufs[part], b_send.at[part], b_recv.at[part], beside)
+
+    def each(action):
+        for far, sign in order:
+            for part in range(total):
+                if far >= spans[part]:
+                    continue
+                where = at + sign * far
+                low = at // spans[part] * spans[part]
+
+                @pl.when((where >= low) & (where < low + spans[part]))
+                def _():
+                    for other in (1, 0):
+                        action(part, where, far, sign, other)
+
+    each(lambda part, where, far, sign, other: c_copy(part, where, other).start())
+
+    def along(part, where, far, sign, other):
+        c_copy(part, where, other).wait_recv()
+        index = index_of(part, where, other)
+        here = slot(part, at)
+        value = view(part, where, other, core)[...].astype(F32) + c_bufs[part][index].astype(F32)
+        goal = outs[part] if far == 0 and not other else t_bufs[part].at[index]
+        kind = F32 if far == 0 and not other else BF
+        goal[...] = value.astype(kind)
+        if far == 0 or sign > 0:
+
+            @pl.when(here > 0)
+            def _():
+                u_copy(part, where, other).wait_recv()
+                goal[...] = (goal[...].astype(F32) + u_bufs[part][index].astype(F32)).astype(kind)
+
+        if far == 0 or sign < 0:
+
+            @pl.when(here < spans[part] - 1)
+            def _():
+                d_copy(part, where, other).wait_recv()
+                goal[...] = (goal[...].astype(F32) + d_bufs[part][index].astype(F32)).astype(kind)
+
+        if far > 0:
+            (u_copy if sign > 0 else d_copy)(part, where, other).start()
+        elif other:
+            s_bufs[part][...] = goal[...]
+            b_copy(part).start()
+
+    each(along)
+    for part in range(total):
+        b_copy(part).wait_recv()
+        outs[part][...] += b_bufs[part][...].astype(F32)
+
+    def finish(part, where, far, sign, other):
+        c_copy(part, where, other).wait_send()
+        if far > 0:
+            (u_copy if sign > 0 else d_copy)(part, where, other).wait_send()
+
+    each(finish)
+    for part in range(total):
+        b_copy(part).wait_send()
+
+
+def settle(arrays, out_shapes, pieces, collective_id):
+    count = lax.axis_size("seq")
+    total = len(pieces)
+    sem = pltpu.SemaphoreType.DMA
+    line = count // 4
+    bufs = []
+    for _ in range(4):
+        bufs += [VMEM((2 * piece[0],) + piece[1], BF) for piece in pieces]
+    for _ in range(2):
+        bufs += [VMEM(piece[1], BF) for piece in pieces]
+    return pl.pallas_call(
+        functools.partial(settle_kernel, (len(arrays), len(out_shapes), pieces), count),
+        out_shape=[jax.ShapeDtypeStruct(shape, F32) for shape in out_shapes],
+        in_specs=[pl.BlockSpec(memory_space=VMEM)] * len(arrays),
+        out_specs=[pl.BlockSpec(memory_space=VMEM)] * len(out_shapes),
+        scratch_shapes=bufs + [sem((total, 2 * line))] * 6 + [sem((total,))] * 2,
+        compiler_params=pltpu.CompilerParams(
+            collective_id=collective_id, has_side_effects=True, vmem_limit_bytes=60 * 2**20
+        ),
+    )(*arrays)
+
+
 def exchange_kernel(x_ref, own_ref, other_ref, own_sem, z_send, z_recv, x_send, x_recv, y_send, y_recv, c_send, c_recv):
     count = own_ref.shape[0]
     line = count // 4
@@ -518,9 +661,6 @@
         index = 4 * number(item) + 2 * other_group + other_side
         return remote(src, dst, c_send, c_recv, index, sibling)
 
-    def by_side(item):
-        return lax.rem(where_of(item), 2) == 0
-
     def z_links(item, act):
         far, turn = item
         if far + 1 < line:
@@ -557,23 +697,10 @@
         core_copy(item, 1, 0, False).start()
 
     def diagonal(item):
-        @pl.when(by_side(item))
-        def _():
-            side_copy(item, 1, False).start()
-
-        @pl.when(jnp.logical_not(by_side(item)))
-        def _():
-            cross_copy(item, 1, False).start()
+        side_copy(item, 1, False).start()
 
     def third(item):
-        @pl.when(by_side(item))
-        def _():
-            side_copy(item, 1, True).wait_recv()
-
-        @pl.when(jnp.logical_not(by_side(item)))
-        def _():
-            cross_copy(item, 1, True).wait_recv()
-
+        side_copy(item, 1, True).wait_recv()
         core_copy(item, 1, 1, False).start()
 
     def at_far(far):
@@ -600,14 +727,7 @@
         side_copy(item, 0, False).wait_send()
         cross_copy(item, 0, False).wait_send()
 
-        @pl.when(by_side(item))
-        def _():
-            side_copy(item, 1, False).wait_send()
-
-        @pl.when(jnp.logical_not(by_side(item)))
-        def _():
-            cross_copy(item, 1, False).wait_send()
-
+        side_copy(item, 1, False).wait_send()
         for other_group in range(2):
             for other_side in range(2):
                 core_copy(item, other_group, other_side, False).wait_send()
@@ -656,23 +776,27 @@
     )
 
 
-def turned_kernel(l_ref, r_ref, o_ref):
-    o_ref[...] = contract(l_ref[...], r_ref[...], 0, 0).astype(BF)
-
-
-def turned_product(left, right, block):
+def turned_kernel(l_ref, k_ref, v_ref, o_ref):
+    width = k_ref.shape[0]
+    o_ref[...] = (
+        contract(l_ref[:width], k_ref[...], 0, 0) + contract(l_ref[width:], v_ref[...], 0, 0)
+    ).astype(BF)
+
+
+def turned_product(left, weights, block):
     depth, rows = left.shape
-    width = right.shape[1]
+    width = weights.shape[1]
     return pl.pallas_call(
         turned_kernel,
         grid=(rows // block,),
         out_shape=jax.ShapeDtypeStruct((rows, width), BF),
         in_specs=[
             pl.BlockSpec((depth, block), lambda i: (0, i)),
-            pl.BlockSpec((depth, width), lambda i: (0, 0)),
+            pl.BlockSpec((width, width), lambda i: (1, 0)),
+            pl.BlockSpec((width, width), lambda i: (2, 0)),
         ],
         out_specs=pl.BlockSpec((block, width), lambda i: (i, 0)),
-    )(left, right)
+    )(left, weights, weights)
 
 
 def visible_rows(kind, run_devs, rows_dev, half, q):
@@ -1075,11 +1199,11 @@
     grad_pairs = grad_pairs.reshape(2 * width, MB * key_rows)
     weight_grad = place_product(weight_grad, grad_query, hidden_one, 0, columns)
     weight_grad = place_product(weight_grad, grad_pairs, hidden_sel, width, columns)
-    low_sel = turned_product(grad_pairs, w_kv, 2 * 2 * rows_dev).reshape(MB, key_rows, width)
+    low_sel = turned_product(grad_pairs, weights, 2 * 2 * rows_dev).reshape(MB, key_rows, width)
     weight_sum = lax.psum_scatter(
         weight_grad.reshape(all_count, -1, width), ("dp", "seq"), scatter_dimension=0, tiled=True
     )[0].astype(F32)
-    (low_own,) = fold(
+    (low_own,) = settle(
         [low_sel],
         [(MB, 2, rows_dev, width)],
         visible_sum(line, run_devs, rows_dev, half, width),

time: 1010 us -> 1050 us (1.040)
  Pallas kernels: 630 us -> 676 us
    pallas_call x0 -> x1, Pallas kernels: none -> 97.3 us  [settle(): pl.pallas_call(functools.partial(settle_kernel, (len(arrays), len(out_sha...]
    pallas_call x3 -> x2, Pallas kernels: 195 us -> 111 us  [fold(): pl.pallas_call(functools.partial(fold_kernel, (len(arrays), len(out_shape...]
    pallas_call x1, Pallas kernels: 136 us -> 164 us  [exchange(): pl.pallas_call(exchange_kernel, out_shape=[jax.ShapeDtypeStruct((count,)...]
  transfers between devices with their start and end apart: 6 -> 6, of which waited for: 2 -> 2; matrix products, arithmetic and copies ran while one was open for 13% -> 12% of each run, Pallas kernels for 50% -> 52%
where the time goes in v6:
time: 1050 us; the launch traced here: 1040 us
  Pallas kernels  676 us (64%)
  matrix products  179 us (17%)
  other arithmetic  74.1 us (7%)
  waiting for transfers between devices  68.3 us (7%)
  local copies, waits for them, and re-layouts  19.5 us (2%)
  between operations  19.2 us (2%)
    dot_general x17, matrix products, contract(): lax.dot_general(left, right, (((left_dim,), (right_dim,)), ((), ())), pre...  178 us
    pallas_call x1, Pallas kernels, exchange(): pl.pallas_call(exchange_kernel, out_shape=[jax.ShapeDtypeStruct((count,)...  164 us
    pallas_call x2, Pallas kernels, fold(): pl.pallas_call(functools.partial(fold_kernel, (len(arrays), len(out_shape...  111 us
    pallas_call x1, Pallas kernels, settle(): pl.pallas_call(functools.partial(settle_kernel, (len(arrays), len(out_sha...  97.3 us
    pallas_call x2, Pallas kernels, spread(): pl.pallas_call(functools.partial(spread_kernel, (len(blocks), len(out_sha...  72.7 us
    ppermute x1, waiting for transfers between devices, on_device(): lax.ppermute(slab_t[0], 'dp', [(i, (i - step) % group_count) for i in ran...  65.2 us
    pallas_call x2, Pallas kernels, lookup(): pl.pallas_call(lookup_kernel, grid=(slots.shape[0] // block,), out_shape=...  51.4 us
    pallas_call x5, Pallas kernels, place_product(): pl.pallas_call(place_kernel, grid=(left.shape[0] // block,), out_shape=ja...  47.7 us
  transfers between devices with their start and end apart: 6, of which 2 were waited for; matrix products, arithmetic and copies ran while one was open for 12% of the time, Pallas kernels for 52%

profile of v6, /device:TPU:0, one launch (start us, length us, event | category | flops | bytes accessed | tf_op | source)
XLA Modules:
  0.0 1041.2 jit_solution(7943818822638553725)
XLA Ops:
  23.0 9.7 shard_map.263
  36.6 25.6 %shard_map.264.refs_0_ = bf16[4096,1088]{1,0:T(8,128)(2,1)} custom-call(s32[1]{0:T(128)} %bitcast.8.first_ref, s32[4096,1]{1,0:T(8,128)} %bitcast.279, bf16[1088,1572]{1,0:T(8,128)(2,1)} %bitcast_convert_fusion.table_ref), custom_call_target="tpu_custom_call" | custom-call | tf_op jit(solution)/shard_map/pallas_call | solution.py:943
  62.3 65.2 %collective-permute-done.1.table_ref = bf16[1088,1572]{1,0:T(8,128)(2,1)} collective-permute-done((bf16[1088,1572]{1,0:T(8,128)(2,1)}, bf16[1088,1572]{1,0:T(8,128)(2,1)}, u32[]{:S(2)}, u32[]{:S(2)}) %collective-permute-start.1) | collective-permute-done | bytes 3420704 | tf_op jit(solution)/shard_map/ppermute | solution.py:1018
  127.4 25.9 %shard_map.265 = bf16[4096,1088]{1,0:T(8,128)(2,1)} custom-call(s32[1]{0:T(128)} %bitcast.3.first_ref, s32[4096,1]{1,0:T(8,128)} %bitcast.280, bf16[1088,1572]{1,0:T(8,128)(2,1)} %collective-permute-done.1.table_ref, bf16[4096,1088]{1,0:T(8,128)(2,1)} %shard_map.264.refs_0_), custom_call_target="tpu_custom_call" | custom-call | tf_op jit(solution)/shard_map/pallas_call | solution.py:943
  153.3 86.1 %shard_map.266 = f32[256,1088]{1,0:T(8,128)} custom-call(bf16[16,256,1088]{2,1,0:T(8,128)(2,1)} %bitcast.275), custom_call_target="tpu_custom_call" | custom-call | tf_op jit(solution)/shard_map/pallas_call | solution.py:448
  244.8 48.3 %shard_map.267 = bf16[2,1536,1088]{2,1,0:T(8,128)(2,1)} custom-call(bf16[2,2,64,1088]{3,2,1,0:T(8,128)(2,1)} %bitcast.285), custom_call_target="tpu_custom_call" | custom-call | tf_op jit(solution)/shard_map/pallas_call | solution.py:285
  296.6 23.4 %convolution_convert_fusion = bf16[3072,2176]{0,1:T(8,128)(2,1)} fusion(bf16[3072,1088]{1,0:T(8,128)(2,1)} %bitcast.276, bf16[13056,1088]{1,0:T(8,128)(2,1)} %all-gather.3.cloned.1.call-done.k_ref.v_ref), kind=kOutput, calls=%fused_computation.5 | convolution fusion | flops 14552530944 | bytes 25460736 | tf_op jit(solution)/shard_map/dot_general | solution.py:860
  320.0 34.5 %shard_map.268.l_ref = bf16[1088,256]{1,0:T(8,128)(2,1)} custom-call(s32[128,1]{1,0:T(8,128)} %copy.165.pos_ref, bf16[1088,256]{1,0:T(8,128)(2,1)} %fusion.48.q_ref, bf16[2,1088,3072]{2,1,0:T(8,128)(2,1)} %bitcast.273), custom_call_target="tpu_custom_call" | custom-call | tf_op jit(solution)/shard_map/pallas_call | solution.py:910
  358.2 16.8 %fusion.23 = (bf16[4352,256]{1,0:T(8,128)(2,1)}, f32[4352,256]{1,0:T(8,128)}, f32[256,4352]{0,1:T(8,128)}) fusion(bf16[256,1088]{1,0:T(8,128)(2,1)S(1)} %add_convert_fusion.2.r_ref, bf16[13056,1088]{1,0:T(8,128)(2,1)} %all-gather.3.cloned.1.call-done.k_ref.v_ref), kind=kOutput, calls=%fused_computation.49 | convolution fusion | flops 2496724992 | bytes 21725184 | tf_op jit(solution)/shard_map/dot_general | solution.py:860
  384.8 24.4 %shard_map.269 = bf16[16,64,1088]{2,1,0:T(8,128)(2,1)} custom-call(bf16[64,1088]{1,0:T(8,128)(2,1)} %bitcast.294), custom_call_target="tpu_custom_call" | custom-call | tf_op jit(solution)/shard_map/pallas_call | solution.py:285
  409.3 7.3 fusion.97
  416.6 8.7 fusion.98
  429.8 8.4 shard_map.270
  441.3 10.0 convolution_convert_fusion.1
  451.4 8.1 fusion.87
  459.5 7.8 fusion.44
  471.6 25.1 %shard_map.271 = f32[64,1088]{1,0:T(8,128)} custom-call(bf16[16,64,1088]{2,1,0:T(8,128)(2,1)} %bitcast.281), custom_call_target="tpu_custom_call" | custom-call | tf_op jit(solution)/shard_map/pallas_call | solution.py:448
  501.9 9.0 shard_map.276.refs_0_
  510.9 10.6 %fusion.29.l_ref = bf16[4352,256]{1,0:T(8,128)(2,1)S(1)} fusion(f32[4352,256]{1,0:T(8,128)} %get-tuple-element.80, bf16[256,1088]{1,0:T(8,128)(2,1)S(1)} %copy-done.15, bf16[13056,1088]{1,0:T(8,128)(2,1)} %all-gather.3.cloned.1.call-done.k_ref.v_ref, f32[256,4352]{0,1:T(8,128)} %get-tuple-element.97), kind=kOutput, calls=%fused_computation.55 | convolution fusion | flops 2439905280 | bytes 21725184 | tf_op jit(solution)/shard_map/dot_general | solution.py:860
  521.5 9.6 fusion.99
  539.7 39.6 %shard_map.272 = (bf16[1088,256]{1,0:T(8,128)(2,1)}, bf16[2,1088,3072]{2,1,0:T(8,128)(2,1)}) custom-call(s32[128,1]{1,0:T(8,128)} %copy.165.pos_ref, bf16[1088,256]{1,0:T(8,128)(2,1)} %fusion.48.q_ref, bf16[2,1088,3072]{2,1,0:T(8,128)(2,1)} %bitcast.274, bf16[1088,256]{1,0:T(8,128)(2,1)} %fusion.49.g_ref), custom_call_target="tpu_custom_call" | custom-call | tf_op jit(solution)/shard_map/pallas_call | solution.py:923
  579.2 9.0 shard_map.277.refs_0_
  595.0 23.0 %shard_map.280 = bf16[13056,1088]{1,0:T(8,128)(2,1)} custom-call(bf16[2176,3072]{1,0:T(8,128)(2,1)} %bitcast.271, bf16[3072,1088]{1,0:T(8,128)(2,1)} %bitcast.277, bf16[13056,1088]{1,0:T(8,128)(2,1)} %shard_map.279.refs_0_), custom_call_target="tpu_custom_call", output_to_operand_aliasing={{}: (2, {})} | custom-call | tf_op jit(solution)/shard_map/pallas_call | solution.py:845
  622.8 26.7 %shard_map.273 = bf16[3072,1088]{1,0:T(8,128)(2,1)} custom-call(bf16[2176,3072]{1,0:T(8,128)(2,1)} %bitcast.272, bf16[13056,1088]{1,0:T(8,128)(2,1)} %all-gather.3.cloned.1.call-done.k_ref.v_ref, bf16[13056,1088]{1,0:T(8,128)(2,1)} %all-gather.3.cloned.1.call-done.k_ref.v_ref), custom_call_target="tpu_custom_call" | custom-call | tf_op jit(solution)/shard_map/pallas_call | solution.py:789
  649.5 97.3 %shard_map.274 = f32[2,2,64,1088]{3,2,1,0:T(8,128)} custom-call(bf16[2,1536,1088]{2,1,0:T(8,128)(2,1)} %bitcast.278), custom_call_target="tpu_custom_call" | custom-call | tf_op jit(solution)/shard_map/pallas_call | solution.py:591
  747.4 7.5 fusion.86
  767.3 163.9 %shard_map.275 = (bf16[16,264,1088]{2,1,0:T(8,128)(2,1)}, bf16[16,264,1088]{2,1,0:T(8,128)(2,1)}) custom-call(bf16[264,1088]{1,0:T(8,128)(2,1)} %concatenate.45.x_ref), custom_call_target="tpu_custom_call" | custom-call | tf_op jit(solution)/shard_map/pallas_call | solution.py:744
  934.1 24.4 %fusion.5 = f32[1088,1572]{1,0:T(8,128)} fusion(f32[1088,1572]{1,0:T(8,128)} %convert_add_fusion, bf16[4224,1088]{1,0:T(8,128)(2,1)} %bitcast.308, s32[4224]{0:T(1024)S(1)} %sub.251), kind=kOutput, calls=%fused_computation.10 | convolution fusion | flops 14457268224 | bytes 22891008 | tf_op jit(solution)/shard_map/dot_general | solution.py:860
  958.4 24.5 %multiply_reduce_fusion = (f32[]{:T(128)}, f32[1088,1572]{1,0:T(8,128)}) fusion(f32[1088,1572]{1,0:T(8,128)} %fusion.5, bf16[4224,1088]{1,0:T(8,128)(2,1)S(1)} %bitcast.307, s32[4224]{0:T(1024)S(1)} %sub.253), kind=kOutput, calls=%fused_computation.27 | convolution fusion | flops 14460688384 | bytes 22891012 | tf_op jit(solution)/shard_map/dot_general | solution.py:860
  987.8 12.8 %shard_map.281 = f32[32,8,128]{2,1,0:T(8,128)} custom-call(f32[8,128]{1,0:T(8,128)} %broadcast_select_fusion.x_ref), custom_call_target="tpu_custom_call" | custom-call | tf_op jit(solution)/shard_map/pallas_call | solution.py:95
  1004.9 21.6 %convert_bitcast_fusion = (bf16[1572,1088]{0,1:T(8,128)(2,1)}, f32[1088,1572]{1,0:T(8,128)}, f32[1572,1088]{0,1:T(8,128)}, f32[1572,1088]{0,1:T(8,128)}) fusion(f32[1572,1088]{0,1:T(8,128)} %param.25, f32[1088,1572]{1,0:T(8,128)} %get-tuple-element.108, f32[]{:T(128)S(6)} %min.3, f32[1572,1088]{0,1:T(8,128)} %param.24, f32[1572,1088]{0,1:T(8,128)} %param.23), kind=kLoop, calls=%fused_computation.70 | loop fusion | flops 29075712 | bytes 51310084 | tf_op jit(solution)/shard_map/transpose | solution.py:1305
  1026.5 6.5 convert_bitcast_fusion.1
  (247 shorter events, 100.9 us)
Async XLA Ops:
  7.2 285.9 %all-gather.3.cloned.1.call-start = ((), (), s32[]{:S(2)}) async-start(), calls=%async_computation.1 | async-start | bytes 31021056 | tf_op jit(solution)/shard_map/all_gather | solution.py:1022
  9.9 973.0 %reduce-scatter.4.cloned.1.call-start = ((), (), s32[]{:S(2)}) async-start(), calls=%async_computation.2 | async-start | bytes 31021056
  10.0 8.3 collective-permute-start
  18.3 109.1 %collective-permute-start.1 = (bf16[1088,1572]{1,0:T(8,128)(2,1)}, bf16[1088,1572]{1,0:T(8,128)(2,1)}, u32[]{:S(2)}, u32[]{:S(2)}) collective-permute-start(bf16[1088,1572]{1,0:T(8,128)(2,1)} %bitcast_convert_fusion.table_ref), channel_id=1, source_target_pairs={{0,16},{16,0},{1,17},{17,1},{2,18},{18,2},{3,19},{19,3},{4,20},{20... | collective-permute-start | bytes 10262024 | tf_op jit(solution)/shard_map/ppermute | solution.py:1018
  33.8 28.3 %copy-start.19 = (s32[16,320]{1,0:T(8,128)}, s32[16,320]{1,0:T(8,128)S(1)}, u32[]{:S(2)}) copy-start(s32[16,320]{1,0:T(8,128)S(1)} %slice_convert_fusion.1) | copy-start | bytes 61444
  62.2 180.2 %copy-start.21 = (f32[1088]{0:T(1024)}, f32[1088]{0:T(1024)S(1)}, u32[]{:S(2)}) copy-start(f32[1088]{0:T(1024)S(1)} %get-tuple-element.58) | copy-start | bytes 13060
  240.8 52.2 %copy-start.23 = (f32[256]{0:T(256)}, f32[256]{0:T(256)S(1)}, u32[]{:S(2)}) copy-start(f32[256]{0:T(256)S(1)} %broadcast_multiply_fusion.8) | copy-start | bytes 3076
  242.4 50.7 %copy-start.26 = (f32[256]{0:T(256)}, f32[256]{0:T(256)S(1)}, u32[]{:S(2)}) copy-start(f32[256]{0:T(256)S(1)} %add_rsqrt_fusion.2) | copy-start | bytes 3076
  244.8 48.3 %copy-start.8 = (bf16[256,1088]{1,0:T(8,128)(2,1)S(1)}, bf16[256,1088]{1,0:T(8,128)(2,1)}, u32[]{:S(2)}) copy-start(bf16[256,1088]{1,0:T(8,128)(2,1)} %add_convert_fusion.3.r_ref) | copy-start | bytes 1671172
  320.0 34.5 %copy-start.2 = (f32[256,1088]{1,0:T(8,128)S(1)}, f32[256,1088]{1,0:T(8,128)}, u32[]{:S(2)}) copy-start(f32[256,1088]{1,0:T(8,128)} %shard_map.266) | copy-start | bytes 3342340
  357.6 17.5 %slice-start = ((s8[30081024]{0:T(1024)(128)(4,1)}), s8[4194304]{0:T(1024)(128)(4,1)S(1)}, s32[]{:S(2)}) async-start(s8[30081024]{0:T(1024)(128)(4,1)} %bitcast.269), calls=%async_computation.3 | async-start | bytes 8388608
  358.2 16.9 %copy-start.12 = (bf16[256,1088]{1,0:T(8,128)(2,1)}, bf16[256,1088]{1,0:T(8,128)(2,1)S(1)}, u32[]{:S(2)}) copy-start(bf16[256,1088]{1,0:T(8,128)(2,1)S(1)} %add_convert_fusion.2.r_ref) | copy-start | bytes 1671172
  358.2 16.9 %slice-start.1 = ((s8[30081024]{0:T(1024)(128)(4,1)}), s8[4194304]{0:T(1024)(128)(4,1)S(1)}, s32[]{:S(2)}) async-start(s8[30081024]{0:T(1024)(128)(4,1)} %bitcast.269), calls=%async_computation.4 | async-start | bytes 8388608
  358.2 16.9 %slice-start.2 = ((s8[30081024]{0:T(1024)(128)(4,1)}), s8[4194304]{0:T(1024)(128)(4,1)S(1)}, s32[]{:S(2)}) async-start(s8[30081024]{0:T(1024)(128)(4,1)} %bitcast.269), calls=%async_computation.5 | async-start | bytes 8388608
  358.2 16.9 %slice-start.3 = ((s8[30081024]{0:T(1024)(128)(4,1)}), s8[4194304]{0:T(1024)(128)(4,1)S(1)}, s32[]{:S(2)}) async-start(s8[30081024]{0:T(1024)(128)(4,1)} %bitcast.269), calls=%async_computation.6 | async-start | bytes 8388608
  358.2 16.9 %slice-start.4 = ((s8[30081024]{0:T(1024)(128)(4,1)}), s8[4194304]{0:T(1024)(128)(4,1)S(1)}, s32[]{:S(2)}) async-start(s8[30081024]{0:T(1024)(128)(4,1)} %bitcast.269), calls=%async_computation.7 | async-start | bytes 8388608
  358.2 16.9 %slice-start.5 = ((s8[30081024]{0:T(1024)(128)(4,1)}), s8[4194304]{0:T(1024)(128)(4,1)S(1)}, s32[]{:S(2)}) async-start(s8[30081024]{0:T(1024)(128)(4,1)} %bitcast.269), calls=%async_computation.8 | async-start | bytes 8388608
  358.2 16.9 %slice-start.6 = ((s8[30081024]{0:T(1024)(128)(4,1)}), s8[4194304]{0:T(1024)(128)(4,1)S(1)}, s32[]{:S(2)}) async-start(s8[30081024]{0:T(1024)(128)(4,1)} %bitcast.269), calls=%async_computation.9 | async-start | bytes 8388608
  358.2 16.9 %slice-start.7 = ((s8[30081024]{0:T(1024)(128)(4,1)}), s8[720896]{0:T(1024)(128)(4,1)S(1)}, s32[]{:S(2)}) async-start(s8[30081024]{0:T(1024)(128)(4,1)} %bitcast.269), calls=%async_computation.10 | async-start | bytes 1441792
  441.3 18.1 %slice-start.8 = ((s8[6455296]{0:T(1024)(128)(4,1)}), s8[4194304]{0:T(1024)(128)(4,1)S(1)}, s32[]{:S(2)}) async-start(s8[6455296]{0:T(1024)(128)(4,1)} %bitcast.283), calls=%async_computation.11 | async-start | bytes 8388608
  471.6 26.8 %copy-start.4 = (f32[256,1088]{1,0:T(8,128)S(1)}, f32[256,1088]{1,0:T(8,128)}, u32[]{:S(2)}) copy-start(f32[256,1088]{1,0:T(8,128)} %get-tuple-element.99) | copy-start | bytes 3342340
  498.9 92.8 %collective-permute-start.2 = (bf16[1088,1572]{1,0:T(8,128)(2,1)}, bf16[1088,1572]{1,0:T(8,128)(2,1)}, u32[]{:S(2)}, u32[]{:S(2)}) collective-permute-start(bf16[1088,1572]{1,0:T(8,128)(2,1)} %convolution_convert_fusion.1), channel_id=1, source_target_pairs={{0,16},{16,0},{1,17},{17,1},{2,18},{18,2},{3,19},{19,3},{4,20},{20... | collective-permute-start | bytes 10262024 | tf_op jit(solution)/shard_map/ppermute | solution.py:1169
  536.0 43.2 %copy-start.16 = (bf16[256,1088]{1,0:T(8,128)(2,1)}, bf16[256,1088]{1,0:T(8,128)(2,1)S(1)}, u32[]{:S(2)}) copy-start(bf16[256,1088]{1,0:T(8,128)(2,1)S(1)} %get-tuple-element.73.r_ref) | copy-start | bytes 1671172
  618.7 3.8 collective-permute-start.3
  649.5 97.9 %copy-start.14 = (bf16[16,64,1088]{2,1,0:T(8,128)(2,1)S(1)}, bf16[16,64,1088]{2,1,0:T(8,128)(2,1)}, u32[]{:S(2)}) copy-start(bf16[16,64,1088]{2,1,0:T(8,128)(2,1)} %shard_map.269) | copy-start | bytes 6684676
  934.1 24.4 %copy-start.28 = (bf16[16,264,1088]{2,1,0:T(8,128)(2,1)S(1)}, bf16[16,264,1088]{2,1,0:T(8,128)(2,1)}, u32[]{:S(2)}) copy-start(bf16[16,264,1088]{2,1,0:T(8,128)(2,1)} %get-tuple-element.35) | copy-start | bytes 27574276
  958.4 45.8 %copy-start.30 = (f32[204]{0:T(256)S(1)}, f32[204]{0:T(256)}, u32[]{:S(2)}) copy-start(f32[204]{0:T(256)} %param.29) | copy-start | bytes 2452
  958.4 45.8 %copy-start.34 = (f32[204]{0:T(256)S(1)}, f32[204]{0:T(256)}, u32[]{:S(2)}) copy-start(f32[204]{0:T(256)} %param.30) | copy-start | bytes 2452
  958.4 45.8 %copy-start.35 = (f32[204]{0:T(256)S(1)}, f32[204]{0:T(256)}, u32[]{:S(2)}) copy-start(f32[204]{0:T(256)} %param.31) | copy-start | bytes 2452
  1004.9 21.6 %copy-start.5 = (f32[1088,408]{0,1:T(8,128)S(1)}, f32[1088,408]{0,1:T(8,128)}, u32[]{:S(2)}) copy-start(f32[1088,408]{0,1:T(8,128)} %param.26) | copy-start | bytes 5326852
  1004.9 21.6 %copy-start.11 = (bf16[1,408,1088]{2,1,0:T(8,128)(2,1)S(1)}, bf16[1,408,1088]{2,1,0:T(8,128)(2,1)}, u32[]{:S(2)}) copy-start(bf16[1,408,1088]{2,1,0:T(8,128)(2,1)} %reduce-scatter.4.cloned.1.call-done) | copy-start | bytes 2663428
  1004.9 28.1 %copy-start.1 = (s32[50304]{0:T(1024)S(1)}, s32[50304]{0:T(1024)}, u32[]{:S(2)}) copy-start(s32[50304]{0:T(1024)} %param.22) | copy-start | bytes 603652
  (24 other events, 180.6 us)
Sparse Core Ops, SparseCore 0:
  11.4 215.6 all-gather.2
  618.1 340.6 reduce-scatter.3

commit v7 on v5

--- a/solution.py
+++ b/solution.py
@@ -656,23 +656,27 @@
     )
 
 
-def turned_kernel(l_ref, r_ref, o_ref):
-    o_ref[...] = contract(l_ref[...], r_ref[...], 0, 0).astype(BF)
-
-
-def turned_product(left, right, block):
+def turned_kernel(l_ref, k_ref, v_ref, o_ref):
+    width = k_ref.shape[0]
+    o_ref[...] = (
+        contract(l_ref[:width], k_ref[...], 0, 0) + contract(l_ref[width:], v_ref[...], 0, 0)
+    ).astype(BF)
+
+
+def turned_product(left, weights, block):
     depth, rows = left.shape
-    width = right.shape[1]
+    width = weights.shape[1]
     return pl.pallas_call(
         turned_kernel,
         grid=(rows // block,),
         out_shape=jax.ShapeDtypeStruct((rows, width), BF),
         in_specs=[
             pl.BlockSpec((depth, block), lambda i: (0, i)),
-            pl.BlockSpec((depth, width), lambda i: (0, 0)),
+            pl.BlockSpec((width, width), lambda i: (1, 0)),
+            pl.BlockSpec((width, width), lambda i: (2, 0)),
         ],
         out_specs=pl.BlockSpec((block, width), lambda i: (i, 0)),
-    )(left, right)
+    )(left, weights, weights)
 
 
 def visible_rows(kind, run_devs, rows_dev, half, q):
@@ -1075,7 +1079,7 @@
     grad_pairs = grad_pairs.reshape(2 * width, MB * key_rows)
     weight_grad = place_product(weight_grad, grad_query, hidden_one, 0, columns)
     weight_grad = place_product(weight_grad, grad_pairs, hidden_sel, width, columns)
-    low_sel = turned_product(grad_pairs, w_kv, 2 * 2 * rows_dev).reshape(MB, key_rows, width)
+    low_sel = turned_product(grad_pairs, weights, 2 * 2 * rows_dev).reshape(MB, key_rows, width)
     weight_sum = lax.psum_scatter(
         weight_grad.reshape(all_count, -1, width), ("dp", "seq"), scatter_dimension=0, tiled=True
     )[0].astype(F32)

time: 1010 us -> 1010 us (level)
  transfers between devices with their start and end apart: 6 -> 6, of which waited for: 2 -> 2; matrix products, arithmetic and copies ran while one was open for 13% -> 12% of each run, Pallas kernels for 50% -> 50%
where the time goes in v7:
time: 1010 us; the launch traced here: 999 us
  Pallas kernels  633 us (63%)
  matrix products  179 us (18%)
  other arithmetic  74.1 us (7%)
  waiting for transfers between devices  68.3 us (7%)
  local copies, waits for them, and re-layouts  19.5 us (2%)
  between operations  19.2 us (2%)
    pallas_call x3, Pallas kernels, fold(): pl.pallas_call(functools.partial(fold_kernel, (len(arrays), len(out_shape...  192 us
    dot_general x17, matrix products, contract(): lax.dot_general(left, right, (((left_dim,), (right_dim,)), ((), ())), pre...  178 us
    pallas_call x1, Pallas kernels, exchange(): pl.pallas_call(exchange_kernel, out_shape=[jax.ShapeDtypeStruct((count,)...  138 us
    pallas_call x2, Pallas kernels, spread(): pl.pallas_call(functools.partial(spread_kernel, (len(blocks), len(out_sha...  72.7 us
    ppermute x1, waiting for transfers between devices, on_device(): lax.ppermute(slab_t[0], 'dp', [(i, (i - step) % group_count) for i in ran...  65.2 us
    pallas_call x2, Pallas kernels, lookup(): pl.pallas_call(lookup_kernel, grid=(slots.shape[0] // block,), out_shape=...  51.4 us
    pallas_call x5, Pallas kernels, place_product(): pl.pallas_call(place_kernel, grid=(left.shape[0] // block,), out_shape=ja...  47.7 us
    pallas_call x1, Pallas kernels, attend_back(): pl.pallas_call(attend_back_kernel, grid=(q.shape[1] // rows, HEADS), out_...  39.6 us
  transfers between devices with their start and end apart: 6, of which 2 were waited for; matrix products, arithmetic and copies ran while one was open for 12% of the time, Pallas kernels for 50%

profile of v7, /device:TPU:0, one launch (start us, length us, event | category | flops | bytes accessed | tf_op | source)
XLA Modules:
  0.0 998.5 jit_solution(2826678800531069999)
XLA Ops:
  23.0 9.7 shard_map.263
  36.6 25.6 %shard_map.264.refs_0_ = bf16[4096,1088]{1,0:T(8,128)(2,1)} custom-call(s32[1]{0:T(128)} %bitcast.8.first_ref, s32[4096,1]{1,0:T(8,128)} %bitcast.279, bf16[1088,1572]{1,0:T(8,128)(2,1)} %bitcast_convert_fusion.table_ref), custom_call_target="tpu_custom_call" | custom-call | tf_op jit(solution)/shard_map/pallas_call | solution.py:823
  62.3 65.2 %collective-permute-done.1.table_ref = bf16[1088,1572]{1,0:T(8,128)(2,1)} collective-permute-done((bf16[1088,1572]{1,0:T(8,128)(2,1)}, bf16[1088,1572]{1,0:T(8,128)(2,1)}, u32[]{:S(2)}, u32[]{:S(2)}) %collective-permute-start.1) | collective-permute-done | bytes 3420704 | tf_op jit(solution)/shard_map/ppermute | solution.py:898
  127.4 25.9 %shard_map.265 = bf16[4096,1088]{1,0:T(8,128)(2,1)} custom-call(s32[1]{0:T(128)} %bitcast.3.first_ref, s32[4096,1]{1,0:T(8,128)} %bitcast.280, bf16[1088,1572]{1,0:T(8,128)(2,1)} %collective-permute-done.1.table_ref, bf16[4096,1088]{1,0:T(8,128)(2,1)} %shard_map.264.refs_0_), custom_call_target="tpu_custom_call" | custom-call | tf_op jit(solution)/shard_map/pallas_call | solution.py:823
  153.3 86.1 %shard_map.266 = f32[256,1088]{1,0:T(8,128)} custom-call(bf16[16,256,1088]{2,1,0:T(8,128)(2,1)} %bitcast.275), custom_call_target="tpu_custom_call" | custom-call | tf_op jit(solution)/shard_map/pallas_call | solution.py:448
  244.8 48.3 %shard_map.267 = bf16[2,1536,1088]{2,1,0:T(8,128)(2,1)} custom-call(bf16[2,2,64,1088]{3,2,1,0:T(8,128)(2,1)} %bitcast.285), custom_call_target="tpu_custom_call" | custom-call | tf_op jit(solution)/shard_map/pallas_call | solution.py:285
  296.6 23.4 %convolution_convert_fusion = bf16[3072,2176]{0,1:T(8,128)(2,1)} fusion(bf16[3072,1088]{1,0:T(8,128)(2,1)} %bitcast.276, bf16[13056,1088]{1,0:T(8,128)(2,1)} %all-gather.3.cloned.1.call-done.k_ref.v_ref), kind=kOutput, calls=%fused_computation.5 | convolution fusion | flops 14552530944 | bytes 25460736 | tf_op jit(solution)/shard_map/dot_general | solution.py:740
  320.0 34.5 %shard_map.268.l_ref = bf16[1088,256]{1,0:T(8,128)(2,1)} custom-call(s32[128,1]{1,0:T(8,128)} %copy.165.pos_ref, bf16[1088,256]{1,0:T(8,128)(2,1)} %fusion.48.q_ref, bf16[2,1088,3072]{2,1,0:T(8,128)(2,1)} %bitcast.273), custom_call_target="tpu_custom_call" | custom-call | tf_op jit(solution)/shard_map/pallas_call | solution.py:790
  358.2 16.8 %fusion.23 = (bf16[4352,256]{1,0:T(8,128)(2,1)}, f32[4352,256]{1,0:T(8,128)}, f32[256,4352]{0,1:T(8,128)}) fusion(bf16[256,1088]{1,0:T(8,128)(2,1)S(1)} %add_convert_fusion.2.r_ref, bf16[13056,1088]{1,0:T(8,128)(2,1)} %all-gather.3.cloned.1.call-done.k_ref.v_ref), kind=kOutput, calls=%fused_computation.49 | convolution fusion | flops 2496724992 | bytes 21725184 | tf_op jit(solution)/shard_map/dot_general | solution.py:740
  384.8 24.4 %shard_map.269 = bf16[16,64,1088]{2,1,0:T(8,128)(2,1)} custom-call(bf16[64,1088]{1,0:T(8,128)(2,1)} %bitcast.294), custom_call_target="tpu_custom_call" | custom-call | tf_op jit(solution)/shard_map/pallas_call | solution.py:285
  409.3 7.3 fusion.97
  416.6 8.7 fusion.98
  429.8 8.4 shard_map.270
  441.3 10.0 %convolution_convert_fusion.1 = bf16[1088,1572]{1,0:T(8,128)(2,1)} fusion(bf16[1024,1088]{1,0:T(8,128)(2,1)} %bitcast.288, f32[1024,1572]{0,1:T(8,128)} %copy-done.7, f32[1024]{0:T(1024)S(1)} %get-tuple-element.78, f32[1024]{0:T(1024)S(1)} %mul.452, s32[1024]{0:T(1024)S(1)} %sub.227), kind=kOutput, calls=%fused_computation.19 | convolution fusion | flops 3514136832 | bytes 12100096 | tf_op jit(solution)/shard_map/dot_general | solution.py:740
  451.4 8.1 fusion.87
  459.5 7.8 fusion.44
  471.6 25.1 %shard_map.271 = f32[64,1088]{1,0:T(8,128)} custom-call(bf16[16,64,1088]{2,1,0:T(8,128)(2,1)} %bitcast.281), custom_call_target="tpu_custom_call" | custom-call | tf_op jit(solution)/shard_map/pallas_call | solution.py:448
  501.9 9.0 shard_map.276.refs_0_
  510.9 10.6 %fusion.29.l_ref = bf16[4352,256]{1,0:T(8,128)(2,1)S(1)} fusion(f32[4352,256]{1,0:T(8,128)} %get-tuple-element.80, bf16[256,1088]{1,0:T(8,128)(2,1)S(1)} %copy-done.15, bf16[13056,1088]{1,0:T(8,128)(2,1)} %all-gather.3.cloned.1.call-done.k_ref.v_ref, f32[256,4352]{0,1:T(8,128)} %get-tuple-element.97), kind=kOutput, calls=%fused_computation.55 | convolution fusion | flops 2439905280 | bytes 21725184 | tf_op jit(solution)/shard_map/dot_general | solution.py:740
  521.5 9.6 fusion.99
  539.7 39.6 %shard_map.272 = (bf16[1088,256]{1,0:T(8,128)(2,1)}, bf16[2,1088,3072]{2,1,0:T(8,128)(2,1)}) custom-call(s32[128,1]{1,0:T(8,128)} %copy.165.pos_ref, bf16[1088,256]{1,0:T(8,128)(2,1)} %fusion.48.q_ref, bf16[2,1088,3072]{2,1,0:T(8,128)(2,1)} %bitcast.274, bf16[1088,256]{1,0:T(8,128)(2,1)} %fusion.49.g_ref), custom_call_target="tpu_custom_call" | custom-call | tf_op jit(solution)/shard_map/pallas_call | solution.py:803
  579.2 9.0 shard_map.277.refs_0_
  595.0 23.0 %shard_map.280 = bf16[13056,1088]{1,0:T(8,128)(2,1)} custom-call(bf16[2176,3072]{1,0:T(8,128)(2,1)} %bitcast.271, bf16[3072,1088]{1,0:T(8,128)(2,1)} %bitcast.277, bf16[13056,1088]{1,0:T(8,128)(2,1)} %shard_map.279.refs_0_), custom_call_target="tpu_custom_call", output_to_operand_aliasing={{}: (2, {})} | custom-call | tf_op jit(solution)/shard_map/pallas_call | solution.py:725
  622.8 26.7 %shard_map.273 = bf16[3072,1088]{1,0:T(8,128)(2,1)} custom-call(bf16[2176,3072]{1,0:T(8,128)(2,1)} %bitcast.272, bf16[13056,1088]{1,0:T(8,128)(2,1)} %all-gather.3.cloned.1.call-done.k_ref.v_ref, bf16[13056,1088]{1,0:T(8,128)(2,1)} %all-gather.3.cloned.1.call-done.k_ref.v_ref), custom_call_target="tpu_custom_call" | custom-call | tf_op jit(solution)/shard_map/pallas_call | solution.py:669
  649.5 80.9 %shard_map.274 = f32[2,2,64,1088]{3,2,1,0:T(8,128)} custom-call(bf16[2,1536,1088]{2,1,0:T(8,128)(2,1)} %bitcast.278), custom_call_target="tpu_custom_call" | custom-call | tf_op jit(solution)/shard_map/pallas_call | solution.py:448
  731.0 8.0 fusion.86
  751.4 138.0 %shard_map.275 = (bf16[16,264,1088]{2,1,0:T(8,128)(2,1)}, bf16[16,264,1088]{2,1,0:T(8,128)(2,1)}) custom-call(bf16[264,1088]{1,0:T(8,128)(2,1)} %concatenate.45.x_ref), custom_call_target="tpu_custom_call" | custom-call | tf_op jit(solution)/shard_map/pallas_call | solution.py:624
  892.2 24.2 %fusion.5 = f32[1088,1572]{1,0:T(8,128)} fusion(f32[1088,1572]{1,0:T(8,128)} %convert_add_fusion, bf16[4224,1088]{1,0:T(8,128)(2,1)} %bitcast.308, s32[4224]{0:T(1024)S(1)} %sub.251), kind=kOutput, calls=%fused_computation.10 | convolution fusion | flops 14457268224 | bytes 22891008 | tf_op jit(solution)/shard_map/dot_general | solution.py:740
  916.4 24.5 %multiply_reduce_fusion = (f32[]{:T(128)}, f32[1088,1572]{1,0:T(8,128)}) fusion(f32[1088,1572]{1,0:T(8,128)} %fusion.5, bf16[4224,1088]{1,0:T(8,128)(2,1)S(1)} %bitcast.307, s32[4224]{0:T(1024)S(1)} %sub.253), kind=kOutput, calls=%fused_computation.27 | convolution fusion | flops 14460688384 | bytes 22891012 | tf_op jit(solution)/shard_map/dot_general | solution.py:740
  945.8 12.1 %shard_map.281 = f32[32,8,128]{2,1,0:T(8,128)} custom-call(f32[8,128]{1,0:T(8,128)} %broadcast_select_fusion.x_ref), custom_call_target="tpu_custom_call" | custom-call | tf_op jit(solution)/shard_map/pallas_call | solution.py:95
  962.3 21.6 %convert_bitcast_fusion = (bf16[1572,1088]{0,1:T(8,128)(2,1)}, f32[1088,1572]{1,0:T(8,128)}, f32[1572,1088]{0,1:T(8,128)}, f32[1572,1088]{0,1:T(8,128)}) fusion(f32[1572,1088]{0,1:T(8,128)} %param.25, f32[1088,1572]{1,0:T(8,128)} %get-tuple-element.108, f32[]{:T(128)S(6)} %min.3, f32[1572,1088]{0,1:T(8,128)} %param.24, f32[1572,1088]{0,1:T(8,128)} %param.23), kind=kLoop, calls=%fused_computation.70 | loop fusion | flops 29075712 | bytes 51310084 | tf_op jit(solution)/shard_map/transpose | solution.py:1185
  983.9 6.5 convert_bitcast_fusion.1
  (247 shorter events, 100.9 us)
Async XLA Ops:
  7.2 285.9 %all-gather.3.cloned.1.call-start = ((), (), s32[]{:S(2)}) async-start(), calls=%async_computation.1 | async-start | bytes 31021056 | tf_op jit(solution)/shard_map/all_gather | solution.py:902
  9.9 931.0 %reduce-scatter.4.cloned.1.call-start = ((), (), s32[]{:S(2)}) async-start(), calls=%async_computation.2 | async-start | bytes 31021056
  10.0 8.3 collective-permute-start
  18.3 109.1 %collective-permute-start.1 = (bf16[1088,1572]{1,0:T(8,128)(2,1)}, bf16[1088,1572]{1,0:T(8,128)(2,1)}, u32[]{:S(2)}, u32[]{:S(2)}) collective-permute-start(bf16[1088,1572]{1,0:T(8,128)(2,1)} %bitcast_convert_fusion.table_ref), channel_id=1, source_target_pairs={{0,16},{16,0},{1,17},{17,1},{2,18},{18,2},{3,19},{19,3},{4,20},{20... | collective-permute-start | bytes 10262024 | tf_op jit(solution)/shard_map/ppermute | solution.py:898
  33.8 28.3 %copy-start.19 = (s32[16,320]{1,0:T(8,128)}, s32[16,320]{1,0:T(8,128)S(1)}, u32[]{:S(2)}) copy-start(s32[16,320]{1,0:T(8,128)S(1)} %slice_convert_fusion.1) | copy-start | bytes 61444
  62.2 180.2 %copy-start.21 = (f32[1088]{0:T(1024)}, f32[1088]{0:T(1024)S(1)}, u32[]{:S(2)}) copy-start(f32[1088]{0:T(1024)S(1)} %get-tuple-element.58) | copy-start | bytes 13060
  240.8 52.2 %copy-start.23 = (f32[256]{0:T(256)}, f32[256]{0:T(256)S(1)}, u32[]{:S(2)}) copy-start(f32[256]{0:T(256)S(1)} %broadcast_multiply_fusion.8) | copy-start | bytes 3076
  242.4 50.7 %copy-start.26 = (f32[256]{0:T(256)}, f32[256]{0:T(256)S(1)}, u32[]{:S(2)}) copy-start(f32[256]{0:T(256)S(1)} %add_rsqrt_fusion.2) | copy-start | bytes 3076
  244.8 48.3 %copy-start.8 = (bf16[256,1088]{1,0:T(8,128)(2,1)S(1)}, bf16[256,1088]{1,0:T(8,128)(2,1)}, u32[]{:S(2)}) copy-start(bf16[256,1088]{1,0:T(8,128)(2,1)} %add_convert_fusion.3.r_ref) | copy-start | bytes 1671172
  320.0 34.5 %copy-start.2 = (f32[256,1088]{1,0:T(8,128)S(1)}, f32[256,1088]{1,0:T(8,128)}, u32[]{:S(2)}) copy-start(f32[256,1088]{1,0:T(8,128)} %shard_map.266) | copy-start | bytes 3342340
  357.6 17.5 %slice-start = ((s8[30081024]{0:T(1024)(128)(4,1)}), s8[4194304]{0:T(1024)(128)(4,1)S(1)}, s32[]{:S(2)}) async-start(s8[30081024]{0:T(1024)(128)(4,1)} %bitcast.269), calls=%async_computation.3 | async-start | bytes 8388608
  358.2 16.9 %copy-start.12 = (bf16[256,1088]{1,0:T(8,128)(2,1)}, bf16[256,1088]{1,0:T(8,128)(2,1)S(1)}, u32[]{:S(2)}) copy-start(bf16[256,1088]{1,0:T(8,128)(2,1)S(1)} %add_convert_fusion.2.r_ref) | copy-start | bytes 1671172
  358.2 16.9 %slice-start.1 = ((s8[30081024]{0:T(1024)(128)(4,1)}), s8[4194304]{0:T(1024)(128)(4,1)S(1)}, s32[]{:S(2)}) async-start(s8[30081024]{0:T(1024)(128)(4,1)} %bitcast.269), calls=%async_computation.4 | async-start | bytes 8388608
  358.2 16.9 %slice-start.2 = ((s8[30081024]{0:T(1024)(128)(4,1)}), s8[4194304]{0:T(1024)(128)(4,1)S(1)}, s32[]{:S(2)}) async-start(s8[30081024]{0:T(1024)(128)(4,1)} %bitcast.269), calls=%async_computation.5 | async-start | bytes 8388608
  358.2 16.9 %slice-start.3 = ((s8[30081024]{0:T(1024)(128)(4,1)}), s8[4194304]{0:T(1024)(128)(4,1)S(1)}, s32[]{:S(2)}) async-start(s8[30081024]{0:T(1024)(128)(4,1)} %bitcast.269), calls=%async_computation.6 | async-start | bytes 8388608
  358.2 16.9 %slice-start.4 = ((s8[30081024]{0:T(1024)(128)(4,1)}), s8[4194304]{0:T(1024)(128)(4,1)S(1)}, s32[]{:S(2)}) async-start(s8[30081024]{0:T(1024)(128)(4,1)} %bitcast.269), calls=%async_computation.7 | async-start | bytes 8388608
  358.2 16.9 %slice-start.5 = ((s8[30081024]{0:T(1024)(128)(4,1)}), s8[4194304]{0:T(1024)(128)(4,1)S(1)}, s32[]{:S(2)}) async-start(s8[30081024]{0:T(1024)(128)(4,1)} %bitcast.269), calls=%async_computation.8 | async-start | bytes 8388608
  358.2 16.9 %slice-start.6 = ((s8[30081024]{0:T(1024)(128)(4,1)}), s8[4194304]{0:T(1024)(128)(4,1)S(1)}, s32[]{:S(2)}) async-start(s8[30081024]{0:T(1024)(128)(4,1)} %bitcast.269), calls=%async_computation.9 | async-start | bytes 8388608
  358.2 16.9 %slice-start.7 = ((s8[30081024]{0:T(1024)(128)(4,1)}), s8[720896]{0:T(1024)(128)(4,1)S(1)}, s32[]{:S(2)}) async-start(s8[30081024]{0:T(1024)(128)(4,1)} %bitcast.269), calls=%async_computation.10 | async-start | bytes 1441792
  441.3 18.1 %slice-start.8 = ((s8[6455296]{0:T(1024)(128)(4,1)}), s8[4194304]{0:T(1024)(128)(4,1)S(1)}, s32[]{:S(2)}) async-start(s8[6455296]{0:T(1024)(128)(4,1)} %bitcast.283), calls=%async_computation.11 | async-start | bytes 8388608
  471.6 26.8 %copy-start.4 = (f32[256,1088]{1,0:T(8,128)S(1)}, f32[256,1088]{1,0:T(8,128)}, u32[]{:S(2)}) copy-start(f32[256,1088]{1,0:T(8,128)} %get-tuple-element.99) | copy-start | bytes 3342340
  498.9 92.8 %collective-permute-start.2 = (bf16[1088,1572]{1,0:T(8,128)(2,1)}, bf16[1088,1572]{1,0:T(8,128)(2,1)}, u32[]{:S(2)}, u32[]{:S(2)}) collective-permute-start(bf16[1088,1572]{1,0:T(8,128)(2,1)} %convolution_convert_fusion.1), channel_id=1, source_target_pairs={{0,16},{16,0},{1,17},{17,1},{2,18},{18,2},{3,19},{19,3},{4,20},{20... | collective-permute-start | bytes 10262024 | tf_op jit(solution)/shard_map/ppermute | solution.py:1049
  536.0 43.2 %copy-start.16 = (bf16[256,1088]{1,0:T(8,128)(2,1)}, bf16[256,1088]{1,0:T(8,128)(2,1)S(1)}, u32[]{:S(2)}) copy-start(bf16[256,1088]{1,0:T(8,128)(2,1)S(1)} %get-tuple-element.73.r_ref) | copy-start | bytes 1671172
  618.7 3.8 collective-permute-start.3
  649.5 81.5 %copy-start.14 = (bf16[16,64,1088]{2,1,0:T(8,128)(2,1)S(1)}, bf16[16,64,1088]{2,1,0:T(8,128)(2,1)}, u32[]{:S(2)}) copy-start(bf16[16,64,1088]{2,1,0:T(8,128)(2,1)} %shard_map.269) | copy-start | bytes 6684676
  892.2 24.2 %copy-start.28 = (bf16[16,264,1088]{2,1,0:T(8,128)(2,1)S(1)}, bf16[16,264,1088]{2,1,0:T(8,128)(2,1)}, u32[]{:S(2)}) copy-start(bf16[16,264,1088]{2,1,0:T(8,128)(2,1)} %get-tuple-element.35) | copy-start | bytes 27574276
  916.4 45.2 %copy-start.30 = (f32[204]{0:T(256)S(1)}, f32[204]{0:T(256)}, u32[]{:S(2)}) copy-start(f32[204]{0:T(256)} %param.29) | copy-start | bytes 2452
  916.4 45.2 %copy-start.34 = (f32[204]{0:T(256)S(1)}, f32[204]{0:T(256)}, u32[]{:S(2)}) copy-start(f32[204]{0:T(256)} %param.30) | copy-start | bytes 2452
  916.4 45.2 %copy-start.35 = (f32[204]{0:T(256)S(1)}, f32[204]{0:T(256)}, u32[]{:S(2)}) copy-start(f32[204]{0:T(256)} %param.31) | copy-start | bytes 2452
  962.3 21.6 %copy-start.5 = (f32[1088,408]{0,1:T(8,128)S(1)}, f32[1088,408]{0,1:T(8,128)}, u32[]{:S(2)}) copy-start(f32[1088,408]{0,1:T(8,128)} %param.26) | copy-start | bytes 5326852
  962.3 21.6 %copy-start.11 = (bf16[1,408,1088]{2,1,0:T(8,128)(2,1)S(1)}, bf16[1,408,1088]{2,1,0:T(8,128)(2,1)}, u32[]{:S(2)}) copy-start(bf16[1,408,1088]{2,1,0:T(8,128)(2,1)} %reduce-scatter.4.cloned.1.call-done) | copy-start | bytes 2663428
  962.3 28.1 %copy-start.1 = (s32[50304]{0:T(1024)S(1)}, s32[50304]{0:T(1024)}, u32[]{:S(2)}) copy-start(s32[50304]{0:T(1024)} %param.22) | copy-start | bytes 603652
  (24 other events, 180.3 us)
Sparse Core Ops, SparseCore 0:
  11.4 215.6 all-gather.2
  618.1 321.9 reduce-scatter.3

commit v8 on v7

--- a/solution.py
+++ b/solution.py
@@ -518,9 +518,6 @@
         index = 4 * number(item) + 2 * other_group + other_side
         return remote(src, dst, c_send, c_recv, index, sibling)
 
-    def by_side(item):
-        return lax.rem(where_of(item), 2) == 0
-
     def z_links(item, act):
         far, turn = item
         if far + 1 < line:
@@ -557,23 +554,10 @@
         core_copy(item, 1, 0, False).start()
 
     def diagonal(item):
-        @pl.when(by_side(item))
-        def _():
-            side_copy(item, 1, False).start()
-
-        @pl.when(jnp.logical_not(by_side(item)))
-        def _():
-            cross_copy(item, 1, False).start()
+        cross_copy(item, 1, False).start()
 
     def third(item):
-        @pl.when(by_side(item))
-        def _():
-            side_copy(item, 1, True).wait_recv()
-
-        @pl.when(jnp.logical_not(by_side(item)))
-        def _():
-            cross_copy(item, 1, True).wait_recv()
-
+        cross_copy(item, 1, True).wait_recv()
         core_copy(item, 1, 1, False).start()
 
     def at_far(far):
@@ -600,14 +584,7 @@
         side_copy(item, 0, False).wait_send()
         cross_copy(item, 0, False).wait_send()
 
-        @pl.when(by_side(item))
-        def _():
-            side_copy(item, 1, False).wait_send()
-
-        @pl.when(jnp.logical_not(by_side(item)))
-        def _():
-            cross_copy(item, 1, False).wait_send()
-
+        cross_copy(item, 1, False).wait_send()
         for other_group in range(2):
             for other_side in range(2):
                 core_copy(item, other_group, other_side, False).wait_send()

time: 1010 us -> 1050 us (1.040)
  Pallas kernels: 633 us -> 671 us
    pallas_call x1, Pallas kernels: 138 us -> 177 us  [exchange(): pl.pallas_call(exchange_kernel, out_shape=[jax.ShapeDtypeStruct((count,)...]
  transfers between devices with their start and end apart: 6 -> 6, of which waited for: 2 -> 2; matrix products, arithmetic and copies ran while one was open for 12% -> 12% of each run, Pallas kernels for 50% -> 52%
where the time goes in v8:
time: 1050 us; the launch traced here: 1040 us
  Pallas kernels  671 us (64%)
  matrix products  179 us (17%)
  other arithmetic  74.1 us (7%)
  waiting for transfers between devices  68.3 us (7%)
  local copies, waits for them, and re-layouts  19.5 us (2%)
  between operations  19.2 us (2%)
    pallas_call x3, Pallas kernels, fold(): pl.pallas_call(functools.partial(fold_kernel, (len(arrays), len(out_shape...  192 us
    dot_general x17, matrix products, contract(): lax.dot_general(left, right, (((left_dim,), (right_dim,)), ((), ())), pre...  178 us
    pallas_call x1, Pallas kernels, exchange(): pl.pallas_call(exchange_kernel, out_shape=[jax.ShapeDtypeStruct((count,)...  177 us
    pallas_call x2, Pallas kernels, spread(): pl.pallas_call(functools.partial(spread_kernel, (len(blocks), len(out_sha...  72.7 us
    ppermute x1, waiting for transfers between devices, on_device(): lax.ppermute(slab_t[0], 'dp', [(i, (i - step) % group_count) for i in ran...  65.2 us
    pallas_call x2, Pallas kernels, lookup(): pl.pallas_call(lookup_kernel, grid=(slots.shape[0] // block,), out_shape=...  51.4 us
    pallas_call x5, Pallas kernels, place_product(): pl.pallas_call(place_kernel, grid=(left.shape[0] // block,), out_shape=ja...  47.7 us
    pallas_call x1, Pallas kernels, attend_back(): pl.pallas_call(attend_back_kernel, grid=(q.shape[1] // rows, HEADS), out_...  39.6 us
  transfers between devices with their start and end apart: 6, of which 2 were waited for; matrix products, arithmetic and copies ran while one was open for 12% of the time, Pallas kernels for 52%

profile of v8, /device:TPU:0, one launch (start us, length us, event | category | flops | bytes accessed | tf_op | source)
XLA Modules:
  0.0 1037.1 jit_solution(15947950538336640433)
XLA Ops:
  23.0 9.7 shard_map.263
  36.6 25.6 %shard_map.264.refs_0_ = bf16[4096,1088]{1,0:T(8,128)(2,1)} custom-call(s32[1]{0:T(128)} %bitcast.8.first_ref, s32[4096,1]{1,0:T(8,128)} %bitcast.279, bf16[1088,1572]{1,0:T(8,128)(2,1)} %bitcast_convert_fusion.table_ref), custom_call_target="tpu_custom_call" | custom-call | tf_op jit(solution)/shard_map/pallas_call | solution.py:800
  62.3 65.2 %collective-permute-done.1.table_ref = bf16[1088,1572]{1,0:T(8,128)(2,1)} collective-permute-done((bf16[1088,1572]{1,0:T(8,128)(2,1)}, bf16[1088,1572]{1,0:T(8,128)(2,1)}, u32[]{:S(2)}, u32[]{:S(2)}) %collective-permute-start.1) | collective-permute-done | bytes 3420704 | tf_op jit(solution)/shard_map/ppermute | solution.py:875
  127.4 25.9 %shard_map.265 = bf16[4096,1088]{1,0:T(8,128)(2,1)} custom-call(s32[1]{0:T(128)} %bitcast.3.first_ref, s32[4096,1]{1,0:T(8,128)} %bitcast.280, bf16[1088,1572]{1,0:T(8,128)(2,1)} %collective-permute-done.1.table_ref, bf16[4096,1088]{1,0:T(8,128)(2,1)} %shard_map.264.refs_0_), custom_call_target="tpu_custom_call" | custom-call | tf_op jit(solution)/shard_map/pallas_call | solution.py:800
  153.3 86.1 %shard_map.266 = f32[256,1088]{1,0:T(8,128)} custom-call(bf16[16,256,1088]{2,1,0:T(8,128)(2,1)} %bitcast.275), custom_call_target="tpu_custom_call" | custom-call | tf_op jit(solution)/shard_map/pallas_call | solution.py:448
  244.8 48.3 %shard_map.267 = bf16[2,1536,1088]{2,1,0:T(8,128)(2,1)} custom-call(bf16[2,2,64,1088]{3,2,1,0:T(8,128)(2,1)} %bitcast.285), custom_call_target="tpu_custom_call" | custom-call | tf_op jit(solution)/shard_map/pallas_call | solution.py:285
  296.6 23.4 %convolution_convert_fusion = bf16[3072,2176]{0,1:T(8,128)(2,1)} fusion(bf16[3072,1088]{1,0:T(8,128)(2,1)} %bitcast.276, bf16[13056,1088]{1,0:T(8,128)(2,1)} %all-gather.3.cloned.1.call-done.k_ref.v_ref), kind=kOutput, calls=%fused_computation.5 | convolution fusion | flops 14552530944 | bytes 25460736 | tf_op jit(solution)/shard_map/dot_general | solution.py:717
  320.0 34.5 %shard_map.268.l_ref = bf16[1088,256]{1,0:T(8,128)(2,1)} custom-call(s32[128,1]{1,0:T(8,128)} %copy.165.pos_ref, bf16[1088,256]{1,0:T(8,128)(2,1)} %fusion.48.q_ref, bf16[2,1088,3072]{2,1,0:T(8,128)(2,1)} %bitcast.273), custom_call_target="tpu_custom_call" | custom-call | tf_op jit(solution)/shard_map/pallas_call | solution.py:767
  358.2 16.8 %fusion.23 = (bf16[4352,256]{1,0:T(8,128)(2,1)}, f32[4352,256]{1,0:T(8,128)}, f32[256,4352]{0,1:T(8,128)}) fusion(bf16[256,1088]{1,0:T(8,128)(2,1)S(1)} %add_convert_fusion.2.r_ref, bf16[13056,1088]{1,0:T(8,128)(2,1)} %all-gather.3.cloned.1.call-done.k_ref.v_ref), kind=kOutput, calls=%fused_computation.49 | convolution fusion | flops 2496724992 | bytes 21725184 | tf_op jit(solution)/shard_map/dot_general | solution.py:717
  384.8 24.4 %shard_map.269 = bf16[16,64,1088]{2,1,0:T(8,128)(2,1)} custom-call(bf16[64,1088]{1,0:T(8,128)(2,1)} %bitcast.294), custom_call_target="tpu_custom_call" | custom-call | tf_op jit(solution)/shard_map/pallas_call | solution.py:285
  409.3 7.3 fusion.97
  416.6 8.7 fusion.98
  429.8 8.4 shard_map.270
  441.3 10.0 convolution_convert_fusion.1
  451.4 8.1 fusion.87
  459.5 7.8 fusion.44
  471.6 25.1 %shard_map.271 = f32[64,1088]{1,0:T(8,128)} custom-call(bf16[16,64,1088]{2,1,0:T(8,128)(2,1)} %bitcast.281), custom_call_target="tpu_custom_call" | custom-call | tf_op jit(solution)/shard_map/pallas_call | solution.py:448
  501.9 9.0 shard_map.276.refs_0_
  510.9 10.6 %fusion.29.l_ref = bf16[4352,256]{1,0:T(8,128)(2,1)S(1)} fusion(f32[4352,256]{1,0:T(8,128)} %get-tuple-element.80, bf16[256,1088]{1,0:T(8,128)(2,1)S(1)} %copy-done.15, bf16[13056,1088]{1,0:T(8,128)(2,1)} %all-gather.3.cloned.1.call-done.k_ref.v_ref, f32[256,4352]{0,1:T(8,128)} %get-tuple-element.97), kind=kOutput, calls=%fused_computation.55 | convolution fusion | flops 2439905280 | bytes 21725184 | tf_op jit(solution)/shard_map/dot_general | solution.py:717
  521.5 9.6 fusion.99
  539.7 39.6 %shard_map.272 = (bf16[1088,256]{1,0:T(8,128)(2,1)}, bf16[2,1088,3072]{2,1,0:T(8,128)(2,1)}) custom-call(s32[128,1]{1,0:T(8,128)} %copy.165.pos_ref, bf16[1088,256]{1,0:T(8,128)(2,1)} %fusion.48.q_ref, bf16[2,1088,3072]{2,1,0:T(8,128)(2,1)} %bitcast.274, bf16[1088,256]{1,0:T(8,128)(2,1)} %fusion.49.g_ref), custom_call_target="tpu_custom_call" | custom-call | tf_op jit(solution)/shard_map/pallas_call | solution.py:780
  579.2 9.0 shard_map.277.refs_0_
  595.0 23.0 %shard_map.280 = bf16[13056,1088]{1,0:T(8,128)(2,1)} custom-call(bf16[2176,3072]{1,0:T(8,128)(2,1)} %bitcast.271, bf16[3072,1088]{1,0:T(8,128)(2,1)} %bitcast.277, bf16[13056,1088]{1,0:T(8,128)(2,1)} %shard_map.279.refs_0_), custom_call_target="tpu_custom_call", output_to_operand_aliasing={{}: (2, {})} | custom-call | tf_op jit(solution)/shard_map/pallas_call | solution.py:702
  622.8 26.7 %shard_map.273 = bf16[3072,1088]{1,0:T(8,128)(2,1)} custom-call(bf16[2176,3072]{1,0:T(8,128)(2,1)} %bitcast.272, bf16[13056,1088]{1,0:T(8,128)(2,1)} %all-gather.3.cloned.1.call-done.k_ref.v_ref, bf16[13056,1088]{1,0:T(8,128)(2,1)} %all-gather.3.cloned.1.call-done.k_ref.v_ref), custom_call_target="tpu_custom_call" | custom-call | tf_op jit(solution)/shard_map/pallas_call | solution.py:646
  649.5 80.9 %shard_map.274 = f32[2,2,64,1088]{3,2,1,0:T(8,128)} custom-call(bf16[2,1536,1088]{2,1,0:T(8,128)(2,1)} %bitcast.278), custom_call_target="tpu_custom_call" | custom-call | tf_op jit(solution)/shard_map/pallas_call | solution.py:448
  731.0 8.0 fusion.86
  751.4 177.1 %shard_map.275 = (bf16[16,264,1088]{2,1,0:T(8,128)(2,1)}, bf16[16,264,1088]{2,1,0:T(8,128)(2,1)}) custom-call(bf16[264,1088]{1,0:T(8,128)(2,1)} %concatenate.45.x_ref), custom_call_target="tpu_custom_call" | custom-call | tf_op jit(solution)/shard_map/pallas_call | solution.py:601
  931.4 24.2 %fusion.5 = f32[1088,1572]{1,0:T(8,128)} fusion(f32[1088,1572]{1,0:T(8,128)} %convert_add_fusion, bf16[4224,1088]{1,0:T(8,128)(2,1)} %bitcast.308, s32[4224]{0:T(1024)S(1)} %sub.251), kind=kOutput, calls=%fused_computation.10 | convolution fusion | flops 14457268224 | bytes 22891008 | tf_op jit(solution)/shard_map/dot_general | solution.py:717
  955.6 24.5 %multiply_reduce_fusion = (f32[]{:T(128)}, f32[1088,1572]{1,0:T(8,128)}) fusion(f32[1088,1572]{1,0:T(8,128)} %fusion.5, bf16[4224,1088]{1,0:T(8,128)(2,1)S(1)} %bitcast.307, s32[4224]{0:T(1024)S(1)} %sub.253), kind=kOutput, calls=%fused_computation.27 | convolution fusion | flops 14460688384 | bytes 22891012 | tf_op jit(solution)/shard_map/dot_general | solution.py:717
  984.9 11.5 %shard_map.281 = f32[32,8,128]{2,1,0:T(8,128)} custom-call(f32[8,128]{1,0:T(8,128)} %broadcast_select_fusion.x_ref), custom_call_target="tpu_custom_call" | custom-call | tf_op jit(solution)/shard_map/pallas_call | solution.py:95
  1000.8 21.6 %convert_bitcast_fusion = (bf16[1572,1088]{0,1:T(8,128)(2,1)}, f32[1088,1572]{1,0:T(8,128)}, f32[1572,1088]{0,1:T(8,128)}, f32[1572,1088]{0,1:T(8,128)}) fusion(f32[1572,1088]{0,1:T(8,128)} %param.25, f32[1088,1572]{1,0:T(8,128)} %get-tuple-element.108, f32[]{:T(128)S(6)} %min.3, f32[1572,1088]{0,1:T(8,128)} %param.24, f32[1572,1088]{0,1:T(8,128)} %param.23), kind=kLoop, calls=%fused_computation.70 | loop fusion | flops 29075712 | bytes 51310084 | tf_op jit(solution)/shard_map/transpose | solution.py:1162
  1022.4 6.5 convert_bitcast_fusion.1
  (247 shorter events, 100.9 us)
Async XLA Ops:
  7.2 285.9 %all-gather.3.cloned.1.call-start = ((), (), s32[]{:S(2)}) async-start(), calls=%async_computation.1 | async-start | bytes 31021056 | tf_op jit(solution)/shard_map/all_gather | solution.py:879
  9.9 970.2 %reduce-scatter.4.cloned.1.call-start = ((), (), s32[]{:S(2)}) async-start(), calls=%async_computation.2 | async-start | bytes 31021056
  10.0 8.3 collective-permute-start
  18.3 109.1 %collective-permute-start.1 = (bf16[1088,1572]{1,0:T(8,128)(2,1)}, bf16[1088,1572]{1,0:T(8,128)(2,1)}, u32[]{:S(2)}, u32[]{:S(2)}) collective-permute-start(bf16[1088,1572]{1,0:T(8,128)(2,1)} %bitcast_convert_fusion.table_ref), channel_id=1, source_target_pairs={{0,16},{16,0},{1,17},{17,1},{2,18},{18,2},{3,19},{19,3},{4,20},{20... | collective-permute-start | bytes 10262024 | tf_op jit(solution)/shard_map/ppermute | solution.py:875
  33.8 28.3 %copy-start.19 = (s32[16,320]{1,0:T(8,128)}, s32[16,320]{1,0:T(8,128)S(1)}, u32[]{:S(2)}) copy-start(s32[16,320]{1,0:T(8,128)S(1)} %slice_convert_fusion.1) | copy-start | bytes 61444
  62.2 180.2 %copy-start.21 = (f32[1088]{0:T(1024)}, f32[1088]{0:T(1024)S(1)}, u32[]{:S(2)}) copy-start(f32[1088]{0:T(1024)S(1)} %get-tuple-element.58) | copy-start | bytes 13060
  240.8 52.2 %copy-start.23 = (f32[256]{0:T(256)}, f32[256]{0:T(256)S(1)}, u32[]{:S(2)}) copy-start(f32[256]{0:T(256)S(1)} %broadcast_multiply_fusion.8) | copy-start | bytes 3076
  242.4 50.7 %copy-start.26 = (f32[256]{0:T(256)}, f32[256]{0:T(256)S(1)}, u32[]{:S(2)}) copy-start(f32[256]{0:T(256)S(1)} %add_rsqrt_fusion.2) | copy-start | bytes 3076
  244.8 48.3 %copy-start.8 = (bf16[256,1088]{1,0:T(8,128)(2,1)S(1)}, bf16[256,1088]{1,0:T(8,128)(2,1)}, u32[]{:S(2)}) copy-start(bf16[256,1088]{1,0:T(8,128)(2,1)} %add_convert_fusion.3.r_ref) | copy-start | bytes 1671172
  320.0 34.5 %copy-start.2 = (f32[256,1088]{1,0:T(8,128)S(1)}, f32[256,1088]{1,0:T(8,128)}, u32[]{:S(2)}) copy-start(f32[256,1088]{1,0:T(8,128)} %shard_map.266) | copy-start | bytes 3342340
  357.6 17.5 %slice-start = ((s8[30081024]{0:T(1024)(128)(4,1)}), s8[4194304]{0:T(1024)(128)(4,1)S(1)}, s32[]{:S(2)}) async-start(s8[30081024]{0:T(1024)(128)(4,1)} %bitcast.269), calls=%async_computation.3 | async-start | bytes 8388608
  358.2 16.9 %copy-start.12 = (bf16[256,1088]{1,0:T(8,128)(2,1)}, bf16[256,1088]{1,0:T(8,128)(2,1)S(1)}, u32[]{:S(2)}) copy-start(bf16[256,1088]{1,0:T(8,128)(2,1)S(1)} %add_convert_fusion.2.r_ref) | copy-start | bytes 1671172
  358.2 16.9 %slice-start.1 = ((s8[30081024]{0:T(1024)(128)(4,1)}), s8[4194304]{0:T(1024)(128)(4,1)S(1)}, s32[]{:S(2)}) async-start(s8[30081024]{0:T(1024)(128)(4,1)} %bitcast.269), calls=%async_computation.4 | async-start | bytes 8388608
  358.2 16.9 %slice-start.2 = ((s8[30081024]{0:T(1024)(128)(4,1)}), s8[4194304]{0:T(1024)(128)(4,1)S(1)}, s32[]{:S(2)}) async-start(s8[30081024]{0:T(1024)(128)(4,1)} %bitcast.269), calls=%async_computation.5 | async-start | bytes 8388608
  358.2 16.9 %slice-start.3 = ((s8[30081024]{0:T(1024)(128)(4,1)}), s8[4194304]{0:T(1024)(128)(4,1)S(1)}, s32[]{:S(2)}) async-start(s8[30081024]{0:T(1024)(128)(4,1)} %bitcast.269), calls=%async_computation.6 | async-start | bytes 8388608
  358.2 16.9 %slice-start.4 = ((s8[30081024]{0:T(1024)(128)(4,1)}), s8[4194304]{0:T(1024)(128)(4,1)S(1)}, s32[]{:S(2)}) async-start(s8[30081024]{0:T(1024)(128)(4,1)} %bitcast.269), calls=%async_computation.7 | async-start | bytes 8388608
  358.2 16.9 %slice-start.5 = ((s8[30081024]{0:T(1024)(128)(4,1)}), s8[4194304]{0:T(1024)(128)(4,1)S(1)}, s32[]{:S(2)}) async-start(s8[30081024]{0:T(1024)(128)(4,1)} %bitcast.269), calls=%async_computation.8 | async-start | bytes 8388608
  358.2 16.9 %slice-start.6 = ((s8[30081024]{0:T(1024)(128)(4,1)}), s8[4194304]{0:T(1024)(128)(4,1)S(1)}, s32[]{:S(2)}) async-start(s8[30081024]{0:T(1024)(128)(4,1)} %bitcast.269), calls=%async_computation.9 | async-start | bytes 8388608
  358.2 16.9 %slice-start.7 = ((s8[30081024]{0:T(1024)(128)(4,1)}), s8[720896]{0:T(1024)(128)(4,1)S(1)}, s32[]{:S(2)}) async-start(s8[30081024]{0:T(1024)(128)(4,1)} %bitcast.269), calls=%async_computation.10 | async-start | bytes 1441792
  441.3 18.1 %slice-start.8 = ((s8[6455296]{0:T(1024)(128)(4,1)}), s8[4194304]{0:T(1024)(128)(4,1)S(1)}, s32[]{:S(2)}) async-start(s8[6455296]{0:T(1024)(128)(4,1)} %bitcast.283), calls=%async_computation.11 | async-start | bytes 8388608
  471.6 26.8 %copy-start.4 = (f32[256,1088]{1,0:T(8,128)S(1)}, f32[256,1088]{1,0:T(8,128)}, u32[]{:S(2)}) copy-start(f32[256,1088]{1,0:T(8,128)} %get-tuple-element.99) | copy-start | bytes 3342340
  498.9 92.8 %collective-permute-start.2 = (bf16[1088,1572]{1,0:T(8,128)(2,1)}, bf16[1088,1572]{1,0:T(8,128)(2,1)}, u32[]{:S(2)}, u32[]{:S(2)}) collective-permute-start(bf16[1088,1572]{1,0:T(8,128)(2,1)} %convolution_convert_fusion.1), channel_id=1, source_target_pairs={{0,16},{16,0},{1,17},{17,1},{2,18},{18,2},{3,19},{19,3},{4,20},{20... | collective-permute-start | bytes 10262024 | tf_op jit(solution)/shard_map/ppermute | solution.py:1026
  536.0 43.2 %copy-start.16 = (bf16[256,1088]{1,0:T(8,128)(2,1)}, bf16[256,1088]{1,0:T(8,128)(2,1)S(1)}, u32[]{:S(2)}) copy-start(bf16[256,1088]{1,0:T(8,128)(2,1)S(1)} %get-tuple-element.73.r_ref) | copy-start | bytes 1671172
  618.7 3.8 collective-permute-start.3
  649.5 81.5 %copy-start.14 = (bf16[16,64,1088]{2,1,0:T(8,128)(2,1)S(1)}, bf16[16,64,1088]{2,1,0:T(8,128)(2,1)}, u32[]{:S(2)}) copy-start(bf16[16,64,1088]{2,1,0:T(8,128)(2,1)} %shard_map.269) | copy-start | bytes 6684676
  931.4 24.2 %copy-start.28 = (bf16[16,264,1088]{2,1,0:T(8,128)(2,1)S(1)}, bf16[16,264,1088]{2,1,0:T(8,128)(2,1)}, u32[]{:S(2)}) copy-start(bf16[16,264,1088]{2,1,0:T(8,128)(2,1)} %get-tuple-element.35) | copy-start | bytes 27574276
  955.5 44.6 %copy-start.30 = (f32[204]{0:T(256)S(1)}, f32[204]{0:T(256)}, u32[]{:S(2)}) copy-start(f32[204]{0:T(256)} %param.29) | copy-start | bytes 2452
  955.6 44.6 %copy-start.34 = (f32[204]{0:T(256)S(1)}, f32[204]{0:T(256)}, u32[]{:S(2)}) copy-start(f32[204]{0:T(256)} %param.30) | copy-start | bytes 2452
  955.6 44.6 %copy-start.35 = (f32[204]{0:T(256)S(1)}, f32[204]{0:T(256)}, u32[]{:S(2)}) copy-start(f32[204]{0:T(256)} %param.31) | copy-start | bytes 2452
  1000.8 21.6 %copy-start.5 = (f32[1088,408]{0,1:T(8,128)S(1)}, f32[1088,408]{0,1:T(8,128)}, u32[]{:S(2)}) copy-start(f32[1088,408]{0,1:T(8,128)} %param.26) | copy-start | bytes 5326852
  1000.8 21.6 %copy-start.11 = (bf16[1,408,1088]{2,1,0:T(8,128)(2,1)S(1)}, bf16[1,408,1088]{2,1,0:T(8,128)(2,1)}, u32[]{:S(2)}) copy-start(bf16[1,408,1088]{2,1,0:T(8,128)(2,1)} %reduce-scatter.4.cloned.1.call-done) | copy-start | bytes 2663428
  1000.8 28.1 %copy-start.1 = (s32[50304]{0:T(1024)S(1)}, s32[50304]{0:T(1024)}, u32[]{:S(2)}) copy-start(s32[50304]{0:T(1024)} %param.22) | copy-start | bytes 603652
  (24 other events, 180.3 us)
Sparse Core Ops, SparseCore 0:
  11.4 215.6 all-gather.2
  618.1 335.6 reduce-scatter.3
